TPU v7x, 128 devices: a whole 4x4x4 slice. The times are simulated.
128 devices in a mesh: band: 2 (over x_hi), chan: 64 (over z, y, x_lo, core).
Axes of the slice: x: 4 (x_hi: 2, x_lo: 2; x = x_hi * 2 + x_lo), y: 4, z: 4, core: 2. Of those that a mesh axis runs over, the one named last changes fastest.
Arguments:
- traces: bfloat16 [10240, 12, 4096], P('chan', 'band'), may hold values from -70 to 70, as said below
- band_start: int32 [2], replicated, may hold values from 0 to 1983
- half_width: int32 [2], replicated, may hold values from 12 to 21
Outputs:
- coherence: float32 [2, 10240, 10240], P('band', 'chan')
Inputs may be any that keep to these rules, and one draw needn't show every extreme that they name: `traces`: records hold noise and a few waves that reach each channel with its own delay.
All inputs are finite; a program needn't handle non-finite values.
Results may differ from a plain program's by a relative error of at most 0.0044.
Values may be sent and summed in bfloat16 or wider, within the bound.
No kernel may reach another device: no remote copies, remote signals or barrier semaphores. Data moves between devices by JAX's collectives and lax.ppermute only.
A program may use at most 192 MiB of HBM per device.

v0:
```python
import math

import jax
import jax.numpy as jnp
from jax import lax
from jax.sharding import PartitionSpec as P

SAMPLES = 4096
BINS = 64


def make_table(band_start):
    sample_ids = jnp.arange(SAMPLES, dtype=jnp.int32)
    freq_ids = band_start[:, None] + jnp.arange(BINS, dtype=jnp.int32)[None, :]
    phases = freq_ids[:, :, None] * sample_ids[None, None, :] % SAMPLES
    angles = phases.astype(jnp.float32) * (2.0 * math.pi / SAMPLES)
    amplitude_scale = 1.0 / math.sqrt(SAMPLES)
    cos_sin = jnp.stack([jnp.cos(angles), -jnp.sin(angles)], axis=1) * amplitude_scale
    band_count = band_start.shape[0]
    return (
        jnp.transpose(cos_sin, (3, 0, 1, 2))
        .reshape(SAMPLES, band_count * 2 * BINS)
        .astype(jnp.bfloat16)
    )


def smoother(half_width):
    row_ids = jnp.arange(BINS, dtype=jnp.int32)[:, None]
    col_ids = jnp.arange(BINS, dtype=jnp.int32)[None, :]
    inside = (jnp.abs(row_ids - col_ids)[None, :, :] <= half_width[:, None, None]).astype(
        jnp.float32
    )
    return inside / jnp.sum(inside, axis=1, keepdims=True)


def whiten(trace_block, dft_table, smooth):
    rows_here = trace_block.shape[0]
    wins_here = trace_block.shape[1]
    band_count = smooth.shape[0]
    flat = trace_block.reshape(rows_here * wins_here, SAMPLES)
    spectra = jnp.dot(flat, dft_table, preferred_element_type=jnp.float32)
    spectra = spectra.reshape(rows_here, wins_here, band_count, 2, BINS)
    amplitude = jnp.sqrt(
        spectra[:, :, :, 0] * spectra[:, :, :, 0] + spectra[:, :, :, 1] * spectra[:, :, :, 1]
    )
    smoothed = jnp.einsum("cwbj,bjk->cwbk", amplitude, smooth, precision=lax.Precision.HIGHEST)
    whitened = spectra / (smoothed[:, :, :, None, :] + 1e-05)
    return whitened.reshape(rows_here, wins_here, band_count, 2 * BINS).astype(jnp.bfloat16)


def cross_rows(normed, shard_rows):
    return jnp.einsum("ck,dk->cd", normed, shard_rows, preferred_element_type=jnp.float32)


def local(traces, band_start, half_width):
    dft_table = make_table(band_start)
    smooth = smoother(half_width)
    whitened = whiten(traces, dft_table, smooth)
    regrouped = lax.all_to_all(whitened, "band", split_axis=2, concat_axis=1, tiled=True)
    values = regrouped[:, :, 0, :].astype(jnp.float32)
    energy = jnp.sum(values * values, axis=(1, 2))
    normed = values / jnp.sqrt(energy + 1e-06)[:, None, None]
    normed = normed.reshape(values.shape[0], values.shape[1] * values.shape[2]).astype(jnp.bfloat16)
    coherence = cross_rows(normed, lax.all_gather(normed, "chan", axis=0, tiled=True))
    return coherence[None]


def solution(mesh):
    placed = (P("chan", "band", None), P(), P())
    return jax.shard_map(
        local, mesh=mesh, in_specs=placed, out_specs=P("band", "chan", None), check_vma=False
    )
```

profile of v0, /device:TPU:1, one launch (start us, length us, event | category | flops | bytes accessed | tf_op | source)
XLA Modules:
  0.0 278.0 jit_solution(1769794796005140131)
XLA Ops:
  6.5 0.0 all-gather.2.cloned.1.call-start
  6.5 0.7 iota_add_fusion
  7.3 9.7 %fusion.8 = (f32[2,1,64,4096]{3,2,1,0:T(8,128)S(1)}, f32[2,1,64,4096]{3,2,1,0:T(8,128)}) fusion(s32[2,64]{1,0:T(2,128)S(1)} %iota_add_fusion), kind=kLoop, calls=%fused_computation.18 | loop fusion | flops 7864320 | bytes 4194816 | tf_op jit(solution)/shard_map/cos | solution.py:18
  16.9 11.6 %copy.24 = bf16[160,6,4096]{2,1,0:T(8,128)(2,1)} copy(bf16[160,6,4096]{2,0,1:T(8,128)(2,1)} %param.3) | data formatting | bytes 15728640 | tf_op args[0]
  28.5 12.2 %reshape.122 = bf16[960,4096]{1,0:T(8,128)(2,1)} reshape(bf16[160,6,4096]{2,1,0:T(8,128)(2,1)} %copy.24) | data formatting | bytes 15728640 | tf_op jit(solution)/shard_map/reshape | solution.py:40
  40.8 1.9 fusion
  42.7 5.5 %convolution_bitcast_fusion.1 = f32[960,256]{1,0:T(8,128)S(1)} fusion(bf16[4096,256]{0,1:T(8,128)(2,1)S(1)} %bitcast.28, bf16[960,4096]{1,0:T(8,128)(2,1)} %reshape.122), kind=kOutput, calls=%fused_computation.13 | convolution fusion | flops 2013265920 | bytes 10944512 | tf_op jit(solution)/shard_map/dot_general | solution.py:41
  48.2 0.0 copy-start
  48.2 0.9 copy-done
  49.1 0.5 reshape.123
  49.6 2.4 reshape.124
  52.1 0.0 copy-start.1
  52.1 3.3 %fusion.13 = f32[160,6,2,1,64]{4,3,2,1,0:T(1,128)S(1)} fusion(f32[160,6,2,2,64]{4,3,2,1,0:T(2,128)S(1)} %reshape.124), kind=kLoop, calls=%fused_computation.27 | loop fusion | flops 368640 | bytes 1474560 | tf_op jit(solution)/shard_map/sqrt | solution.py:43
  55.4 0.0 copy-done.1
  55.4 0.2 convert_reduce_fusion
  55.6 2.1 fusion.7
  57.6 0.1 copy.26
  57.7 0.2 div.30
  57.9 1.4 copy.28
  59.3 1.3 fusion.11
  60.7 12.9 %all_to_all.4 = bf16[160,6,2,128]{3,0,1,2:T(8,128)(2,1)S(1)} all-to-all(bf16[160,6,2,128]{3,0,1,2:T(8,128)(2,1)S(1)} %copy.29), channel_id=1, replica_groups=mesh['band'=2,'chan'=64] {'band'}, dimensions={2} | all-to-all | bytes 983040 | tf_op jit(solution)/shard_map/all_to_all | solution.py:59
  73.5 0.2 fusion.9
  73.7 0.1 convert_bitcast_fusion
  73.8 0.6 copy.30
  74.4 0.2 reshape.125
  74.6 0.9 divide_convert_fusion
  75.6 0.0 all-gather.2.cloned.1.call-update
  75.6 178.1 %all-gather.2.cloned.1.call-done = bf16[10240,1536]{1,0:T(8,128)(2,1)} async-done(((bf16[160,1536]{1,0:T(8,128)(2,1)}), bf16[10240,1536]{1,0:T(8,128)(2,1)}) %all-gather.2.cloned.1.call-update) | async-done | bytes 31457296 | tf_op jit(solution)/shard_map/all_gather | solution.py:64
  253.7 17.5 %convolution_bitcast_fusion = f32[1,160,10240]{2,1,0:T(8,128)} fusion(bf16[160,1536]{1,0:T(8,128)(2,1)} %divide_convert_fusion, bf16[10240,1536]{1,0:T(8,128)(2,1)} %all-gather.2.cloned.1.call-done), kind=kOutput, calls=%fused_computation | convolution fusion | flops 5033164800 | bytes 38502400 | tf_op jit(solution)/shard_map/ck,dk->cd/dot_general | solution.py:52
  (3 shorter events, 0.1 us)
Async XLA Ops:
  6.5 247.1 %all-gather.2.cloned.1.call-start = ((), (), s32[]{:S(2)}) async-start(), calls=%async_computation.1 | async-start | bytes 31948800 | tf_op jit(solution)/shard_map/all_gather | solution.py:64
  48.2 0.9 copy-start
  52.1 3.3 %copy-start.1 = (s32[2]{0:T(128)S(1)}, s32[2]{0:T(128)}, u32[]{:S(2)}) copy-start(s32[2]{0:T(128)} %param.5) | copy-start | bytes 28
Sparse Core Ops, SparseCore 0:
  75.7 177.8 all-gather.1
where the time goes:
time: 279 us; the launch traced here: 278 us
  waiting for transfers between devices  178 us (64%)
  local copies, waits for them, and re-layouts  30.2 us (11%)
  matrix products  25 us (9%)
  other arithmetic  18.3 us (7%)
  between operations  13.5 us (5%)
  blocking collectives  12.9 us (5%)
    all_gather x1, waiting for transfers between devices, local(): lax.all_gather(normed, 'chan', axis=0, tiled=True)  178 us
    dot_general x1, matrix products, cross_rows(): jnp.einsum('ck,dk->cd', normed, shard_rows, preferred_element_type=jnp.fl...  17.5 us
    all_to_all x1, blocking collectives, local(): lax.all_to_all(whitened, 'band', split_axis=2, concat_axis=1, tiled=True)  12.9 us
    unnamed x5, local copies, waits for them, and re-layouts  12.6 us
    reshape x1, local copies, waits for them, and re-layouts, whiten(): flat = trace_block.reshape(rows_here * wins_here, SAMPLES)  12.2 us
    cos x1, other arithmetic, make_table(): jnp.cos(angles)  9.66 us
  transfers between devices with their start and end apart: 1, of which 1 were waited for; matrix products, arithmetic and copies ran while one was open for 0% of the time, Pallas kernels for 0%

commit v1 on v0

v1 whole, which is shorter than its diff:
```python
import math

import jax
import jax.numpy as jnp
from jax import lax
from jax.experimental import pallas as pl
from jax.experimental.pallas import tpu as pltpu
from jax.sharding import PartitionSpec as P

SAMPLES = 4096
BINS = 64
WINS = 6
ROWS = 160
DEPTH = 1536
GROUP = 640
STEP_ROWS = 320
PARTS = 128
TURN = 2.0 * math.pi / SAMPLES


def whiten_kernel(meta, x_ref, keep_ref, send_ref, table, mask, share):
    @pl.when(pl.program_id(0) == 0)
    def _():
        lane = lax.broadcasted_iota(jnp.int32, (1, 128), 1)
        freq = jnp.where(lane < BINS, meta[0] + lane, meta[1] + lane - BINS)
        coarse = lax.broadcasted_iota(jnp.int32, (SAMPLES // PARTS, 128), 0) * PARTS
        fine = lax.broadcasted_iota(jnp.int32, (PARTS, 128), 0)
        angle_a = ((freq * coarse) & (SAMPLES - 1)).astype(jnp.float32) * TURN
        angle_b = ((freq * fine) & (SAMPLES - 1)).astype(jnp.float32) * TURN
        root = 1.0 / math.sqrt(SAMPLES)
        cos_a, sin_a = jnp.cos(angle_a) * root, jnp.sin(angle_a) * root
        cos_b, sin_b = jnp.cos(angle_b), jnp.sin(angle_b)
        for part in range(SAMPLES // PARTS):
            rows = pl.ds(part * PARTS, PARTS)
            ca, sa = cos_a[part : part + 1], sin_a[part : part + 1]
            table[rows, 0:128] = (ca * cos_b - sa * sin_b).astype(jnp.bfloat16)
            table[rows, 128:256] = (-(sa * cos_b + ca * sin_b)).astype(jnp.bfloat16)
        row = lax.broadcasted_iota(jnp.int32, (256, 128), 0) & 127
        col = lax.broadcasted_iota(jnp.int32, (256, 128), 1)
        half = jnp.where(col < BINS, meta[2], meta[3])
        inside = ((row < BINS) == (col < BINS)) & (jnp.abs(row - col) <= half)
        mask[...] = inside.astype(jnp.float32).astype(jnp.bfloat16)
        bin_id = lane & (BINS - 1)
        width = jnp.where(lane < BINS, meta[2], meta[3])
        count = jnp.minimum(bin_id + width, BINS - 1) - jnp.maximum(bin_id - width, 0) + 1
        share[...] = 1.0 / count.astype(jnp.float32)

    spectra = jnp.dot(x_ref[...], table[...], preferred_element_type=jnp.float32)
    re, im = spectra[:, :128], spectra[:, 128:]
    amplitude = jnp.sqrt(re * re + im * im)
    high = amplitude.astype(jnp.bfloat16)
    low = (amplitude - high.astype(jnp.float32)).astype(jnp.bfloat16)
    sums = jnp.dot(
        jnp.concatenate([high, low], axis=1), mask[...], preferred_element_type=jnp.float32
    )
    gain = 1.0 / (sums * share[...] + 1e-05)
    re, im = re * gain, im * gain
    turned = pltpu.roll(im, BINS, 1)
    first = lax.broadcasted_iota(jnp.int32, re.shape, 1) < BINS
    band0 = jnp.where(first, re, turned)
    band1 = jnp.where(first, turned, re)
    mine = meta[4] == 0
    keep_ref[...] = jnp.where(mine, band0, band1).astype(jnp.bfloat16)
    send_ref[...] = jnp.where(mine, band1, band0).astype(jnp.bfloat16)


def whiten(flat, meta):
    total = flat.shape[0]
    out = jax.ShapeDtypeStruct((total, 128), jnp.bfloat16)
    block = pl.BlockSpec((STEP_ROWS, 128), lambda i, m: (i, 0))
    return pl.pallas_call(
        whiten_kernel,
        grid_spec=pltpu.PrefetchScalarGridSpec(
            num_scalar_prefetch=1,
            grid=(total // STEP_ROWS,),
            in_specs=[pl.BlockSpec((STEP_ROWS, SAMPLES), lambda i, m: (i, 0))],
            out_specs=[block, block],
            scratch_shapes=[
                pltpu.VMEM((SAMPLES, 256), jnp.bfloat16),
                pltpu.VMEM((256, 128), jnp.bfloat16),
                pltpu.VMEM((1, 128), jnp.float32),
            ],
        ),
        out_shape=[out, out],
        compiler_params=pltpu.CompilerParams(vmem_limit_bytes=40 << 20),
        name="whiten",
    )(meta, flat)


def normalize_kernel(keep_ref, got_ref, out_ref):
    energy = jnp.zeros((ROWS, 128), jnp.float32)
    for ref in (keep_ref, got_ref):
        for win in range(WINS):
            value = ref[win * ROWS : (win + 1) * ROWS, :].astype(jnp.float32)
            energy = energy + value * value
    scale = 1.0 / jnp.sqrt(jnp.sum(energy, axis=1, keepdims=True) + 1e-06)
    for side, ref in enumerate((keep_ref, got_ref)):
        for win in range(WINS):
            value = ref[win * ROWS : (win + 1) * ROWS, :].astype(jnp.float32)
            at = (side * WINS + win) * 128
            out_ref[:, at : at + 128] = (value * scale).astype(jnp.bfloat16)


def normalize(keep, got):
    return pl.pallas_call(
        normalize_kernel,
        out_shape=jax.ShapeDtypeStruct((ROWS, DEPTH), jnp.bfloat16),
        name="normalize",
    )(keep, got)


def cross_kernel(swap, meta, *refs):
    row_refs, col_refs = refs[:4], refs[4:8]
    mine_ref, c_ref, x_ref, xc_ref = refs[8:12]
    rows, cols, row_sems, col_sems = refs[12:]
    for i in range(4):
        pltpu.make_async_copy(
            row_refs[i], rows.at[pl.ds(i * ROWS, ROWS)], row_sems.at[i]
        ).start()

    def fetch(order):
        for i in range(4):
            pltpu.make_async_copy(
                col_refs[order[i]], cols.at[pl.ds(i * ROWS, ROWS)], col_sems.at[i]
            ).start()

    @pl.when(meta[0] == 0)
    def _():
        fetch((0, 1, 2, 3))

    @pl.when(meta[0] != 0)
    def _():
        fetch(swap)

    for i in range(4):
        pltpu.make_async_copy(
            row_refs[i], rows.at[pl.ds(i * ROWS, ROWS)], row_sems.at[i]
        ).wait()
        pltpu.make_async_copy(
            col_refs[i], cols.at[pl.ds(i * ROWS, ROWS)], col_sems.at[i]
        ).wait()
    product = lax.dot_general(
        rows[...], cols[...], (((1,), (1,)), ((), ())), preferred_element_type=jnp.float32
    )
    mine_ref[...] = product[:ROWS]
    c_ref[...] = product[ROWS : 2 * ROWS].astype(jnp.bfloat16)
    x_ref[...] = product[2 * ROWS : 3 * ROWS].astype(jnp.bfloat16)
    xc_ref[...] = product[3 * ROWS :].astype(jnp.bfloat16)


def cross(place, rows, cols, swap):
    narrow = jax.ShapeDtypeStruct((ROWS, GROUP), jnp.bfloat16)
    return pl.pallas_call(
        lambda *refs: cross_kernel(swap, *refs),
        in_specs=[pl.BlockSpec(memory_space=pltpu.SMEM)] + [pl.BlockSpec(memory_space=pl.ANY)] * 8,
        out_shape=[jax.ShapeDtypeStruct((ROWS, GROUP), jnp.float32), narrow, narrow, narrow],
        scratch_shapes=[
            pltpu.VMEM((4 * ROWS, DEPTH), jnp.bfloat16),
            pltpu.VMEM((4 * ROWS, DEPTH), jnp.bfloat16),
            pltpu.SemaphoreType.DMA((4,)),
            pltpu.SemaphoreType.DMA((4,)),
        ],
        compiler_params=pltpu.CompilerParams(vmem_limit_bytes=32 << 20),
        name="cross",
    )(place, *rows, *cols)


def place_kernel(meta, own, got_c, got_x, got_xc, *refs):
    out, buf, sems = refs[-3:]
    for slot in range(4):

        @pl.when(meta[0] == slot)
        def _():
            for g in range(4):
                for flip, piece in enumerate((own, got_c, got_x, got_xc)):
                    at = (slot ^ flip) * ROWS
                    value = piece[:, g * ROWS : (g + 1) * ROWS].astype(jnp.float32)
                    buf[g, :, at : at + ROWS] = value

    copies = []
    for g in range(4):
        start = pl.multiple_of(meta[1 + g] * GROUP, 128)
        copies.append(
            pltpu.make_async_copy(buf.at[g], out.at[:, pl.ds(start, GROUP)], sems.at[g])
        )
        copies[-1].start()
    for copy in copies:
        copy.wait()


def place_group(meta, pieces, out):
    vmem = pl.BlockSpec(memory_space=pltpu.VMEM)
    prior = () if out is None else (out,)
    return pl.pallas_call(
        place_kernel,
        in_specs=[pl.BlockSpec(memory_space=pltpu.SMEM)]
        + [vmem] * 4
        + [pl.BlockSpec(memory_space=pl.ANY)] * len(prior),
        out_specs=pl.BlockSpec(memory_space=pl.ANY),
        out_shape=jax.ShapeDtypeStruct((ROWS, 16 * GROUP), jnp.float32),
        scratch_shapes=[
            pltpu.VMEM((4, ROWS, GROUP), jnp.float32),
            pltpu.SemaphoreType.DMA((4,)),
        ],
        input_output_aliases={5: 0} if prior else {},
        compiler_params=pltpu.CompilerParams(vmem_limit_bytes=32 << 20),
        name="place",
    )(meta, *pieces, *prior)


def unit(index):
    return index // 16, index // 4 % 4, index // 2 % 2, index % 2


def join(z, y, x, c):
    return (z % 4) * 16 + (y % 4) * 4 + x * 2 + c


def from_first(shift):
    pairs = []
    for dst in range(64):
        z, y, x, c = unit(dst)
        src = join(z + shift, y, x, c) if c == 0 else join(z, y + shift, x, c)
        pairs.append((src, dst))
    return pairs


def from_second(shift):
    pairs = []
    for dst in range(64):
        z, y, x, c = unit(dst)
        src = join(z, y + shift, x, c) if c == 0 else join(z + shift, y, x, c)
        pairs.append((src, dst))
    return pairs


def flip(bits):
    return [(i, i ^ bits) for i in range(64)]


GROUPS = (
    (((1, 0), (0, 1), (-1, 0), (0, -1)), (1, 0, 3, 2)),
    (((1, 1), (-1, -1), (1, -1), (-1, 1)), (0, 1, 3, 2)),
    (((0, 0), (2, 2), (2, 0), (0, 2)), (0, 1, 3, 2)),
    (((1, 2), (2, 1), (-1, 2), (2, -1)), (1, 0, 3, 2)),
)


def local(traces, band_start, half_width):
    band = lax.axis_index("band").astype(jnp.int32)
    chan = lax.axis_index("chan").astype(jnp.int32)
    meta = jnp.concatenate([band_start, half_width, band[None]])
    flat = jnp.transpose(traces, (1, 0, 2)).reshape(WINS * ROWS, SAMPLES)
    keep, send = whiten(flat, meta)
    got = lax.ppermute(send, "band", [(0, 1), (1, 0)])
    own = normalize(keep, got)

    def move(value, pairs):
        return lax.ppermute(value, "chan", pairs)

    near = {}
    near[0, 0] = own
    near[1, 0] = move(own, from_first(1))
    near[-1, 0] = move(own, from_first(-1))
    row_x = move(own, flip(2))
    row_c = move(own, flip(1))
    near[0, 1] = move(own, from_second(1))
    near[0, -1] = move(own, from_second(-1))
    row_xc = move(row_x, flip(1))
    near[2, 0] = move(near[1, 0], from_first(1))
    for du in (1, -1, 2):
        for dv in (1, -1):
            near[du, dv] = move(near[du, 0], from_second(dv))
    for du, dv in ((0, 1), (1, 1), (-1, -1), (2, -1)):
        near[du, 2] = move(near[du, dv], from_second(dv))

    z, y, _, c = unit(chan)
    place = c[None]
    rows = (own, row_c, row_x, row_xc)
    out = None
    for offsets, swap in GROUPS:
        mine, to_c, to_x, to_xc = cross(place, rows, [near[o] for o in offsets], swap)
        pieces = (mine, move(to_c, flip(1)), move(to_x, flip(2)), move(to_xc, flip(3)))
        where = [((z + dz) & 3) * 4 + ((y + dy) & 3) for dz, dy in offsets]
        out = place_group(jnp.stack([chan & 3] + where), pieces, out)
    return out[None]


def solution(mesh):
    placed = (P("chan", "band", None), P(), P())
    return jax.shard_map(
        local, mesh=mesh, in_specs=placed, out_specs=P("band", "chan", None), check_vma=False
    )
```

time: 279 us -> 129 us (0.46)
  waiting for transfers between devices: 178 us -> 19.8 us
  starting transfers between devices: 0.01 us -> 51.6 us
  Pallas kernels: 0 us -> 35 us
  matrix products: 25 us -> 0 us
  other arithmetic: 18.3 us -> 0.75 us
  between operations: 13.5 us -> 0.46 us
  blocking collectives: 12.9 us -> 0 us
  local copies, waits for them, and re-layouts: 30.2 us -> 21.1 us
    all_gather x1 -> x0, waiting for transfers between devices: 178 us -> none  [local(): lax.all_gather(normed, 'chan', axis=0, tiled=True)]
    ppermute x0 -> x31, starting transfers between devices: none -> 51.6 us  [the longest x30 48.1 us: move(): return lax.ppermute(value, 'chan', pairs)]
    pallas_call x0 -> x10, Pallas kernels: none -> 35 us  [the longest x4 19.4 us: cross(): pl.pallas_call(lambda *refs: cross_kernel(swap, *refs), in_specs=[pl.Bloc...]
    dot_general x3 -> x0, matrix products: 25 us -> none  [the longest x1 17.5 us: cross_rows(): jnp.einsum('ck,dk->cd', normed, shard_rows, preferred_element_type=jnp.fl...]
    ppermute x0 -> x31, waiting for transfers between devices: none -> 19.8 us  [the longest x30 14.6 us: move(): return lax.ppermute(value, 'chan', pairs)]
    reshape x3 -> x0, local copies, waits for them, and re-layouts: 15.2 us -> none  [the longest x1 12.2 us: whiten(): flat = trace_block.reshape(rows_here * wins_here, SAMPLES)]
    all_to_all x1 -> x0, blocking collectives: 12.9 us -> none  [local(): lax.all_to_all(whitened, 'band', split_axis=2, concat_axis=1, tiled=True)]
    cos x1 -> x0, other arithmetic: 9.66 us -> none  [make_table(): jnp.cos(angles)]
  transfers between devices with their start and end apart: 1 -> 31, of which waited for: 1 -> 10; matrix products, arithmetic and copies ran while one was open for 0% -> 0% of each run, Pallas kernels for 0% -> 20%
where the time goes in v1:
time: 129 us
  starting transfers between devices  51.6 us (40%)
  Pallas kernels  35 us (27%)
  local copies, waits for them, and re-layouts  21.1 us (16%)
  waiting for transfers between devices  19.8 us (15%)
    ppermute x30, starting transfers between devices, move(): return lax.ppermute(value, 'chan', pairs)  48.1 us
    unnamed x66, local copies, waits for them, and re-layouts  20.8 us
    pallas_call x4, Pallas kernels, cross(): pl.pallas_call(lambda *refs: cross_kernel(swap, *refs), in_specs=[pl.Bloc...  19.4 us
    ppermute x30, waiting for transfers between devices, move(): return lax.ppermute(value, 'chan', pairs)  14.6 us
    pallas_call x4, Pallas kernels, place_group(): pl.pallas_call(place_kernel, in_specs=[pl.BlockSpec(memory_space=pltpu.SM...  8.61 us
    ppermute x1, waiting for transfers between devices, local(): got = lax.ppermute(send, 'band', [(0, 1), (1, 0)])  5.19 us
    pallas_call x1, Pallas kernels, whiten(): pl.pallas_call(whiten_kernel, grid_spec=pltpu.PrefetchScalarGridSpec(num_...  4.98 us
    ppermute x1, starting transfers between devices, local(): got = lax.ppermute(send, 'band', [(0, 1), (1, 0)])  3.57 us
  transfers between devices with their start and end apart: 31, of which 10 were waited for; matrix products, arithmetic and copies ran while one was open for 0% of the time, Pallas kernels for 20%

profile of v1, /device:TPU:1, one launch (start us, length us, event | category | flops | bytes accessed | tf_op | source)
XLA Modules:
  0.0 128.8 jit_solution(4429088979516309076)
XLA Ops:
  0.8 3.2 %copy-done.2 = bf16[160,6,4096]{2,0,1:T(8,128)(2,1)S(1)} copy-done((bf16[160,6,4096]{2,0,1:T(8,128)(2,1)S(1)}, bf16[160,6,4096]{2,0,1:T(8,128)(2,1)}, u32[]{:S(2)}) %copy-start.2) | copy-done | bytes 7864344
  4.0 5.0 %whiten.1 = (bf16[960,128]{1,0:T(8,128)(2,1)S(1)}, bf16[960,128]{1,0:T(8,128)(2,1)S(1)}) custom-call(s32[5]{0:T(128)S(1)} %pad_add_fusion.meta, bf16[960,4096]{1,0:T(8,128)(2,1)S(1)} %bitcast.23), custom_call_target="tpu_custom_call" | custom-call | tf_op jit(solution)/shard_map/whiten/pallas_call | solution.py:71
  9.7 3.6 %collective-permute-start = (bf16[960,128]{1,0:T(8,128)(2,1)S(1)}, bf16[960,128]{1,0:T(8,128)(2,1)S(1)}, u32[]{:S(2)}, u32[]{:S(2)}) collective-permute-start(bf16[960,128]{1,0:T(8,128)(2,1)S(1)} %get-tuple-element.24), channel_id=1, source_target_pairs={{0,64},{64,0},{1,65},{65,1},{2,66},{66,2},{3,67},{67,3},{4,68},{68... | collective-permute-start | bytes 737288 | tf_op jit(solution)/shard_map/ppermute | solution.py:255
  13.2 5.2 %collective-permute-done.got_ref = bf16[960,128]{1,0:T(8,128)(2,1)S(1)} collective-permute-done((bf16[960,128]{1,0:T(8,128)(2,1)S(1)}, bf16[960,128]{1,0:T(8,128)(2,1)S(1)}, u32[]{:S(2)}, u32[]{:S(2)}) %collective-permute-start) | collective-permute-done | bytes 245792 | tf_op jit(solution)/shard_map/ppermute | solution.py:255
  19.1 2.1 %normalize.1.refs_1_.refs_5_ = bf16[160,1536]{1,0:T(8,128)(2,1)} custom-call(bf16[960,128]{1,0:T(8,128)(2,1)} %copy-done.19, bf16[960,128]{1,0:T(8,128)(2,1)} %copy-done.32), custom_call_target="tpu_custom_call" | custom-call | tf_op jit(solution)/shard_map/normalize/pallas_call | solution.py:105
  21.2 3.1 %collective-permute-start.4 = (bf16[160,1536]{1,0:T(8,128)(2,1)}, bf16[160,1536]{1,0:T(8,128)(2,1)S(1)}, u32[]{:S(2)}, u32[]{:S(2)}) collective-permute-start(bf16[160,1536]{1,0:T(8,128)(2,1)} %normalize.1.refs_1_.refs_5_), channel_id=1, source_target_pairs={{16,0},{5,1},{18,2},{7,3},{20,4},{9,5},{22,6},{11,7},{24,8},{13,9}... | collective-permute-start | bytes 1474568 | tf_op jit(solution)/shard_map/ppermute | solution.py:259
  24.3 1.6 %collective-permute-start.27 = (bf16[160,1536]{1,0:T(8,128)(2,1)}, bf16[160,1536]{1,0:T(8,128)(2,1)S(1)}, u32[]{:S(2)}, u32[]{:S(2)}) collective-permute-start(bf16[160,1536]{1,0:T(8,128)(2,1)} %normalize.1.refs_1_.refs_5_), channel_id=1, source_target_pairs={{12,0},{49,1},{14,2},{51,3},{0,4},{53,5},{2,6},{55,7},{4,8},{57,9}... | collective-permute-start | bytes 1474568 | tf_op jit(solution)/shard_map/ppermute | solution.py:259
  26.0 2.1 %collective-permute-start.17 = (bf16[160,1536]{1,0:T(8,128)(2,1)}, bf16[160,1536]{1,0:T(8,128)(2,1)S(1)}, u32[]{:S(2)}, u32[]{:S(2)}) collective-permute-start(bf16[160,1536]{1,0:T(8,128)(2,1)} %normalize.1.refs_1_.refs_5_), channel_id=1, source_target_pairs={{4,0},{17,1},{6,2},{19,3},{8,4},{21,5},{10,6},{23,7},{12,8},{25,9}... | collective-permute-start | bytes 1474568 | tf_op jit(solution)/shard_map/ppermute | solution.py:259
  28.1 2.3 %collective-permute-done.4.refs_5_ = bf16[160,1536]{1,0:T(8,128)(2,1)S(1)} collective-permute-done((bf16[160,1536]{1,0:T(8,128)(2,1)}, bf16[160,1536]{1,0:T(8,128)(2,1)S(1)}, u32[]{:S(2)}, u32[]{:S(2)}) %collective-permute-start.4) | collective-permute-done | bytes 491552 | tf_op jit(solution)/shard_map/ppermute | solution.py:259
  30.4 3.0 %collective-permute-start.7 = (bf16[160,1536]{1,0:T(8,128)(2,1)S(1)}, bf16[160,1536]{1,0:T(8,128)(2,1)S(1)}, u32[]{:S(2)}, u32[]{:S(2)}) collective-permute-start(bf16[160,1536]{1,0:T(8,128)(2,1)S(1)} %collective-permute-done.4.refs_5_), channel_id=1, source_target_pairs={{16,0},{5,1},{18,2},{7,3},{20,4},{9,5},{22,6},{11,7},{24,8},{13,9}... | collective-permute-start | bytes 1474568 | tf_op jit(solution)/shard_map/ppermute | solution.py:259
  35.6 8.6 %collective-permute-start.1 = (bf16[160,1536]{1,0:T(8,128)(2,1)}, bf16[160,1536]{1,0:T(8,128)(2,1)S(1)}, u32[]{:S(2)}, u32[]{:S(2)}) collective-permute-start(bf16[160,1536]{1,0:T(8,128)(2,1)} %normalize.1.refs_1_.refs_5_), channel_id=1, source_target_pairs={{0,1},{1,0},{2,3},{3,2},{4,5},{5,4},{6,7},{7,6},{8,9},{9,8},{10,11... | collective-permute-start | bytes 1474568 | tf_op jit(solution)/shard_map/ppermute | solution.py:259
  45.1 1.5 %collective-permute-start.12 = (bf16[160,1536]{1,0:T(8,128)(2,1)S(1)}, bf16[160,1536]{1,0:T(8,128)(2,1)S(1)}, u32[]{:S(2)}, u32[]{:S(2)}) collective-permute-start(bf16[160,1536]{1,0:T(8,128)(2,1)S(1)} %collective-permute-done.7.refs_7_), channel_id=1, source_target_pairs={{12,0},{49,1},{14,2},{51,3},{0,4},{53,5},{2,6},{55,7},{4,8},{57,9}... | collective-permute-start | bytes 1474568 | tf_op jit(solution)/shard_map/ppermute | solution.py:259
  46.6 2.8 %collective-permute-start.10 = (bf16[160,1536]{1,0:T(8,128)(2,1)S(1)}, bf16[160,1536]{1,0:T(8,128)(2,1)}, u32[]{:S(2)}, u32[]{:S(2)}) collective-permute-start(bf16[160,1536]{1,0:T(8,128)(2,1)S(1)} %collective-permute-done.9.refs_7_), channel_id=1, source_target_pairs={{12,0},{49,1},{14,2},{51,3},{0,4},{53,5},{2,6},{55,7},{4,8},{57,9}... | collective-permute-start | bytes 1474568 | tf_op jit(solution)/shard_map/ppermute | solution.py:259
  50.2 1.9 %collective-permute-start.5 = (bf16[160,1536]{1,0:T(8,128)(2,1)S(1)}, bf16[160,1536]{1,0:T(8,128)(2,1)S(1)}, u32[]{:S(2)}, u32[]{:S(2)}) collective-permute-start(bf16[160,1536]{1,0:T(8,128)(2,1)S(1)} %collective-permute-done.4.refs_5_), channel_id=1, source_target_pairs={{4,0},{17,1},{6,2},{19,3},{8,4},{21,5},{10,6},{23,7},{12,8},{25,9}... | collective-permute-start | bytes 1474568 | tf_op jit(solution)/shard_map/ppermute | solution.py:259
  54.0 2.5 %collective-permute-start.3 = (bf16[160,1536]{1,0:T(8,128)(2,1)S(1)}, bf16[160,1536]{1,0:T(8,128)(2,1)S(1)}, u32[]{:S(2)}, u32[]{:S(2)}) collective-permute-start(bf16[160,1536]{1,0:T(8,128)(2,1)S(1)} %collective-permute-done.2.refs_3_), channel_id=1, source_target_pairs={{0,1},{1,0},{2,3},{3,2},{4,5},{5,4},{6,7},{7,6},{8,9},{9,8},{10,11... | collective-permute-start | bytes 1474568 | tf_op jit(solution)/shard_map/ppermute | solution.py:259
  56.4 2.0 %collective-permute-done.23.refs_8_ = bf16[160,1536]{1,0:T(8,128)(2,1)S(1)} collective-permute-done((bf16[160,1536]{1,0:T(8,128)(2,1)S(1)}, bf16[160,1536]{1,0:T(8,128)(2,1)S(1)}, u32[]{:S(2)}, u32[]{:S(2)}) %collective-permute-start.23) | collective-permute-done | bytes 491552 | tf_op jit(solution)/shard_map/ppermute | solution.py:259
  60.6 3.0 %collective-permute-start.11 = (bf16[160,1536]{1,0:T(8,128)(2,1)}, bf16[160,1536]{1,0:T(8,128)(2,1)}, u32[]{:S(2)}, u32[]{:S(2)}) collective-permute-start(bf16[160,1536]{1,0:T(8,128)(2,1)} %collective-permute-done.10.refs_6_), channel_id=1, source_target_pairs={{12,0},{49,1},{14,2},{51,3},{0,4},{53,5},{2,6},{55,7},{4,8},{57,9}... | collective-permute-start | bytes 1474568 | tf_op jit(solution)/shard_map/ppermute | solution.py:259
  63.7 3.5 %collective-permute-start.8 = (bf16[160,1536]{1,0:T(8,128)(2,1)S(1)}, bf16[160,1536]{1,0:T(8,128)(2,1)}, u32[]{:S(2)}, u32[]{:S(2)}) collective-permute-start(bf16[160,1536]{1,0:T(8,128)(2,1)S(1)} %collective-permute-done.7.refs_7_), channel_id=1, source_target_pairs={{4,0},{17,1},{6,2},{19,3},{8,4},{21,5},{10,6},{23,7},{12,8},{25,9}... | collective-permute-start | bytes 1474568 | tf_op jit(solution)/shard_map/ppermute | solution.py:259
  71.4 4.3 %cross.7 = (f32[160,640]{1,0:T(8,128)S(1)}, bf16[160,640]{1,0:T(8,128)(2,1)S(1)}, bf16[160,640]{1,0:T(8,128)(2,1)S(1)}, bf16[160,640]{1,0:T(8,128)(2,1)S(1)}) custom-call(s32[1]{0:T(128)} %bitcast.5.refs_0_, bf16[160,1536]{1,0:T(8,128)(2,1)S(1)} %copy-done, bf16[160,1536]{1,0:T(8,128)(2,1)S(1)} %collective-permute-done.1.refs_2_, ...), custom_call_target="tpu_custom_call" | custom-call | tf_op jit(solution)/shard_map/cross/pallas_call | solution.py:153
  76.5 2.9 %collective-permute-start.28 = (bf16[160,640]{1,0:T(8,128)(2,1)S(1)}, bf16[160,640]{1,0:T(8,128)(2,1)S(1)}, u32[]{:S(2)}, u32[]{:S(2)}) collective-permute-start(bf16[160,640]{1,0:T(8,128)(2,1)S(1)} %get-tuple-element.38), channel_id=1, source_target_pairs={{0,1},{1,0},{2,3},{3,2},{4,5},{5,4},{6,7},{7,6},{8,9},{9,8},{10,11... | collective-permute-start | bytes 614408 | tf_op jit(solution)/shard_map/ppermute | solution.py:259
  79.4 2.2 %collective-permute-start.29 = (bf16[160,640]{1,0:T(8,128)(2,1)S(1)}, bf16[160,640]{1,0:T(8,128)(2,1)S(1)}, u32[]{:S(2)}, u32[]{:S(2)}) collective-permute-start(bf16[160,640]{1,0:T(8,128)(2,1)S(1)} %get-tuple-element.39), channel_id=1, source_target_pairs={{0,2},{1,3},{2,0},{3,1},{4,6},{5,7},{6,4},{7,5},{8,10},{9,11},{10,... | collective-permute-start | bytes 614408 | tf_op jit(solution)/shard_map/ppermute | solution.py:259
  82.6 4.7 %cross.6 = (f32[160,640]{1,0:T(8,128)S(1)}, bf16[160,640]{1,0:T(8,128)(2,1)S(1)}, bf16[160,640]{1,0:T(8,128)(2,1)S(1)}, bf16[160,640]{1,0:T(8,128)(2,1)S(1)}) custom-call(s32[1]{0:T(128)} %bitcast.5.refs_0_, bf16[160,1536]{1,0:T(8,128)(2,1)S(1)} %copy-done, bf16[160,1536]{1,0:T(8,128)(2,1)S(1)} %collective-permute-done.1.refs_2_, ...), custom_call_target="tpu_custom_call" | custom-call | tf_op jit(solution)/shard_map/cross/pallas_call | solution.py:153
  88.1 5.1 %cross.5 = (f32[160,640]{1,0:T(8,128)S(1)}, bf16[160,640]{1,0:T(8,128)(2,1)S(1)}, bf16[160,640]{1,0:T(8,128)(2,1)}, bf16[160,640]{1,0:T(8,128)(2,1)}) custom-call(s32[1]{0:T(128)} %bitcast.5.refs_0_, bf16[160,1536]{1,0:T(8,128)(2,1)S(1)} %copy-done.1, bf16[160,1536]{1,0:T(8,128)(2,1)S(1)} %collective-permute-done.1.refs_2_, ...), custom_call_target="tpu_custom_call" | custom-call | tf_op jit(solution)/shard_map/cross/pallas_call | solution.py:153
  93.7 1.5 %collective-permute-start.25 = (bf16[160,640]{1,0:T(8,128)(2,1)S(1)}, bf16[160,640]{1,0:T(8,128)(2,1)S(1)}, u32[]{:S(2)}, u32[]{:S(2)}) collective-permute-start(bf16[160,640]{1,0:T(8,128)(2,1)S(1)} %get-tuple-element.35), channel_id=1, source_target_pairs={{0,2},{1,3},{2,0},{3,1},{4,6},{5,7},{6,4},{7,5},{8,10},{9,11},{10,... | collective-permute-start | bytes 614408 | tf_op jit(solution)/shard_map/ppermute | solution.py:259
  95.8 5.2 %cross.4 = (f32[160,640]{1,0:T(8,128)S(1)}, bf16[160,640]{1,0:T(8,128)(2,1)}, bf16[160,640]{1,0:T(8,128)(2,1)}, bf16[160,640]{1,0:T(8,128)(2,1)}) custom-call(s32[1]{0:T(128)} %bitcast.5.refs_0_, bf16[160,1536]{1,0:T(8,128)(2,1)S(1)} %copy-done.1, bf16[160,1536]{1,0:T(8,128)(2,1)S(1)} %collective-permute-done.1.refs_2_, ...), custom_call_target="tpu_custom_call" | custom-call | tf_op jit(solution)/shard_map/cross/pallas_call | solution.py:153
  102.7 1.4 %collective-permute-start.20 = (bf16[160,640]{1,0:T(8,128)(2,1)}, bf16[160,640]{1,0:T(8,128)(2,1)S(1)}, u32[]{:S(2)}, u32[]{:S(2)}) collective-permute-start(bf16[160,640]{1,0:T(8,128)(2,1)} %get-tuple-element.31), channel_id=1, source_target_pairs={{0,2},{1,3},{2,0},{3,1},{4,6},{5,7},{6,4},{7,5},{8,10},{9,11},{10,... | collective-permute-start | bytes 614408 | tf_op jit(solution)/shard_map/ppermute | solution.py:259
  106.3 3.2 %collective-permute-done.26.got_xc = bf16[160,640]{1,0:T(8,128)(2,1)S(1)} collective-permute-done((bf16[160,640]{1,0:T(8,128)(2,1)S(1)}, bf16[160,640]{1,0:T(8,128)(2,1)S(1)}, u32[]{:S(2)}, u32[]{:S(2)}) %collective-permute-start.26) | collective-permute-done | bytes 204832 | tf_op jit(solution)/shard_map/ppermute | solution.py:259
  114.6 2.1 %place.4.refs_0_ = f32[160,10240]{1,0:T(8,128)} custom-call(s32[5]{0:T(128)S(1)} %stack.86.meta, f32[160,640]{1,0:T(8,128)S(1)} %copy-done.14, bf16[160,640]{1,0:T(8,128)(2,1)S(1)} %copy-done.21, bf16[160,640]{1,0:T(8,128)(2,1)S(1)} %copy-done.23, bf16[160,640]{1,0:T(8,128)(2,1)S(1)} %copy-done.25), custom_call_target="tpu_custom_call" | custom-call | tf_op jit(solution)/shard_map/place/pallas_call | solution.py:194
  116.8 2.2 %place.5.refs_0_ = f32[160,10240]{1,0:T(8,128)} custom-call(s32[5]{0:T(128)S(1)} %stack.81.meta, f32[160,640]{1,0:T(8,128)S(1)} %copy-done.18, bf16[160,640]{1,0:T(8,128)(2,1)S(1)} %copy-done.27, bf16[160,640]{1,0:T(8,128)(2,1)S(1)} %copy-done.29, bf16[160,640]{1,0:T(8,128)(2,1)S(1)} %copy-done.31, ...), custom_call_target="tpu_custom_call", output_to_operand_aliasing={{}: (5, {})} | custom-call | tf_op jit(solution)/shard_map/place/pallas_call | solution.py:194
  119.0 2.2 %place.6.refs_0_ = f32[160,10240]{1,0:T(8,128)} custom-call(s32[5]{0:T(128)S(1)} %stack.76.meta, f32[160,640]{1,0:T(8,128)S(1)} %copy-done.16, bf16[160,640]{1,0:T(8,128)(2,1)S(1)} %collective-permute-done.19.got_c, bf16[160,640]{1,0:T(8,128)(2,1)S(1)} %collective-permute-done.20.got_x, ...), custom_call_target="tpu_custom_call", output_to_operand_aliasing={{}: (5, {})} | custom-call | tf_op jit(solution)/shard_map/place/pallas_call | solution.py:194
  122.0 4.6 %collective-permute-done.15.got_xc = bf16[160,640]{1,0:T(8,128)(2,1)S(1)} collective-permute-done((bf16[160,640]{1,0:T(8,128)(2,1)}, bf16[160,640]{1,0:T(8,128)(2,1)S(1)}, u32[]{:S(2)}, u32[]{:S(2)}) %collective-permute-start.15) | collective-permute-done | bytes 204832 | tf_op jit(solution)/shard_map/ppermute | solution.py:259
  126.5 2.1 %place.7 = f32[160,10240]{1,0:T(8,128)} custom-call(s32[5]{0:T(128)S(1)} %stack.71.meta, f32[160,640]{1,0:T(8,128)S(1)} %get-tuple-element.25.own, bf16[160,640]{1,0:T(8,128)(2,1)S(1)} %collective-permute-done.13.got_c, bf16[160,640]{1,0:T(8,128)(2,1)S(1)} %collective-permute-done.14.got_x, ...), custom_call_target="tpu_custom_call", output_to_operand_aliasing={{}: (5, {})} | custom-call | tf_op jit(solution)/shard_map/place/pallas_call | solution.py:194
  (111 shorter events, 27.6 us)
Async XLA Ops:
  9.7 8.8 %collective-permute-start = (bf16[960,128]{1,0:T(8,128)(2,1)S(1)}, bf16[960,128]{1,0:T(8,128)(2,1)S(1)}, u32[]{:S(2)}, u32[]{:S(2)}) collective-permute-start(bf16[960,128]{1,0:T(8,128)(2,1)S(1)} %get-tuple-element.24), channel_id=1, source_target_pairs={{0,64},{64,0},{1,65},{65,1},{2,66},{66,2},{3,67},{67,3},{4,68},{68... | collective-permute-start | bytes 737288 | tf_op jit(solution)/shard_map/ppermute | solution.py:255
  21.2 9.2 %collective-permute-start.4 = (bf16[160,1536]{1,0:T(8,128)(2,1)}, bf16[160,1536]{1,0:T(8,128)(2,1)S(1)}, u32[]{:S(2)}, u32[]{:S(2)}) collective-permute-start(bf16[160,1536]{1,0:T(8,128)(2,1)} %normalize.1.refs_1_.refs_5_), channel_id=1, source_target_pairs={{16,0},{5,1},{18,2},{7,3},{20,4},{9,5},{22,6},{11,7},{24,8},{13,9}... | collective-permute-start | bytes 1474568 | tf_op jit(solution)/shard_map/ppermute | solution.py:259
  24.3 10.5 %collective-permute-start.27 = (bf16[160,1536]{1,0:T(8,128)(2,1)}, bf16[160,1536]{1,0:T(8,128)(2,1)S(1)}, u32[]{:S(2)}, u32[]{:S(2)}) collective-permute-start(bf16[160,1536]{1,0:T(8,128)(2,1)} %normalize.1.refs_1_.refs_5_), channel_id=1, source_target_pairs={{12,0},{49,1},{14,2},{51,3},{0,4},{53,5},{2,6},{55,7},{4,8},{57,9}... | collective-permute-start | bytes 1474568 | tf_op jit(solution)/shard_map/ppermute | solution.py:259
  26.0 18.3 %collective-permute-start.17 = (bf16[160,1536]{1,0:T(8,128)(2,1)}, bf16[160,1536]{1,0:T(8,128)(2,1)S(1)}, u32[]{:S(2)}, u32[]{:S(2)}) collective-permute-start(bf16[160,1536]{1,0:T(8,128)(2,1)} %normalize.1.refs_1_.refs_5_), channel_id=1, source_target_pairs={{4,0},{17,1},{6,2},{19,3},{8,4},{21,5},{10,6},{23,7},{12,8},{25,9}... | collective-permute-start | bytes 1474568 | tf_op jit(solution)/shard_map/ppermute | solution.py:259
  28.1 17.0 %collective-permute-start.9 = (bf16[160,1536]{1,0:T(8,128)(2,1)}, bf16[160,1536]{1,0:T(8,128)(2,1)S(1)}, u32[]{:S(2)}, u32[]{:S(2)}) collective-permute-start(bf16[160,1536]{1,0:T(8,128)(2,1)} %normalize.1.refs_1_.refs_5_), channel_id=1, source_target_pairs={{48,0},{13,1},{50,2},{15,3},{52,4},{1,5},{54,6},{3,7},{56,8},{5,9}... | collective-permute-start | bytes 1474568 | tf_op jit(solution)/shard_map/ppermute | solution.py:259
  30.4 14.7 %collective-permute-start.7 = (bf16[160,1536]{1,0:T(8,128)(2,1)S(1)}, bf16[160,1536]{1,0:T(8,128)(2,1)S(1)}, u32[]{:S(2)}, u32[]{:S(2)}) collective-permute-start(bf16[160,1536]{1,0:T(8,128)(2,1)S(1)} %collective-permute-done.4.refs_5_), channel_id=1, source_target_pairs={{16,0},{5,1},{18,2},{7,3},{20,4},{9,5},{22,6},{11,7},{24,8},{13,9}... | collective-permute-start | bytes 1474568 | tf_op jit(solution)/shard_map/ppermute | solution.py:259
  33.4 13.2 %collective-permute-start.2 = (bf16[160,1536]{1,0:T(8,128)(2,1)}, bf16[160,1536]{1,0:T(8,128)(2,1)S(1)}, u32[]{:S(2)}, u32[]{:S(2)}) collective-permute-start(bf16[160,1536]{1,0:T(8,128)(2,1)} %normalize.1.refs_1_.refs_5_), channel_id=1, source_target_pairs={{0,2},{1,3},{2,0},{3,1},{4,6},{5,7},{6,4},{7,5},{8,10},{9,11},{10,... | collective-permute-start | bytes 1474568 | tf_op jit(solution)/shard_map/ppermute | solution.py:259
  35.6 14.6 %collective-permute-start.1 = (bf16[160,1536]{1,0:T(8,128)(2,1)}, bf16[160,1536]{1,0:T(8,128)(2,1)S(1)}, u32[]{:S(2)}, u32[]{:S(2)}) collective-permute-start(bf16[160,1536]{1,0:T(8,128)(2,1)} %normalize.1.refs_1_.refs_5_), channel_id=1, source_target_pairs={{0,1},{1,0},{2,3},{3,2},{4,5},{5,4},{6,7},{7,6},{8,9},{9,8},{10,11... | collective-permute-start | bytes 1474568 | tf_op jit(solution)/shard_map/ppermute | solution.py:259
  44.3 8.9 %collective-permute-start.18 = (bf16[160,1536]{1,0:T(8,128)(2,1)S(1)}, bf16[160,1536]{1,0:T(8,128)(2,1)S(1)}, u32[]{:S(2)}, u32[]{:S(2)}) collective-permute-start(bf16[160,1536]{1,0:T(8,128)(2,1)S(1)} %collective-permute-done.17.refs_6_), channel_id=1, source_target_pairs={{4,0},{17,1},{6,2},{19,3},{8,4},{21,5},{10,6},{23,7},{12,8},{25,9}... | collective-permute-start | bytes 1474568 | tf_op jit(solution)/shard_map/ppermute | solution.py:259
  45.1 13.4 %collective-permute-start.23 = (bf16[160,1536]{1,0:T(8,128)(2,1)S(1)}, bf16[160,1536]{1,0:T(8,128)(2,1)S(1)}, u32[]{:S(2)}, u32[]{:S(2)}) collective-permute-start(bf16[160,1536]{1,0:T(8,128)(2,1)S(1)} %collective-permute-done.9.refs_7_), channel_id=1, source_target_pairs={{4,0},{17,1},{6,2},{19,3},{8,4},{21,5},{10,6},{23,7},{12,8},{25,9}... | collective-permute-start | bytes 1474568 | tf_op jit(solution)/shard_map/ppermute | solution.py:259
  45.1 14.2 %collective-permute-start.12 = (bf16[160,1536]{1,0:T(8,128)(2,1)S(1)}, bf16[160,1536]{1,0:T(8,128)(2,1)S(1)}, u32[]{:S(2)}, u32[]{:S(2)}) collective-permute-start(bf16[160,1536]{1,0:T(8,128)(2,1)S(1)} %collective-permute-done.7.refs_7_), channel_id=1, source_target_pairs={{12,0},{49,1},{14,2},{51,3},{0,4},{53,5},{2,6},{55,7},{4,8},{57,9}... | collective-permute-start | bytes 1474568 | tf_op jit(solution)/shard_map/ppermute | solution.py:259
  46.6 14.0 %collective-permute-start.10 = (bf16[160,1536]{1,0:T(8,128)(2,1)S(1)}, bf16[160,1536]{1,0:T(8,128)(2,1)}, u32[]{:S(2)}, u32[]{:S(2)}) collective-permute-start(bf16[160,1536]{1,0:T(8,128)(2,1)S(1)} %collective-permute-done.9.refs_7_), channel_id=1, source_target_pairs={{12,0},{49,1},{14,2},{51,3},{0,4},{53,5},{2,6},{55,7},{4,8},{57,9}... | collective-permute-start | bytes 1474568 | tf_op jit(solution)/shard_map/ppermute | solution.py:259
  50.2 13.5 %collective-permute-start.5 = (bf16[160,1536]{1,0:T(8,128)(2,1)S(1)}, bf16[160,1536]{1,0:T(8,128)(2,1)S(1)}, u32[]{:S(2)}, u32[]{:S(2)}) collective-permute-start(bf16[160,1536]{1,0:T(8,128)(2,1)S(1)} %collective-permute-done.4.refs_5_), channel_id=1, source_target_pairs={{4,0},{17,1},{6,2},{19,3},{8,4},{21,5},{10,6},{23,7},{12,8},{25,9}... | collective-permute-start | bytes 1474568 | tf_op jit(solution)/shard_map/ppermute | solution.py:259
  54.0 13.3 %collective-permute-start.3 = (bf16[160,1536]{1,0:T(8,128)(2,1)S(1)}, bf16[160,1536]{1,0:T(8,128)(2,1)S(1)}, u32[]{:S(2)}, u32[]{:S(2)}) collective-permute-start(bf16[160,1536]{1,0:T(8,128)(2,1)S(1)} %collective-permute-done.2.refs_3_), channel_id=1, source_target_pairs={{0,1},{1,0},{2,3},{3,2},{4,5},{5,4},{6,7},{7,6},{8,9},{9,8},{10,11... | collective-permute-start | bytes 1474568 | tf_op jit(solution)/shard_map/ppermute | solution.py:259
  59.3 17.2 %collective-permute-start.22 = (bf16[160,1536]{1,0:T(8,128)(2,1)S(1)}, bf16[160,1536]{1,0:T(8,128)(2,1)}, u32[]{:S(2)}, u32[]{:S(2)}) collective-permute-start(bf16[160,1536]{1,0:T(8,128)(2,1)S(1)} %collective-permute-done.4.refs_5_), channel_id=1, source_target_pairs={{12,0},{49,1},{14,2},{51,3},{0,4},{53,5},{2,6},{55,7},{4,8},{57,9}... | collective-permute-start | bytes 1474568 | tf_op jit(solution)/shard_map/ppermute | solution.py:259
  59.3 20.1 %collective-permute-start.16 = (bf16[160,1536]{1,0:T(8,128)(2,1)S(1)}, bf16[160,1536]{1,0:T(8,128)(2,1)}, u32[]{:S(2)}, u32[]{:S(2)}) collective-permute-start(bf16[160,1536]{1,0:T(8,128)(2,1)S(1)} %collective-permute-done.12.refs_8_), channel_id=1, source_target_pairs={{12,0},{49,1},{14,2},{51,3},{0,4},{53,5},{2,6},{55,7},{4,8},{57,9}... | collective-permute-start | bytes 1474568 | tf_op jit(solution)/shard_map/ppermute | solution.py:259
  60.6 33.1 %collective-permute-start.11 = (bf16[160,1536]{1,0:T(8,128)(2,1)}, bf16[160,1536]{1,0:T(8,128)(2,1)}, u32[]{:S(2)}, u32[]{:S(2)}) collective-permute-start(bf16[160,1536]{1,0:T(8,128)(2,1)} %collective-permute-done.10.refs_6_), channel_id=1, source_target_pairs={{12,0},{49,1},{14,2},{51,3},{0,4},{53,5},{2,6},{55,7},{4,8},{57,9}... | collective-permute-start | bytes 1474568 | tf_op jit(solution)/shard_map/ppermute | solution.py:259
  63.7 31.5 %collective-permute-start.8 = (bf16[160,1536]{1,0:T(8,128)(2,1)S(1)}, bf16[160,1536]{1,0:T(8,128)(2,1)}, u32[]{:S(2)}, u32[]{:S(2)}) collective-permute-start(bf16[160,1536]{1,0:T(8,128)(2,1)S(1)} %collective-permute-done.7.refs_7_), channel_id=1, source_target_pairs={{4,0},{17,1},{6,2},{19,3},{8,4},{21,5},{10,6},{23,7},{12,8},{25,9}... | collective-permute-start | bytes 1474568 | tf_op jit(solution)/shard_map/ppermute | solution.py:259
  67.3 28.4 %collective-permute-start.6 = (bf16[160,1536]{1,0:T(8,128)(2,1)S(1)}, bf16[160,1536]{1,0:T(8,128)(2,1)}, u32[]{:S(2)}, u32[]{:S(2)}) collective-permute-start(bf16[160,1536]{1,0:T(8,128)(2,1)S(1)} %collective-permute-done.5.refs_5_), channel_id=1, source_target_pairs={{4,0},{17,1},{6,2},{19,3},{8,4},{21,5},{10,6},{23,7},{12,8},{25,9}... | collective-permute-start | bytes 1474568 | tf_op jit(solution)/shard_map/ppermute | solution.py:259
  76.5 16.7 %collective-permute-start.28 = (bf16[160,640]{1,0:T(8,128)(2,1)S(1)}, bf16[160,640]{1,0:T(8,128)(2,1)S(1)}, u32[]{:S(2)}, u32[]{:S(2)}) collective-permute-start(bf16[160,640]{1,0:T(8,128)(2,1)S(1)} %get-tuple-element.38), channel_id=1, source_target_pairs={{0,1},{1,0},{2,3},{3,2},{4,5},{5,4},{6,7},{7,6},{8,9},{9,8},{10,11... | collective-permute-start | bytes 614408 | tf_op jit(solution)/shard_map/ppermute | solution.py:259
  79.4 14.0 %collective-permute-start.29 = (bf16[160,640]{1,0:T(8,128)(2,1)S(1)}, bf16[160,640]{1,0:T(8,128)(2,1)S(1)}, u32[]{:S(2)}, u32[]{:S(2)}) collective-permute-start(bf16[160,640]{1,0:T(8,128)(2,1)S(1)} %get-tuple-element.39), channel_id=1, source_target_pairs={{0,2},{1,3},{2,0},{3,1},{4,6},{5,7},{6,4},{7,5},{8,10},{9,11},{10,... | collective-permute-start | bytes 614408 | tf_op jit(solution)/shard_map/ppermute | solution.py:259
  82.6 29.2 %copy-start.14 = (f32[160,640]{1,0:T(8,128)S(1)}, f32[160,640]{1,0:T(8,128)}, u32[]{:S(2)}) copy-start(f32[160,640]{1,0:T(8,128)} %copy-done.13) | copy-start | bytes 1228804
  93.3 7.7 %collective-permute-start.30 = (bf16[160,640]{1,0:T(8,128)(2,1)S(1)}, bf16[160,640]{1,0:T(8,128)(2,1)S(1)}, u32[]{:S(2)}, u32[]{:S(2)}) collective-permute-start(bf16[160,640]{1,0:T(8,128)(2,1)S(1)} %get-tuple-element.40), channel_id=1, source_target_pairs={{0,3},{1,2},{2,1},{3,0},{4,7},{5,6},{6,5},{7,4},{8,11},{9,10},{10,... | collective-permute-start | bytes 614408 | tf_op jit(solution)/shard_map/ppermute | solution.py:259
  93.4 8.6 %collective-permute-start.24 = (bf16[160,640]{1,0:T(8,128)(2,1)S(1)}, bf16[160,640]{1,0:T(8,128)(2,1)S(1)}, u32[]{:S(2)}, u32[]{:S(2)}) collective-permute-start(bf16[160,640]{1,0:T(8,128)(2,1)S(1)} %get-tuple-element.34), channel_id=1, source_target_pairs={{0,1},{1,0},{2,3},{3,2},{4,5},{5,4},{6,7},{7,6},{8,9},{9,8},{10,11... | collective-permute-start | bytes 614408 | tf_op jit(solution)/shard_map/ppermute | solution.py:259
  93.7 10.7 %collective-permute-start.25 = (bf16[160,640]{1,0:T(8,128)(2,1)S(1)}, bf16[160,640]{1,0:T(8,128)(2,1)S(1)}, u32[]{:S(2)}, u32[]{:S(2)}) collective-permute-start(bf16[160,640]{1,0:T(8,128)(2,1)S(1)} %get-tuple-element.35), channel_id=1, source_target_pairs={{0,2},{1,3},{2,0},{3,1},{4,6},{5,7},{6,4},{7,5},{8,10},{9,11},{10,... | collective-permute-start | bytes 614408 | tf_op jit(solution)/shard_map/ppermute | solution.py:259
  95.2 14.2 %collective-permute-start.26 = (bf16[160,640]{1,0:T(8,128)(2,1)S(1)}, bf16[160,640]{1,0:T(8,128)(2,1)S(1)}, u32[]{:S(2)}, u32[]{:S(2)}) collective-permute-start(bf16[160,640]{1,0:T(8,128)(2,1)S(1)} %get-tuple-element.36), channel_id=1, source_target_pairs={{0,3},{1,2},{2,1},{3,0},{4,7},{5,6},{6,5},{7,4},{8,11},{9,10},{10,... | collective-permute-start | bytes 614408 | tf_op jit(solution)/shard_map/ppermute | solution.py:259
  95.6 14.5 %collective-permute-start.19 = (bf16[160,640]{1,0:T(8,128)(2,1)S(1)}, bf16[160,640]{1,0:T(8,128)(2,1)S(1)}, u32[]{:S(2)}, u32[]{:S(2)}) collective-permute-start(bf16[160,640]{1,0:T(8,128)(2,1)S(1)} %get-tuple-element.30), channel_id=1, source_target_pairs={{0,1},{1,0},{2,3},{3,2},{4,5},{5,4},{6,7},{7,6},{8,9},{9,8},{10,11... | collective-permute-start | bytes 614408 | tf_op jit(solution)/shard_map/ppermute | solution.py:259
  101.7 19.5 %collective-permute-start.13 = (bf16[160,640]{1,0:T(8,128)(2,1)}, bf16[160,640]{1,0:T(8,128)(2,1)S(1)}, u32[]{:S(2)}, u32[]{:S(2)}) collective-permute-start(bf16[160,640]{1,0:T(8,128)(2,1)} %get-tuple-element.26), channel_id=1, source_target_pairs={{0,1},{1,0},{2,3},{3,2},{4,5},{5,4},{6,7},{7,6},{8,9},{9,8},{10,11... | collective-permute-start | bytes 614408 | tf_op jit(solution)/shard_map/ppermute | solution.py:259
  102.7 16.3 %collective-permute-start.20 = (bf16[160,640]{1,0:T(8,128)(2,1)}, bf16[160,640]{1,0:T(8,128)(2,1)S(1)}, u32[]{:S(2)}, u32[]{:S(2)}) collective-permute-start(bf16[160,640]{1,0:T(8,128)(2,1)} %get-tuple-element.31), channel_id=1, source_target_pairs={{0,2},{1,3},{2,0},{3,1},{4,6},{5,7},{6,4},{7,5},{8,10},{9,11},{10,... | collective-permute-start | bytes 614408 | tf_op jit(solution)/shard_map/ppermute | solution.py:259
  105.1 13.9 %collective-permute-start.21 = (bf16[160,640]{1,0:T(8,128)(2,1)}, bf16[160,640]{1,0:T(8,128)(2,1)S(1)}, u32[]{:S(2)}, u32[]{:S(2)}) collective-permute-start(bf16[160,640]{1,0:T(8,128)(2,1)} %get-tuple-element.32), channel_id=1, source_target_pairs={{0,3},{1,2},{2,1},{3,0},{4,7},{5,6},{6,5},{7,4},{8,11},{9,10},{10,... | collective-permute-start | bytes 614408 | tf_op jit(solution)/shard_map/ppermute | solution.py:259
  110.1 11.8 %collective-permute-start.14 = (bf16[160,640]{1,0:T(8,128)(2,1)}, bf16[160,640]{1,0:T(8,128)(2,1)S(1)}, u32[]{:S(2)}, u32[]{:S(2)}) collective-permute-start(bf16[160,640]{1,0:T(8,128)(2,1)} %get-tuple-element.27), channel_id=1, source_target_pairs={{0,2},{1,3},{2,0},{3,1},{4,6},{5,7},{6,4},{7,5},{8,10},{9,11},{10,... | collective-permute-start | bytes 614408 | tf_op jit(solution)/shard_map/ppermute | solution.py:259
  110.1 16.4 %collective-permute-start.15 = (bf16[160,640]{1,0:T(8,128)(2,1)}, bf16[160,640]{1,0:T(8,128)(2,1)S(1)}, u32[]{:S(2)}, u32[]{:S(2)}) collective-permute-start(bf16[160,640]{1,0:T(8,128)(2,1)} %get-tuple-element.28), channel_id=1, source_target_pairs={{0,3},{1,2},{2,1},{3,0},{4,7},{5,6},{6,5},{7,4},{8,11},{9,10},{10,... | collective-permute-start | bytes 614408 | tf_op jit(solution)/shard_map/ppermute | solution.py:259
  (32 other events, 108.4 us)

commit v2 on v0

v2 whole, which is shorter than its diff:
```python
import math

import jax
import jax.numpy as jnp
from jax import lax
from jax.experimental import pallas as pl
from jax.experimental.pallas import tpu as pltpu
from jax.sharding import PartitionSpec as P

SAMPLES = 4096
BINS = 64
WINS = 6
ROWS = 160
DEPTH = 1536
GROUP = 640
STEP_ROWS = 320
CHUNK = 1024
LOAD = 2
PARTS = 128
TURN = 2.0 * math.pi / SAMPLES


def whiten_kernel(start, width_ref, x_hbm, keep_ref, send_ref, held, table, total, sems):
    def fetch(piece):
        block = pl.ds(piece * ROWS, ROWS)
        return pltpu.make_async_copy(x_hbm.at[block], held.at[block], sems.at[piece])

    for piece in range(0, WINS):
        fetch(piece).start()
    lane = lax.broadcasted_iota(jnp.int32, (1, 128), 1)
    freq = jnp.where(lane < BINS, start[0] + lane, start[1] + lane - BINS)
    coarse = lax.broadcasted_iota(jnp.int32, (SAMPLES // PARTS, 128), 0) * PARTS
    fine = lax.broadcasted_iota(jnp.int32, (PARTS, 128), 0)
    angle_a = ((freq * coarse) & (SAMPLES - 1)).astype(jnp.float32) * TURN
    angle_b = ((freq * fine) & (SAMPLES - 1)).astype(jnp.float32) * TURN
    root = 1.0 / math.sqrt(SAMPLES)
    cos_a, sin_a = jnp.cos(angle_a) * root, jnp.sin(angle_a) * root
    cos_b, sin_b = jnp.cos(angle_b), jnp.sin(angle_b)
    row = lax.broadcasted_iota(jnp.int32, (256, 128), 0) & 127
    col = lax.broadcasted_iota(jnp.int32, (256, 128), 1)
    half = jnp.where(col < BINS, width_ref[0], width_ref[1])
    inside = ((row < BINS) == (col < BINS)) & (jnp.abs(row - col) <= half)
    mask = inside.astype(jnp.float32).astype(jnp.bfloat16)
    bin_id = lane & (BINS - 1)
    width = jnp.where(lane < BINS, width_ref[0], width_ref[1])
    count = jnp.minimum(bin_id + width, BINS - 1) - jnp.maximum(bin_id - width, 0) + 1
    share = 1.0 / count.astype(jnp.float32)
    first = lax.broadcasted_iota(jnp.int32, (STEP_ROWS, 128), 1) < BINS
    mine = lax.axis_index("band") == 0

    for part in range(SAMPLES // PARTS):
        at = slice(part * PARTS, (part + 1) * PARTS)
        ca, sa = cos_a[part : part + 1], sin_a[part : part + 1]
        table[at, 0:128] = (ca * cos_b - sa * sin_b).astype(jnp.bfloat16)
        table[at, 128:256] = (-(sa * cos_b + ca * sin_b)).astype(jnp.bfloat16)

    for piece in range(0, WINS, LOAD):
        for i in range(LOAD):
            fetch(piece + i).wait()
        block = slice(piece * ROWS, (piece + LOAD) * ROWS)
        for at in range(0, SAMPLES, CHUNK):
            product = jnp.dot(
                held[block, at : at + CHUNK],
                table[at : at + CHUNK, :],
                preferred_element_type=jnp.float32,
            )
            if at == 0:
                total[block, :] = product
            else:
                total[block, :] += product

    for at in range(0, WINS * ROWS, STEP_ROWS):
        block = slice(at, at + STEP_ROWS)
        re, im = total[block, :128], total[block, 128:]
        amplitude = jnp.sqrt(re * re + im * im)
        high = amplitude.astype(jnp.bfloat16)
        low = (amplitude - high.astype(jnp.float32)).astype(jnp.bfloat16)
        sums = jnp.dot(
            jnp.concatenate([high, low], axis=1), mask, preferred_element_type=jnp.float32
        )
        gain = 1.0 / (sums * share + 1e-05)
        re, im = re * gain, im * gain
        turned = pltpu.roll(im, BINS, 1)
        band0 = jnp.where(first, re, turned)
        band1 = jnp.where(first, turned, re)
        keep_ref[block, :] = jnp.where(mine, band0, band1).astype(jnp.bfloat16)
        send_ref[block, :] = jnp.where(mine, band1, band0).astype(jnp.bfloat16)


def whiten(flat, band_start, half_width):
    total = flat.shape[0]
    out = jax.ShapeDtypeStruct((total, 128), jnp.bfloat16)
    return pl.pallas_call(
        whiten_kernel,
        in_specs=[
            pl.BlockSpec(memory_space=pltpu.SMEM),
            pl.BlockSpec(memory_space=pltpu.SMEM),
            pl.BlockSpec(memory_space=pltpu.HBM),
        ],
        out_shape=[out, out],
        scratch_shapes=[
            pltpu.VMEM((total, SAMPLES), jnp.bfloat16),
            pltpu.VMEM((SAMPLES, 256), jnp.bfloat16),
            pltpu.VMEM((total, 256), jnp.float32),
            pltpu.SemaphoreType.DMA((WINS,)),
        ],
        compiler_params=pltpu.CompilerParams(vmem_limit_bytes=57 << 20),
        name="whiten",
    )(band_start, half_width, flat)


def normalize_kernel(keep_ref, got_ref, out_ref):
    energy = jnp.zeros((ROWS, 128), jnp.float32)
    for ref in (keep_ref, got_ref):
        for win in range(WINS):
            value = ref[win * ROWS : (win + 1) * ROWS, :].astype(jnp.float32)
            energy = energy + value * value
    scale = 1.0 / jnp.sqrt(jnp.sum(energy, axis=1, keepdims=True) + 1e-06)
    for side, ref in enumerate((keep_ref, got_ref)):
        for win in range(WINS):
            value = ref[win * ROWS : (win + 1) * ROWS, :].astype(jnp.float32)
            at = (side * WINS + win) * 128
            out_ref[:, at : at + 128] = (value * scale).astype(jnp.bfloat16)


def normalize(keep, got):
    return pl.pallas_call(
        normalize_kernel,
        out_shape=jax.ShapeDtypeStruct((ROWS, DEPTH), jnp.bfloat16),
        compiler_params=pltpu.CompilerParams(vmem_limit_bytes=8 << 20),
        name="normalize",
    )(keep, got)


def stack_kernel(*refs):
    at = 0
    for ref in refs[:-1]:
        refs[-1][at : at + ref.shape[0], :] = ref[...]
        at += ref.shape[0]


def stack(*shards):
    total = sum(shard.shape[0] for shard in shards)
    return pl.pallas_call(
        stack_kernel,
        out_shape=jax.ShapeDtypeStruct((total, DEPTH), jnp.bfloat16),
        compiler_params=pltpu.CompilerParams(vmem_limit_bytes=8 << 20),
        name="stack",
    )(*shards)


def cross_kernel(rows, first, second, mine_ref, c_ref, x_ref, *refs):
    cols = refs[-1]
    half = GROUP // 2
    cols[:half, :] = first[...]
    cols[half:, :] = second[...]
    product = lax.dot_general(
        rows[...], cols[...], (((1,), (1,)), ((), ())), preferred_element_type=jnp.float32
    )
    mine_ref[...] = product[:ROWS]
    to_x = product[ROWS : 2 * ROWS].astype(jnp.bfloat16)
    c_ref[...] = product[2 * ROWS : 3 * ROWS].astype(jnp.bfloat16)
    to_xc = product[3 * ROWS :].astype(jnp.bfloat16)
    if len(refs) == 1:
        x_ref[:, :GROUP] = to_x
        x_ref[:, GROUP:] = to_xc
    else:
        x_ref[...] = to_x
        refs[0][...] = to_xc


def cross(rows, first, second, merged):
    narrow = jax.ShapeDtypeStruct((ROWS, GROUP), jnp.bfloat16)
    wide = jax.ShapeDtypeStruct((ROWS, 2 * GROUP), jnp.bfloat16)
    mine = jax.ShapeDtypeStruct((ROWS, GROUP), jnp.float32)
    return pl.pallas_call(
        cross_kernel,
        out_shape=[mine, narrow, wide] if merged else [mine, narrow, narrow, narrow],
        scratch_shapes=[pltpu.VMEM((4 * ROWS, DEPTH), jnp.bfloat16)],
        compiler_params=pltpu.CompilerParams(vmem_limit_bytes=12 << 20),
        cost_estimate=pl.CostEstimate(
            flops=2 * GROUP * GROUP * DEPTH, transcendentals=0, bytes_accessed=12 << 20
        ),
        name="cross",
    )(rows, first, second)


NEAR = (0, 1, -1, 2)
GROUPS = (
    ((0, 0), (1, 0), (-1, 0), (2, 0)),
    ((0, 1), (1, 1), (-1, -1), (2, -1)),
    ((-1, 1), (2, 1), (0, -1), (1, -1)),
    ((0, 2), (1, 2), (-1, 2), (2, 2)),
)
SPOT = {offset: (g, i) for g, group in enumerate(GROUPS) for i, offset in enumerate(group)}


def place_kernel(blocks, groups, kinds, *refs):
    out, buf, sems = refs[-3:]
    pieces = {}
    for index, kind in enumerate(kinds):
        pieces[kind] = refs[index]
    chan = lax.axis_index("chan")
    z, y, spot, core = chan // 16, (chan // 4) % 4, chan % 4, chan % 2

    def copy(n):
        du, dv = blocks[n]
        dz, dy = jnp.where(core == 0, du, dv), jnp.where(core == 0, dv, du)
        unit_id = ((z + dz + 4) % 4) * 4 + (y + dy + 4) % 4
        start = pl.multiple_of(unit_id * GROUP, 128)
        return pltpu.make_async_copy(buf.at[n], out.at[:, pl.ds(start, GROUP)], sems.at[n])

    for slot in range(4):

        @pl.when(spot == slot)
        def _():
            for n, (du, dv) in enumerate(blocks):
                for turn in range(4):
                    g, i = SPOT[(dv, du) if turn % 2 else (du, dv)]
                    ref, base = pieces[turn, g], 0
                    if ref.shape[1] == 2 * GROUP and turn == 3:
                        base = GROUP
                    value = ref[:, base + i * ROWS : base + (i + 1) * ROWS].astype(jnp.float32)
                    at = (slot ^ turn) * ROWS
                    buf[n, :, at : at + ROWS] = value
                copy(n).start()

    for n in range(len(blocks)):
        copy(n).wait()


def place(blocks, pieces, out):
    vmem = pl.BlockSpec(memory_space=pltpu.VMEM)
    groups = sorted({g for _, g in pieces})
    kinds = sorted(pieces)
    prior = () if out is None else (out,)
    return pl.pallas_call(
        lambda *refs: place_kernel(blocks, groups, kinds, *refs),
        in_specs=[vmem] * len(kinds) + [pl.BlockSpec(memory_space=pl.ANY)] * len(prior),
        out_specs=pl.BlockSpec(memory_space=pl.ANY),
        out_shape=jax.ShapeDtypeStruct((ROWS, 16 * GROUP), jnp.float32),
        scratch_shapes=[
            pltpu.VMEM((len(blocks), ROWS, GROUP), jnp.float32),
            pltpu.SemaphoreType.DMA((len(blocks),)),
        ],
        input_output_aliases={len(kinds): 0} if prior else {},
        compiler_params=pltpu.CompilerParams(vmem_limit_bytes=16 << 20),
        name="place",
    )(*[pieces[kind] for kind in kinds], *prior)


def unit(index):
    return index // 16, index // 4 % 4, index // 2 % 2, index % 2


def join(z, y, x, c):
    return (z % 4) * 16 + (y % 4) * 4 + x * 2 + c


def from_first(shift):
    pairs = []
    for dst in range(64):
        z, y, x, c = unit(dst)
        src = join(z + shift, y, x, c) if c == 0 else join(z, y + shift, x, c)
        pairs.append((src, dst))
    return pairs


def from_second(shift):
    pairs = []
    for dst in range(64):
        z, y, x, c = unit(dst)
        src = join(z, y + shift, x, c) if c == 0 else join(z + shift, y, x, c)
        pairs.append((src, dst))
    return pairs


def flip(bits):
    return [(i, i ^ bits) for i in range(64)]


def local(traces, band_start, half_width):
    flat = jnp.transpose(traces, (1, 0, 2)).reshape(WINS * ROWS, SAMPLES)
    keep, send = whiten(flat, band_start, half_width)
    got = lax.ppermute(send, "band", [(0, 1), (1, 0)])
    own = normalize(keep, got)
    hold = lax.optimization_barrier

    def move(value, pairs):
        return lax.ppermute(value, "chan", pairs)

    ahead, behind = move(own, from_first(1)), move(own, from_first(-1))
    far, over = move(own, from_first(2)), move(own, flip(2))
    ahead, behind, far = hold((ahead, behind, far))
    pair0, pair1 = stack(own, ahead), stack(behind, far)
    up0, down1 = move(pair0, from_second(1)), move(pair1, from_second(-1))
    up1, down0 = move(pair1, from_second(1)), move(pair0, from_second(-1))
    mates = stack(own, over)
    rows = stack(mates, move(mates, flip(1)))
    mine0, c0, x0 = cross(rows, pair0, pair1, True)
    x0 = move(x0, flip(2))
    c0 = move(c0, flip(1))
    mine1, c1, x1 = cross(rows, up0, down1, True)
    x1 = move(x1, flip(2))
    up0, down1, up1, down0, x0, c0, x1, c1 = hold((up0, down1, up1, down0, x0, c0, x1, c1))
    up2, down2 = move(up0, from_second(1)), move(down1, from_second(-1))
    mine2, c2, x2 = cross(rows, up1, down0, True)
    x2 = move(x2, flip(2))
    xc0 = move(x0, flip(1))
    c1 = move(c1, flip(1))
    c2 = move(c2, flip(1))
    up2, down2, x2, c2, xc0, c1, x1 = hold((up2, down2, x2, c2, xc0, c1, x1))
    mine3, c3, x3, xc3 = cross(rows, up2, down2, False)
    x3, xc3, c3 = move(x3, flip(2)), move(xc3, flip(3)), move(c3, flip(1))
    xc1 = move(x1, flip(1))
    xc2 = move(x2, flip(1))
    early = [(du, dv) for du in NEAR for dv in NEAR if du != 2 and dv != 2]
    late = [(du, dv) for du in NEAR for dv in NEAR if du == 2 or dv == 2]
    pieces = {}
    for g, parts in enumerate(((mine0, c0, x0, xc0), (mine1, c1, x1, xc1), (mine2, c2, x2, xc2))):
        for turn in range(4):
            pieces[turn, g] = parts[turn]
    out = place(early, pieces, None)
    for turn, part in enumerate((mine3, c3, x3, xc3)):
        pieces[turn, 3] = part
    return place(late, pieces, out)[None]


def solution(mesh):
    placed = (P("chan", "band", None), P(), P())
    return jax.shard_map(
        local, mesh=mesh, in_specs=placed, out_specs=P("band", "chan", None), check_vma=False
    )
```

time: 279 us -> 98.5 us (0.35)
  waiting for transfers between devices: 178 us -> 42.1 us
  starting transfers between devices: 0.01 us -> 36.3 us
  local copies, waits for them, and re-layouts: 30.2 us -> 0.94 us
  matrix products: 25 us -> 0 us
  Pallas kernels: 0 us -> 18.7 us
  other arithmetic: 18.3 us -> 0 us
  between operations: 13.5 us -> 0.27 us
  blocking collectives: 12.9 us -> 0 us
    all_gather x1 -> x0, waiting for transfers between devices: 178 us -> none  [local(): lax.all_gather(normed, 'chan', axis=0, tiled=True)]
    ppermute x0 -> x24, waiting for transfers between devices: none -> 42.1 us  [the longest x23 36.7 us: move(): return lax.ppermute(value, 'chan', pairs)]
    ppermute x0 -> x24, starting transfers between devices: none -> 36.3 us  [the longest x23 32.7 us: move(): return lax.ppermute(value, 'chan', pairs)]
    dot_general x3 -> x0, matrix products: 25 us -> none  [the longest x1 17.5 us: cross_rows(): jnp.einsum('ck,dk->cd', normed, shard_rows, preferred_element_type=jnp.fl...]
    pallas_call x0 -> x12, Pallas kernels: none -> 18.7 us  [the longest x1 7.4 us: whiten(): pl.pallas_call(whiten_kernel, in_specs=[pl.BlockSpec(memory_space=pltpu.S...]
    reshape x3 -> x0, local copies, waits for them, and re-layouts: 15.2 us -> none  [the longest x1 12.2 us: whiten(): flat = trace_block.reshape(rows_here * wins_here, SAMPLES)]
    all_to_all x1 -> x0, blocking collectives: 12.9 us -> none  [local(): lax.all_to_all(whitened, 'band', split_axis=2, concat_axis=1, tiled=True)]
    unnamed x5 -> x2, local copies, waits for them, and re-layouts: 12.6 us -> 0.94 us
  transfers between devices with their start and end apart: 1 -> 24, of which waited for: 1 -> 12; matrix products, arithmetic and copies ran while one was open for 0% -> 0% of each run, Pallas kernels for 0% -> 9%
where the time goes in v2:
time: 98.5 us; the launch traced here: 98.3 us
  waiting for transfers between devices  42.1 us (43%)
  starting transfers between devices  36.3 us (37%)
  Pallas kernels  18.7 us (19%)
    ppermute x23, waiting for transfers between devices, move(): return lax.ppermute(value, 'chan', pairs)  36.7 us
    ppermute x23, starting transfers between devices, move(): return lax.ppermute(value, 'chan', pairs)  32.7 us
    pallas_call x1, Pallas kernels, whiten(): pl.pallas_call(whiten_kernel, in_specs=[pl.BlockSpec(memory_space=pltpu.S...  7.4 us
    pallas_call x4, Pallas kernels, cross(): pl.pallas_call(cross_kernel, out_shape=[mine, narrow, wide] if merged els...  6.87 us
    ppermute x1, waiting for transfers between devices, local(): got = lax.ppermute(send, 'band', [(0, 1), (1, 0)])  5.41 us
    pallas_call x2, Pallas kernels, place(): pl.pallas_call(lambda *refs: place_kernel(blocks, groups, kinds, *refs),...  3.86 us
    ppermute x1, starting transfers between devices, local(): got = lax.ppermute(send, 'band', [(0, 1), (1, 0)])  3.65 us
  transfers between devices with their start and end apart: 24, of which 12 were waited for; matrix products, arithmetic and copies ran while one was open for 0% of the time, Pallas kernels for 9%

profile of v2, /device:TPU:1, one launch (start us, length us, event | category | flops | bytes accessed | tf_op | source)
XLA Modules:
  0.0 98.3 jit_solution(4265360493921697315)
XLA Ops:
  0.0 7.4 %whiten.1 = (bf16[960,128]{1,0:T(8,128)(2,1)}, bf16[960,128]{1,0:T(8,128)(2,1)}) custom-call(s32[2]{0:T(128)} %start.1, s32[2]{0:T(128)} %width_ref.1, bf16[960,4096]{1,0:T(8,128)(2,1)} %bitcast.4), custom_call_target="tpu_custom_call" | custom-call | tf_op jit(solution)/shard_map/whiten/pallas_call | solution.py:93
  7.4 3.7 %collective-permute-start = (bf16[960,128]{1,0:T(8,128)(2,1)}, bf16[960,128]{1,0:T(8,128)(2,1)S(1)}, u32[]{:S(2)}, u32[]{:S(2)}) collective-permute-start(bf16[960,128]{1,0:T(8,128)(2,1)} %get-tuple-element.39), channel_id=1, source_target_pairs={{0,64},{64,0},{1,65},{65,1},{2,66},{66,2},{3,67},{67,3},{4,68},{68... | collective-permute-start | bytes 737288 | tf_op jit(solution)/shard_map/ppermute | solution.py:285
  11.1 5.4 %collective-permute-done.got_ref = bf16[960,128]{1,0:T(8,128)(2,1)S(1)} collective-permute-done((bf16[960,128]{1,0:T(8,128)(2,1)}, bf16[960,128]{1,0:T(8,128)(2,1)S(1)}, u32[]{:S(2)}, u32[]{:S(2)}) %collective-permute-start) | collective-permute-done | bytes 245792 | tf_op jit(solution)/shard_map/ppermute | solution.py:285
  16.5 0.9 copy-done
  17.7 1.7 %collective-permute-start.1 = (bf16[160,1536]{1,0:T(8,128)(2,1)S(1)}, bf16[160,1536]{1,0:T(8,128)(2,1)S(1)}, u32[]{:S(2)}, u32[]{:S(2)}) collective-permute-start(bf16[160,1536]{1,0:T(8,128)(2,1)S(1)} %normalize.1.refs_0_), channel_id=1, source_target_pairs={{0,2},{1,3},{2,0},{3,1},{4,6},{5,7},{6,4},{7,5},{8,10},{9,11},{10,... | collective-permute-start | bytes 1474568 | tf_op jit(solution)/shard_map/ppermute | solution.py:290
  19.3 2.9 %collective-permute-start.5 = (bf16[160,1536]{1,0:T(8,128)(2,1)S(1)}, bf16[160,1536]{1,0:T(8,128)(2,1)S(1)}, u32[]{:S(2)}, u32[]{:S(2)}) collective-permute-start(bf16[160,1536]{1,0:T(8,128)(2,1)S(1)} %normalize.1.refs_0_), channel_id=1, source_target_pairs={{32,0},{9,1},{34,2},{11,3},{36,4},{13,5},{38,6},{15,7},{40,8},{1,9... | collective-permute-start | bytes 1474568 | tf_op jit(solution)/shard_map/ppermute | solution.py:290
  22.6 2.3 %collective-permute-start.3 = (bf16[160,1536]{1,0:T(8,128)(2,1)S(1)}, bf16[160,1536]{1,0:T(8,128)(2,1)S(1)}, u32[]{:S(2)}, u32[]{:S(2)}) collective-permute-start(bf16[160,1536]{1,0:T(8,128)(2,1)S(1)} %normalize.1.refs_0_), channel_id=1, source_target_pairs={{16,0},{5,1},{18,2},{7,3},{20,4},{9,5},{22,6},{11,7},{24,8},{13,9}... | collective-permute-start | bytes 1474568 | tf_op jit(solution)/shard_map/ppermute | solution.py:290
  24.9 4.1 %collective-permute-done.1.refs_1_ = bf16[160,1536]{1,0:T(8,128)(2,1)S(1)} collective-permute-done((bf16[160,1536]{1,0:T(8,128)(2,1)S(1)}, bf16[160,1536]{1,0:T(8,128)(2,1)S(1)}, u32[]{:S(2)}, u32[]{:S(2)}) %collective-permute-start.1) | collective-permute-done | bytes 491552 | tf_op jit(solution)/shard_map/ppermute | solution.py:290
  29.1 2.6 %collective-permute-start.2 = (bf16[320,1536]{1,0:T(8,128)(2,1)S(1)}, bf16[320,1536]{1,0:T(8,128)(2,1)S(1)}, u32[]{:S(2)}, u32[]{:S(2)}) collective-permute-start(bf16[320,1536]{1,0:T(8,128)(2,1)S(1)} %stack.4.refs_0_), channel_id=1, source_target_pairs={{0,1},{1,0},{2,3},{3,2},{4,5},{5,4},{6,7},{7,6},{8,9},{9,8},{10,11... | collective-permute-start | bytes 2949128 | tf_op jit(solution)/shard_map/ppermute | solution.py:290
  31.7 2.4 %collective-permute-done.4.refs_0_ = bf16[160,1536]{1,0:T(8,128)(2,1)S(1)} collective-permute-done((bf16[160,1536]{1,0:T(8,128)(2,1)S(1)}, bf16[160,1536]{1,0:T(8,128)(2,1)S(1)}, u32[]{:S(2)}, u32[]{:S(2)}) %collective-permute-start.4) | collective-permute-done | bytes 491552 | tf_op jit(solution)/shard_map/ppermute | solution.py:290
  34.6 1.7 %collective-permute-start.7 = (bf16[320,1536]{1,0:T(8,128)(2,1)S(1)}, bf16[320,1536]{1,0:T(8,128)(2,1)S(1)}, u32[]{:S(2)}, u32[]{:S(2)}) collective-permute-start(bf16[320,1536]{1,0:T(8,128)(2,1)S(1)} %stack.7.second), channel_id=1, source_target_pairs={{12,0},{49,1},{14,2},{51,3},{0,4},{53,5},{2,6},{55,7},{4,8},{57,9}... | collective-permute-start | bytes 2949128 | tf_op jit(solution)/shard_map/ppermute | solution.py:290
  36.3 2.2 %collective-permute-start.6 = (bf16[320,1536]{1,0:T(8,128)(2,1)S(1)}, bf16[320,1536]{1,0:T(8,128)(2,1)S(1)}, u32[]{:S(2)}, u32[]{:S(2)}) collective-permute-start(bf16[320,1536]{1,0:T(8,128)(2,1)S(1)} %stack.6.first), channel_id=1, source_target_pairs={{4,0},{17,1},{6,2},{19,3},{8,4},{21,5},{10,6},{23,7},{12,8},{25,9}... | collective-permute-start | bytes 2949128 | tf_op jit(solution)/shard_map/ppermute | solution.py:290
  38.5 1.4 %collective-permute-start.8 = (bf16[320,1536]{1,0:T(8,128)(2,1)S(1)}, bf16[320,1536]{1,0:T(8,128)(2,1)S(1)}, u32[]{:S(2)}, u32[]{:S(2)}) collective-permute-start(bf16[320,1536]{1,0:T(8,128)(2,1)S(1)} %stack.7.second), channel_id=1, source_target_pairs={{4,0},{17,1},{6,2},{19,3},{8,4},{21,5},{10,6},{23,7},{12,8},{25,9}... | collective-permute-start | bytes 2949128 | tf_op jit(solution)/shard_map/ppermute | solution.py:290
  40.1 1.7 %cross.4 = (f32[160,640]{1,0:T(8,128)S(1)}, bf16[160,640]{1,0:T(8,128)(2,1)S(1)}, bf16[160,1280]{1,0:T(8,128)(2,1)S(1)}) custom-call(bf16[640,1536]{1,0:T(8,128)(2,1)S(1)} %stack.5.rows, bf16[320,1536]{1,0:T(8,128)(2,1)S(1)} %stack.6.first, bf16[320,1536]{1,0:T(8,128)(2,1)S(1)} %stack.7.second), custom_call_target="tpu_custom_call" | custom-call | flops 1258291200 | bytes 12582912 | tf_op jit(solution)/shard_map/cross/pallas_call | solution.py:176
  42.2 8.0 %collective-permute-done.7.second = bf16[320,1536]{1,0:T(8,128)(2,1)S(1)} collective-permute-done((bf16[320,1536]{1,0:T(8,128)(2,1)S(1)}, bf16[320,1536]{1,0:T(8,128)(2,1)S(1)}, u32[]{:S(2)}, u32[]{:S(2)}) %collective-permute-start.7) | collective-permute-done | bytes 983072 | tf_op jit(solution)/shard_map/ppermute | solution.py:290
  50.2 1.7 %cross.5 = (f32[160,640]{1,0:T(8,128)S(1)}, bf16[160,640]{1,0:T(8,128)(2,1)S(1)}, bf16[160,1280]{1,0:T(8,128)(2,1)S(1)}) custom-call(bf16[640,1536]{1,0:T(8,128)(2,1)S(1)} %stack.5.rows, bf16[320,1536]{1,0:T(8,128)(2,1)S(1)} %collective-permute-done.6.first, bf16[320,1536]{1,0:T(8,128)(2,1)S(1)} %collective-permute-done.7.second), custom_call_target="tpu_custom_call" | custom-call | flops 1258291200 | bytes 12582912 | tf_op jit(solution)/shard_map/cross/pallas_call | solution.py:176
  52.3 4.1 %collective-permute-start.11 = (bf16[160,640]{1,0:T(8,128)(2,1)S(1)}, bf16[160,640]{1,0:T(8,128)(2,1)S(1)}, u32[]{:S(2)}, u32[]{:S(2)}) collective-permute-start(bf16[160,640]{1,0:T(8,128)(2,1)S(1)} %get-tuple-element.46), channel_id=1, source_target_pairs={{0,1},{1,0},{2,3},{3,2},{4,5},{5,4},{6,7},{7,6},{8,9},{9,8},{10,11... | collective-permute-start | bytes 614408 | tf_op jit(solution)/shard_map/ppermute | solution.py:290
  56.4 3.9 %collective-permute-done.8.first = bf16[320,1536]{1,0:T(8,128)(2,1)S(1)} collective-permute-done((bf16[320,1536]{1,0:T(8,128)(2,1)S(1)}, bf16[320,1536]{1,0:T(8,128)(2,1)S(1)}, u32[]{:S(2)}, u32[]{:S(2)}) %collective-permute-start.8) | collective-permute-done | bytes 983072 | tf_op jit(solution)/shard_map/ppermute | solution.py:290
  60.3 0.5 collective-permute-done.9.second
  60.8 2.8 %collective-permute-start.13 = (bf16[320,1536]{1,0:T(8,128)(2,1)S(1)}, bf16[320,1536]{1,0:T(8,128)(2,1)S(1)}, u32[]{:S(2)}, u32[]{:S(2)}) collective-permute-start(bf16[320,1536]{1,0:T(8,128)(2,1)S(1)} %collective-permute-done.6.first), channel_id=1, source_target_pairs={{4,0},{17,1},{6,2},{19,3},{8,4},{21,5},{10,6},{23,7},{12,8},{25,9}... | collective-permute-start | bytes 2949128 | tf_op jit(solution)/shard_map/ppermute | solution.py:290
  63.6 1.7 %cross.6 = (f32[160,640]{1,0:T(8,128)S(1)}, bf16[160,640]{1,0:T(8,128)(2,1)S(1)}, bf16[160,1280]{1,0:T(8,128)(2,1)S(1)}) custom-call(bf16[640,1536]{1,0:T(8,128)(2,1)S(1)} %stack.5.rows, bf16[320,1536]{1,0:T(8,128)(2,1)S(1)} %collective-permute-done.8.first, bf16[320,1536]{1,0:T(8,128)(2,1)S(1)} %collective-permute-done.9.second), custom_call_target="tpu_custom_call" | custom-call | flops 1258291200 | bytes 12582912 | tf_op jit(solution)/shard_map/cross/pallas_call | solution.py:176
  65.3 4.2 %collective-permute-start.16 = (bf16[160,640]{1,0:T(8,128)(2,1)S(1)}, bf16[160,640]{1,0:T(8,128)(2,1)S(1)}, u32[]{:S(2)}, u32[]{:S(2)}) collective-permute-start(bf16[160,640]{1,0:T(8,128)(2,1)S(1)} %get-tuple-element.55), channel_id=1, source_target_pairs={{0,1},{1,0},{2,3},{3,2},{4,5},{5,4},{6,7},{7,6},{8,9},{9,8},{10,11... | collective-permute-start | bytes 614408 | tf_op jit(solution)/shard_map/ppermute | solution.py:290
  71.0 1.1 %collective-permute-done.18.refs_4_.refs_5_ = bf16[160,640]{1,0:T(8,128)(2,1)S(1)} collective-permute-done((bf16[160,640]{1,0:T(8,128)(2,1)S(1)}, bf16[160,640]{1,0:T(8,128)(2,1)S(1)}, u32[]{:S(2)}, u32[]{:S(2)}) %collective-permute-start.18) | collective-permute-done | bytes 204832 | tf_op jit(solution)/shard_map/ppermute | solution.py:290
  72.1 8.5 %collective-permute-done.15.refs_8_.refs_10_ = bf16[160,1280]{1,0:T(8,128)(2,1)S(1)} collective-permute-done((bf16[160,1280]{1,0:T(8,128)(2,1)S(1)}, bf16[160,1280]{1,0:T(8,128)(2,1)S(1)}, u32[]{:S(2)}, u32[]{:S(2)}) %collective-permute-start.15) | collective-permute-done | bytes 409632 | tf_op jit(solution)/shard_map/ppermute | solution.py:290
  80.6 2.3 %collective-permute-start.21 = (bf16[160,1280]{1,0:T(8,128)(2,1)S(1)}, bf16[160,1280]{1,0:T(8,128)(2,1)S(1)}, u32[]{:S(2)}, u32[]{:S(2)}) collective-permute-start(bf16[160,1280]{1,0:T(8,128)(2,1)S(1)} %collective-permute-done.12.refs_7_.refs_9_), channel_id=1, source_target_pairs={{0,1},{1,0},{2,3},{3,2},{4,5},{5,4},{6,7},{7,6},{8,9},{9,8},{10,11... | collective-permute-start | bytes 1228808 | tf_op jit(solution)/shard_map/ppermute | solution.py:290
  82.9 1.7 %cross.7 = (f32[160,640]{1,0:T(8,128)S(1)}, bf16[160,640]{1,0:T(8,128)(2,1)S(1)}, bf16[160,640]{1,0:T(8,128)(2,1)S(1)}, bf16[160,640]{1,0:T(8,128)(2,1)S(1)}) custom-call(bf16[640,1536]{1,0:T(8,128)(2,1)S(1)} %stack.5.rows, bf16[320,1536]{1,0:T(8,128)(2,1)S(1)} %collective-permute-done.13.first, bf16[320,1536]{1,0:T(8,128)(2,1)S(1)} %collective-permute-done.14.second), custom_call_target="tpu_custom_call" | custom-call | flops 1258291200 | bytes 12582912 | tf_op jit(solution)/shard_map/cross/pallas_call | solution.py:176
  84.6 0.6 collective-permute-start.19
  85.4 1.4 %collective-permute-start.23 = (bf16[160,640]{1,0:T(8,128)(2,1)S(1)}, bf16[160,640]{1,0:T(8,128)(2,1)S(1)}, u32[]{:S(2)}, u32[]{:S(2)}) collective-permute-start(bf16[160,640]{1,0:T(8,128)(2,1)S(1)} %get-tuple-element.70), channel_id=1, source_target_pairs={{0,3},{1,2},{2,1},{3,0},{4,7},{5,6},{6,5},{7,4},{8,11},{9,10},{10,... | collective-permute-start | bytes 614408 | tf_op jit(solution)/shard_map/ppermute | solution.py:290
  86.9 2.1 %place.2.refs_16_ = f32[160,10240]{1,0:T(8,128)} custom-call(f32[160,640]{1,0:T(8,128)S(1)} %get-tuple-element.43.refs_0_, f32[160,640]{1,0:T(8,128)S(1)} %get-tuple-element.44.refs_1_, f32[160,640]{1,0:T(8,128)S(1)} %get-tuple-element.51.refs_2_, bf16[160,640]{1,0:T(8,128)(2,1)S(1)} %collective-permute-done.11.refs_3_.refs_4_, ...), custom_call_target="tpu_custom_call" | custom-call | tf_op jit(solution)/shard_map/place/pallas_call | solution.py:237
  89.0 2.8 %collective-permute-done.20.refs_11_ = bf16[160,640]{1,0:T(8,128)(2,1)S(1)} collective-permute-done((bf16[160,640]{1,0:T(8,128)(2,1)S(1)}, bf16[160,640]{1,0:T(8,128)(2,1)S(1)}, u32[]{:S(2)}, u32[]{:S(2)}) %collective-permute-start.20) | collective-permute-done | bytes 204832 | tf_op jit(solution)/shard_map/ppermute | solution.py:290
  91.8 4.6 %collective-permute-done.23.refs_15_ = bf16[160,640]{1,0:T(8,128)(2,1)S(1)} collective-permute-done((bf16[160,640]{1,0:T(8,128)(2,1)S(1)}, bf16[160,640]{1,0:T(8,128)(2,1)S(1)}, u32[]{:S(2)}, u32[]{:S(2)}) %collective-permute-start.23) | collective-permute-done | bytes 204832 | tf_op jit(solution)/shard_map/ppermute | solution.py:290
  96.4 1.8 %place.3 = f32[160,10240]{1,0:T(8,128)} custom-call(f32[160,640]{1,0:T(8,128)S(1)} %get-tuple-element.43.refs_0_, f32[160,640]{1,0:T(8,128)S(1)} %get-tuple-element.44.refs_1_, f32[160,640]{1,0:T(8,128)S(1)} %get-tuple-element.51.refs_2_, f32[160,640]{1,0:T(8,128)S(1)} %get-tuple-element.61.refs_3_, ...), custom_call_target="tpu_custom_call", output_to_operand_aliasing={{}: (16, {})} | custom-call | tf_op jit(solution)/shard_map/place/pallas_call | solution.py:237
  (30 shorter events, 3.9 us)
Async XLA Ops:
  7.4 9.1 %collective-permute-start = (bf16[960,128]{1,0:T(8,128)(2,1)}, bf16[960,128]{1,0:T(8,128)(2,1)S(1)}, u32[]{:S(2)}, u32[]{:S(2)}) collective-permute-start(bf16[960,128]{1,0:T(8,128)(2,1)} %get-tuple-element.39), channel_id=1, source_target_pairs={{0,64},{64,0},{1,65},{65,1},{2,66},{66,2},{3,67},{67,3},{4,68},{68... | collective-permute-start | bytes 737288 | tf_op jit(solution)/shard_map/ppermute | solution.py:285
  16.5 0.9 copy-start
  17.7 11.3 %collective-permute-start.1 = (bf16[160,1536]{1,0:T(8,128)(2,1)S(1)}, bf16[160,1536]{1,0:T(8,128)(2,1)S(1)}, u32[]{:S(2)}, u32[]{:S(2)}) collective-permute-start(bf16[160,1536]{1,0:T(8,128)(2,1)S(1)} %normalize.1.refs_0_), channel_id=1, source_target_pairs={{0,2},{1,3},{2,0},{3,1},{4,6},{5,7},{6,4},{7,5},{8,10},{9,11},{10,... | collective-permute-start | bytes 1474568 | tf_op jit(solution)/shard_map/ppermute | solution.py:290
  19.3 12.3 %collective-permute-start.5 = (bf16[160,1536]{1,0:T(8,128)(2,1)S(1)}, bf16[160,1536]{1,0:T(8,128)(2,1)S(1)}, u32[]{:S(2)}, u32[]{:S(2)}) collective-permute-start(bf16[160,1536]{1,0:T(8,128)(2,1)S(1)} %normalize.1.refs_0_), channel_id=1, source_target_pairs={{32,0},{9,1},{34,2},{11,3},{36,4},{13,5},{38,6},{15,7},{40,8},{1,9... | collective-permute-start | bytes 1474568 | tf_op jit(solution)/shard_map/ppermute | solution.py:290
  22.2 11.8 %collective-permute-start.4 = (bf16[160,1536]{1,0:T(8,128)(2,1)S(1)}, bf16[160,1536]{1,0:T(8,128)(2,1)S(1)}, u32[]{:S(2)}, u32[]{:S(2)}) collective-permute-start(bf16[160,1536]{1,0:T(8,128)(2,1)S(1)} %normalize.1.refs_0_), channel_id=1, source_target_pairs={{48,0},{13,1},{50,2},{15,3},{52,4},{1,5},{54,6},{3,7},{56,8},{5,9}... | collective-permute-start | bytes 1474568 | tf_op jit(solution)/shard_map/ppermute | solution.py:290
  22.6 11.8 %collective-permute-start.3 = (bf16[160,1536]{1,0:T(8,128)(2,1)S(1)}, bf16[160,1536]{1,0:T(8,128)(2,1)S(1)}, u32[]{:S(2)}, u32[]{:S(2)}) collective-permute-start(bf16[160,1536]{1,0:T(8,128)(2,1)S(1)} %normalize.1.refs_0_), channel_id=1, source_target_pairs={{16,0},{5,1},{18,2},{7,3},{20,4},{9,5},{22,6},{11,7},{24,8},{13,9}... | collective-permute-start | bytes 1474568 | tf_op jit(solution)/shard_map/ppermute | solution.py:290
  29.1 10.9 %collective-permute-start.2 = (bf16[320,1536]{1,0:T(8,128)(2,1)S(1)}, bf16[320,1536]{1,0:T(8,128)(2,1)S(1)}, u32[]{:S(2)}, u32[]{:S(2)}) collective-permute-start(bf16[320,1536]{1,0:T(8,128)(2,1)S(1)} %stack.4.refs_0_), channel_id=1, source_target_pairs={{0,1},{1,0},{2,3},{3,2},{4,5},{5,4},{6,7},{7,6},{8,9},{9,8},{10,11... | collective-permute-start | bytes 2949128 | tf_op jit(solution)/shard_map/ppermute | solution.py:290
  34.6 15.6 %collective-permute-start.7 = (bf16[320,1536]{1,0:T(8,128)(2,1)S(1)}, bf16[320,1536]{1,0:T(8,128)(2,1)S(1)}, u32[]{:S(2)}, u32[]{:S(2)}) collective-permute-start(bf16[320,1536]{1,0:T(8,128)(2,1)S(1)} %stack.7.second), channel_id=1, source_target_pairs={{12,0},{49,1},{14,2},{51,3},{0,4},{53,5},{2,6},{55,7},{4,8},{57,9}... | collective-permute-start | bytes 2949128 | tf_op jit(solution)/shard_map/ppermute | solution.py:290
  36.3 13.9 %collective-permute-start.6 = (bf16[320,1536]{1,0:T(8,128)(2,1)S(1)}, bf16[320,1536]{1,0:T(8,128)(2,1)S(1)}, u32[]{:S(2)}, u32[]{:S(2)}) collective-permute-start(bf16[320,1536]{1,0:T(8,128)(2,1)S(1)} %stack.6.first), channel_id=1, source_target_pairs={{4,0},{17,1},{6,2},{19,3},{8,4},{21,5},{10,6},{23,7},{12,8},{25,9}... | collective-permute-start | bytes 2949128 | tf_op jit(solution)/shard_map/ppermute | solution.py:290
  38.5 21.8 %collective-permute-start.8 = (bf16[320,1536]{1,0:T(8,128)(2,1)S(1)}, bf16[320,1536]{1,0:T(8,128)(2,1)S(1)}, u32[]{:S(2)}, u32[]{:S(2)}) collective-permute-start(bf16[320,1536]{1,0:T(8,128)(2,1)S(1)} %stack.7.second), channel_id=1, source_target_pairs={{4,0},{17,1},{6,2},{19,3},{8,4},{21,5},{10,6},{23,7},{12,8},{25,9}... | collective-permute-start | bytes 2949128 | tf_op jit(solution)/shard_map/ppermute | solution.py:290
  39.9 20.8 %collective-permute-start.9 = (bf16[320,1536]{1,0:T(8,128)(2,1)S(1)}, bf16[320,1536]{1,0:T(8,128)(2,1)S(1)}, u32[]{:S(2)}, u32[]{:S(2)}) collective-permute-start(bf16[320,1536]{1,0:T(8,128)(2,1)S(1)} %stack.6.first), channel_id=1, source_target_pairs={{12,0},{49,1},{14,2},{51,3},{0,4},{53,5},{2,6},{55,7},{4,8},{57,9}... | collective-permute-start | bytes 2949128 | tf_op jit(solution)/shard_map/ppermute | solution.py:290
  41.8 18.9 %collective-permute-start.10 = (bf16[160,1280]{1,0:T(8,128)(2,1)S(1)}, bf16[160,1280]{1,0:T(8,128)(2,1)S(1)}, u32[]{:S(2)}, u32[]{:S(2)}) collective-permute-start(bf16[160,1280]{1,0:T(8,128)(2,1)S(1)} %get-tuple-element.45), channel_id=1, source_target_pairs={{0,2},{1,3},{2,0},{3,1},{4,6},{5,7},{6,4},{7,5},{8,10},{9,11},{10,... | collective-permute-start | bytes 1228808 | tf_op jit(solution)/shard_map/ppermute | solution.py:290
  51.9 8.8 %collective-permute-start.12 = (bf16[160,1280]{1,0:T(8,128)(2,1)S(1)}, bf16[160,1280]{1,0:T(8,128)(2,1)S(1)}, u32[]{:S(2)}, u32[]{:S(2)}) collective-permute-start(bf16[160,1280]{1,0:T(8,128)(2,1)S(1)} %get-tuple-element.47), channel_id=1, source_target_pairs={{0,2},{1,3},{2,0},{3,1},{4,6},{5,7},{6,4},{7,5},{8,10},{9,11},{10,... | collective-permute-start | bytes 1228808 | tf_op jit(solution)/shard_map/ppermute | solution.py:290
  52.3 8.5 %collective-permute-start.11 = (bf16[160,640]{1,0:T(8,128)(2,1)S(1)}, bf16[160,640]{1,0:T(8,128)(2,1)S(1)}, u32[]{:S(2)}, u32[]{:S(2)}) collective-permute-start(bf16[160,640]{1,0:T(8,128)(2,1)S(1)} %get-tuple-element.46), channel_id=1, source_target_pairs={{0,1},{1,0},{2,3},{3,2},{4,5},{5,4},{6,7},{7,6},{8,9},{9,8},{10,11... | collective-permute-start | bytes 614408 | tf_op jit(solution)/shard_map/ppermute | solution.py:290
  60.8 19.8 %collective-permute-start.13 = (bf16[320,1536]{1,0:T(8,128)(2,1)S(1)}, bf16[320,1536]{1,0:T(8,128)(2,1)S(1)}, u32[]{:S(2)}, u32[]{:S(2)}) collective-permute-start(bf16[320,1536]{1,0:T(8,128)(2,1)S(1)} %collective-permute-done.6.first), channel_id=1, source_target_pairs={{4,0},{17,1},{6,2},{19,3},{8,4},{21,5},{10,6},{23,7},{12,8},{25,9}... | collective-permute-start | bytes 2949128 | tf_op jit(solution)/shard_map/ppermute | solution.py:290
  63.6 17.0 %collective-permute-start.14 = (bf16[320,1536]{1,0:T(8,128)(2,1)S(1)}, bf16[320,1536]{1,0:T(8,128)(2,1)S(1)}, u32[]{:S(2)}, u32[]{:S(2)}) collective-permute-start(bf16[320,1536]{1,0:T(8,128)(2,1)S(1)} %collective-permute-done.7.second), channel_id=1, source_target_pairs={{12,0},{49,1},{14,2},{51,3},{0,4},{53,5},{2,6},{55,7},{4,8},{57,9}... | collective-permute-start | bytes 2949128 | tf_op jit(solution)/shard_map/ppermute | solution.py:290
  65.3 5.3 %collective-permute-start.16 = (bf16[160,640]{1,0:T(8,128)(2,1)S(1)}, bf16[160,640]{1,0:T(8,128)(2,1)S(1)}, u32[]{:S(2)}, u32[]{:S(2)}) collective-permute-start(bf16[160,640]{1,0:T(8,128)(2,1)S(1)} %get-tuple-element.55), channel_id=1, source_target_pairs={{0,1},{1,0},{2,3},{3,2},{4,5},{5,4},{6,7},{7,6},{8,9},{9,8},{10,11... | collective-permute-start | bytes 614408 | tf_op jit(solution)/shard_map/ppermute | solution.py:290
  69.5 11.0 %collective-permute-start.15 = (bf16[160,1280]{1,0:T(8,128)(2,1)S(1)}, bf16[160,1280]{1,0:T(8,128)(2,1)S(1)}, u32[]{:S(2)}, u32[]{:S(2)}) collective-permute-start(bf16[160,1280]{1,0:T(8,128)(2,1)S(1)} %get-tuple-element.54), channel_id=1, source_target_pairs={{0,2},{1,3},{2,0},{3,1},{4,6},{5,7},{6,4},{7,5},{8,10},{9,11},{10,... | collective-permute-start | bytes 1228808 | tf_op jit(solution)/shard_map/ppermute | solution.py:290
  69.8 10.7 %collective-permute-start.17 = (bf16[160,1280]{1,0:T(8,128)(2,1)S(1)}, bf16[160,1280]{1,0:T(8,128)(2,1)S(1)}, u32[]{:S(2)}, u32[]{:S(2)}) collective-permute-start(bf16[160,1280]{1,0:T(8,128)(2,1)S(1)} %collective-permute-done.10.refs_6_.refs_8_), channel_id=1, source_target_pairs={{0,1},{1,0},{2,3},{3,2},{4,5},{5,4},{6,7},{7,6},{8,9},{9,8},{10,11... | collective-permute-start | bytes 1228808 | tf_op jit(solution)/shard_map/ppermute | solution.py:290
  70.6 1.5 %collective-permute-start.18 = (bf16[160,640]{1,0:T(8,128)(2,1)S(1)}, bf16[160,640]{1,0:T(8,128)(2,1)S(1)}, u32[]{:S(2)}, u32[]{:S(2)}) collective-permute-start(bf16[160,640]{1,0:T(8,128)(2,1)S(1)} %get-tuple-element.57), channel_id=1, source_target_pairs={{0,1},{1,0},{2,3},{3,2},{4,5},{5,4},{6,7},{7,6},{8,9},{9,8},{10,11... | collective-permute-start | bytes 614408 | tf_op jit(solution)/shard_map/ppermute | solution.py:290
  80.6 6.3 %collective-permute-start.21 = (bf16[160,1280]{1,0:T(8,128)(2,1)S(1)}, bf16[160,1280]{1,0:T(8,128)(2,1)S(1)}, u32[]{:S(2)}, u32[]{:S(2)}) collective-permute-start(bf16[160,1280]{1,0:T(8,128)(2,1)S(1)} %collective-permute-done.12.refs_7_.refs_9_), channel_id=1, source_target_pairs={{0,1},{1,0},{2,3},{3,2},{4,5},{5,4},{6,7},{7,6},{8,9},{9,8},{10,11... | collective-permute-start | bytes 1228808 | tf_op jit(solution)/shard_map/ppermute | solution.py:290
  82.9 4.0 %collective-permute-start.22 = (bf16[160,1280]{1,0:T(8,128)(2,1)S(1)}, bf16[160,1280]{1,0:T(8,128)(2,1)S(1)}, u32[]{:S(2)}, u32[]{:S(2)}) collective-permute-start(bf16[160,1280]{1,0:T(8,128)(2,1)S(1)} %collective-permute-done.15.refs_8_.refs_10_), channel_id=1, source_target_pairs={{0,1},{1,0},{2,3},{3,2},{4,5},{5,4},{6,7},{7,6},{8,9},{9,8},{10,11... | collective-permute-start | bytes 1228808 | tf_op jit(solution)/shard_map/ppermute | solution.py:290
  84.6 4.4 %collective-permute-start.19 = (bf16[160,640]{1,0:T(8,128)(2,1)S(1)}, bf16[160,640]{1,0:T(8,128)(2,1)S(1)}, u32[]{:S(2)}, u32[]{:S(2)}) collective-permute-start(bf16[160,640]{1,0:T(8,128)(2,1)S(1)} %get-tuple-element.65), channel_id=1, source_target_pairs={{0,1},{1,0},{2,3},{3,2},{4,5},{5,4},{6,7},{7,6},{8,9},{9,8},{10,11... | collective-permute-start | bytes 614408 | tf_op jit(solution)/shard_map/ppermute | solution.py:290
  85.2 6.6 %collective-permute-start.20 = (bf16[160,640]{1,0:T(8,128)(2,1)S(1)}, bf16[160,640]{1,0:T(8,128)(2,1)S(1)}, u32[]{:S(2)}, u32[]{:S(2)}) collective-permute-start(bf16[160,640]{1,0:T(8,128)(2,1)S(1)} %get-tuple-element.68), channel_id=1, source_target_pairs={{0,2},{1,3},{2,0},{3,1},{4,6},{5,7},{6,4},{7,5},{8,10},{9,11},{10,... | collective-permute-start | bytes 614408 | tf_op jit(solution)/shard_map/ppermute | solution.py:290
  85.4 10.9 %collective-permute-start.23 = (bf16[160,640]{1,0:T(8,128)(2,1)S(1)}, bf16[160,640]{1,0:T(8,128)(2,1)S(1)}, u32[]{:S(2)}, u32[]{:S(2)}) collective-permute-start(bf16[160,640]{1,0:T(8,128)(2,1)S(1)} %get-tuple-element.70), channel_id=1, source_target_pairs={{0,3},{1,2},{2,1},{3,0},{4,7},{5,6},{6,5},{7,4},{8,11},{9,10},{10,... | collective-permute-start | bytes 614408 | tf_op jit(solution)/shard_map/ppermute | solution.py:290

commit v3 on v2

--- a/solution.py
+++ b/solution.py
@@ -104,7 +104,7 @@
             pltpu.VMEM((total, 256), jnp.float32),
             pltpu.SemaphoreType.DMA((WINS,)),
         ],
-        compiler_params=pltpu.CompilerParams(vmem_limit_bytes=57 << 20),
+        compiler_params=pltpu.CompilerParams(vmem_limit_bytes=53 << 20),
         name="whiten",
     )(band_start, half_width, flat)
 
@@ -291,28 +291,30 @@
 
     ahead, behind = move(own, from_first(1)), move(own, from_first(-1))
     far, over = move(own, from_first(2)), move(own, flip(2))
-    ahead, behind, far = hold((ahead, behind, far))
+    ahead, behind, far, over = hold((ahead, behind, far, over))
+    mates = stack(own, over)
+    across = move(mates, flip(1))
     pair0, pair1 = stack(own, ahead), stack(behind, far)
     up0, down1 = move(pair0, from_second(1)), move(pair1, from_second(-1))
     up1, down0 = move(pair1, from_second(1)), move(pair0, from_second(-1))
-    mates = stack(own, over)
-    rows = stack(mates, move(mates, flip(1)))
+    rows = stack(mates, across)
     mine0, c0, x0 = cross(rows, pair0, pair1, True)
     x0 = move(x0, flip(2))
     c0 = move(c0, flip(1))
     mine1, c1, x1 = cross(rows, up0, down1, True)
+    x1, x0, c0, up0, down1 = hold((x1, x0, c0, up0, down1))
     x1 = move(x1, flip(2))
-    up0, down1, up1, down0, x0, c0, x1, c1 = hold((up0, down1, up1, down0, x0, c0, x1, c1))
     up2, down2 = move(up0, from_second(1)), move(down1, from_second(-1))
-    mine2, c2, x2 = cross(rows, up1, down0, True)
-    x2 = move(x2, flip(2))
     xc0 = move(x0, flip(1))
     c1 = move(c1, flip(1))
+    mine2, c2, x2 = cross(rows, up1, down0, True)
+    x2, x1, c1, xc0 = hold((x2, x1, c1, xc0))
+    x2 = move(x2, flip(2))
+    xc1 = move(x1, flip(1))
     c2 = move(c2, flip(1))
-    up2, down2, x2, c2, xc0, c1, x1 = hold((up2, down2, x2, c2, xc0, c1, x1))
     mine3, c3, x3, xc3 = cross(rows, up2, down2, False)
+    x3, xc3, x2, c2, xc1 = hold((x3, xc3, x2, c2, xc1))
     x3, xc3, c3 = move(x3, flip(2)), move(xc3, flip(3)), move(c3, flip(1))
-    xc1 = move(x1, flip(1))
     xc2 = move(x2, flip(1))
     early = [(du, dv) for du in NEAR for dv in NEAR if du != 2 and dv != 2]
     late = [(du, dv) for du in NEAR for dv in NEAR if du == 2 or dv == 2]

time: 98.5 us -> 92.5 us (0.939)
  starting transfers between devices: 36.3 us -> 33 us
  waiting for transfers between devices: 42.1 us -> 39.2 us
    ppermute x23, starting transfers between devices: 32.7 us -> 29.3 us  [move(): return lax.ppermute(value, 'chan', pairs)]
    ppermute x23, waiting for transfers between devices: 36.7 us -> 34 us  [move(): return lax.ppermute(value, 'chan', pairs)]
  transfers between devices with their start and end apart: 24 -> 24, of which waited for: 12 -> 11; matrix products, arithmetic and copies ran while one was open for 0% -> 0% of each run, Pallas kernels for 9% -> 10%
where the time goes in v3:
time: 92.5 us; the launch traced here: 91.6 us
  waiting for transfers between devices  39.2 us (42%)
  starting transfers between devices  33 us (36%)
  Pallas kernels  17.8 us (19%)
  local copies, waits for them, and re-layouts  1.31 us (1%)
    ppermute x23, waiting for transfers between devices, move(): return lax.ppermute(value, 'chan', pairs)  34 us
    ppermute x23, starting transfers between devices, move(): return lax.ppermute(value, 'chan', pairs)  29.3 us
    pallas_call x4, Pallas kernels, cross(): pl.pallas_call(cross_kernel, out_shape=[mine, narrow, wide] if merged els...  6.86 us
    pallas_call x1, Pallas kernels, whiten(): pl.pallas_call(whiten_kernel, in_specs=[pl.BlockSpec(memory_space=pltpu.S...  6.5 us
    ppermute x1, waiting for transfers between devices, local(): got = lax.ppermute(send, 'band', [(0, 1), (1, 0)])  5.2 us
    pallas_call x2, Pallas kernels, place(): pl.pallas_call(lambda *refs: place_kernel(blocks, groups, kinds, *refs),...  3.86 us
    ppermute x1, starting transfers between devices, local(): got = lax.ppermute(send, 'band', [(0, 1), (1, 0)])  3.65 us
  transfers between devices with their start and end apart: 24, of which 11 were waited for; matrix products, arithmetic and copies ran while one was open for 0% of the time, Pallas kernels for 10%

profile of v3, /device:TPU:1, one launch (start us, length us, event | category | flops | bytes accessed | tf_op | source)
XLA Modules:
  0.0 91.6 jit_solution(5768950623369996741)
XLA Ops:
  0.0 0.7 copy-done
  0.7 0.7 copy-done.1
  1.3 6.5 %whiten.1 = (bf16[960,128]{1,0:T(8,128)(2,1)S(1)}, bf16[960,128]{1,0:T(8,128)(2,1)S(1)}) custom-call(s32[2]{0:T(128)S(1)} %copy-done, s32[2]{0:T(128)S(1)} %copy-done.1, bf16[960,4096]{1,0:T(8,128)(2,1)} %bitcast.4), custom_call_target="tpu_custom_call" | custom-call | tf_op jit(solution)/shard_map/whiten/pallas_call | solution.py:93
  7.8 3.7 %collective-permute-start = (bf16[960,128]{1,0:T(8,128)(2,1)S(1)}, bf16[960,128]{1,0:T(8,128)(2,1)S(1)}, u32[]{:S(2)}, u32[]{:S(2)}) collective-permute-start(bf16[960,128]{1,0:T(8,128)(2,1)S(1)} %get-tuple-element.39), channel_id=1, source_target_pairs={{0,64},{64,0},{1,65},{65,1},{2,66},{66,2},{3,67},{67,3},{4,68},{68... | collective-permute-start | bytes 737288 | tf_op jit(solution)/shard_map/ppermute | solution.py:285
  11.5 5.2 %collective-permute-done.got_ref = bf16[960,128]{1,0:T(8,128)(2,1)S(1)} collective-permute-done((bf16[960,128]{1,0:T(8,128)(2,1)S(1)}, bf16[960,128]{1,0:T(8,128)(2,1)S(1)}, u32[]{:S(2)}, u32[]{:S(2)}) %collective-permute-start) | collective-permute-done | bytes 245792 | tf_op jit(solution)/shard_map/ppermute | solution.py:285
  16.9 1.7 %collective-permute-start.4 = (bf16[160,1536]{1,0:T(8,128)(2,1)S(1)}, bf16[160,1536]{1,0:T(8,128)(2,1)S(1)}, u32[]{:S(2)}, u32[]{:S(2)}) collective-permute-start(bf16[160,1536]{1,0:T(8,128)(2,1)S(1)} %normalize.1.refs_0_), channel_id=1, source_target_pairs={{0,2},{1,3},{2,0},{3,1},{4,6},{5,7},{6,4},{7,5},{8,10},{9,11},{10,... | collective-permute-start | bytes 1474568 | tf_op jit(solution)/shard_map/ppermute | solution.py:290
  18.6 2.9 %collective-permute-start.3 = (bf16[160,1536]{1,0:T(8,128)(2,1)S(1)}, bf16[160,1536]{1,0:T(8,128)(2,1)S(1)}, u32[]{:S(2)}, u32[]{:S(2)}) collective-permute-start(bf16[160,1536]{1,0:T(8,128)(2,1)S(1)} %normalize.1.refs_0_), channel_id=1, source_target_pairs={{32,0},{9,1},{34,2},{11,3},{36,4},{13,5},{38,6},{15,7},{40,8},{1,9... | collective-permute-start | bytes 1474568 | tf_op jit(solution)/shard_map/ppermute | solution.py:290
  21.9 2.3 %collective-permute-start.1 = (bf16[160,1536]{1,0:T(8,128)(2,1)S(1)}, bf16[160,1536]{1,0:T(8,128)(2,1)S(1)}, u32[]{:S(2)}, u32[]{:S(2)}) collective-permute-start(bf16[160,1536]{1,0:T(8,128)(2,1)S(1)} %normalize.1.refs_0_), channel_id=1, source_target_pairs={{16,0},{5,1},{18,2},{7,3},{20,4},{9,5},{22,6},{11,7},{24,8},{13,9}... | collective-permute-start | bytes 1474568 | tf_op jit(solution)/shard_map/ppermute | solution.py:290
  24.2 4.1 %collective-permute-done.4.refs_1_ = bf16[160,1536]{1,0:T(8,128)(2,1)S(1)} collective-permute-done((bf16[160,1536]{1,0:T(8,128)(2,1)S(1)}, bf16[160,1536]{1,0:T(8,128)(2,1)S(1)}, u32[]{:S(2)}, u32[]{:S(2)}) %collective-permute-start.4) | collective-permute-done | bytes 491552 | tf_op jit(solution)/shard_map/ppermute | solution.py:290
  28.3 5.1 %collective-permute-done.2.refs_0_ = bf16[160,1536]{1,0:T(8,128)(2,1)S(1)} collective-permute-done((bf16[160,1536]{1,0:T(8,128)(2,1)S(1)}, bf16[160,1536]{1,0:T(8,128)(2,1)S(1)}, u32[]{:S(2)}, u32[]{:S(2)}) %collective-permute-start.2) | collective-permute-done | bytes 491552 | tf_op jit(solution)/shard_map/ppermute | solution.py:290
  33.8 3.8 %collective-permute-start.5 = (bf16[320,1536]{1,0:T(8,128)(2,1)S(1)}, bf16[320,1536]{1,0:T(8,128)(2,1)S(1)}, u32[]{:S(2)}, u32[]{:S(2)}) collective-permute-start(bf16[320,1536]{1,0:T(8,128)(2,1)S(1)} %stack.4.refs_0_), channel_id=1, source_target_pairs={{0,1},{1,0},{2,3},{3,2},{4,5},{5,4},{6,7},{7,6},{8,9},{9,8},{10,11... | collective-permute-start | bytes 2949128 | tf_op jit(solution)/shard_map/ppermute | solution.py:290
  37.6 0.8 collective-permute-start.7
  38.5 2.0 %collective-permute-start.6 = (bf16[320,1536]{1,0:T(8,128)(2,1)S(1)}, bf16[320,1536]{1,0:T(8,128)(2,1)S(1)}, u32[]{:S(2)}, u32[]{:S(2)}) collective-permute-start(bf16[320,1536]{1,0:T(8,128)(2,1)S(1)} %stack.6.first), channel_id=1, source_target_pairs={{4,0},{17,1},{6,2},{19,3},{8,4},{21,5},{10,6},{23,7},{12,8},{25,9}... | collective-permute-start | bytes 2949128 | tf_op jit(solution)/shard_map/ppermute | solution.py:290
  40.5 1.1 %collective-permute-start.8 = (bf16[320,1536]{1,0:T(8,128)(2,1)S(1)}, bf16[320,1536]{1,0:T(8,128)(2,1)S(1)}, u32[]{:S(2)}, u32[]{:S(2)}) collective-permute-start(bf16[320,1536]{1,0:T(8,128)(2,1)S(1)} %stack.7.second), channel_id=1, source_target_pairs={{4,0},{17,1},{6,2},{19,3},{8,4},{21,5},{10,6},{23,7},{12,8},{25,9}... | collective-permute-start | bytes 2949128 | tf_op jit(solution)/shard_map/ppermute | solution.py:290
  42.1 1.7 %cross.4 = (f32[160,640]{1,0:T(8,128)S(1)}, bf16[160,640]{1,0:T(8,128)(2,1)S(1)}, bf16[160,1280]{1,0:T(8,128)(2,1)S(1)}) custom-call(bf16[640,1536]{1,0:T(8,128)(2,1)S(1)} %stack.5.rows, bf16[320,1536]{1,0:T(8,128)(2,1)S(1)} %stack.6.first, bf16[320,1536]{1,0:T(8,128)(2,1)S(1)} %stack.7.second), custom_call_target="tpu_custom_call" | custom-call | flops 1258291200 | bytes 12582912 | tf_op jit(solution)/shard_map/cross/pallas_call | solution.py:176
  44.2 8.0 %collective-permute-done.7.second = bf16[320,1536]{1,0:T(8,128)(2,1)S(1)} collective-permute-done((bf16[320,1536]{1,0:T(8,128)(2,1)S(1)}, bf16[320,1536]{1,0:T(8,128)(2,1)S(1)}, u32[]{:S(2)}, u32[]{:S(2)}) %collective-permute-start.7) | collective-permute-done | bytes 983072 | tf_op jit(solution)/shard_map/ppermute | solution.py:290
  52.2 0.9 collective-permute-start.11
  53.0 1.7 %cross.5 = (f32[160,640]{1,0:T(8,128)S(1)}, bf16[160,640]{1,0:T(8,128)(2,1)S(1)}, bf16[160,1280]{1,0:T(8,128)(2,1)S(1)}) custom-call(bf16[640,1536]{1,0:T(8,128)(2,1)S(1)} %stack.5.rows, bf16[320,1536]{1,0:T(8,128)(2,1)S(1)} %collective-permute-done.6.first, bf16[320,1536]{1,0:T(8,128)(2,1)S(1)} %collective-permute-done.7.second), custom_call_target="tpu_custom_call" | custom-call | flops 1258291200 | bytes 12582912 | tf_op jit(solution)/shard_map/cross/pallas_call | solution.py:176
  54.8 2.4 %collective-permute-start.12 = (bf16[320,1536]{1,0:T(8,128)(2,1)S(1)}, bf16[320,1536]{1,0:T(8,128)(2,1)S(1)}, u32[]{:S(2)}, u32[]{:S(2)}) collective-permute-start(bf16[320,1536]{1,0:T(8,128)(2,1)S(1)} %collective-permute-done.6.first), channel_id=1, source_target_pairs={{4,0},{17,1},{6,2},{19,3},{8,4},{21,5},{10,6},{23,7},{12,8},{25,9}... | collective-permute-start | bytes 2949128 | tf_op jit(solution)/shard_map/ppermute | solution.py:290
  57.5 4.9 %collective-permute-done.8.first = bf16[320,1536]{1,0:T(8,128)(2,1)S(1)} collective-permute-done((bf16[320,1536]{1,0:T(8,128)(2,1)S(1)}, bf16[320,1536]{1,0:T(8,128)(2,1)S(1)}, u32[]{:S(2)}, u32[]{:S(2)}) %collective-permute-start.8) | collective-permute-done | bytes 983072 | tf_op jit(solution)/shard_map/ppermute | solution.py:290
  62.4 1.7 %collective-permute-start.16 = (bf16[160,1280]{1,0:T(8,128)(2,1)S(1)}, bf16[160,1280]{1,0:T(8,128)(2,1)S(1)}, u32[]{:S(2)}, u32[]{:S(2)}) collective-permute-start(bf16[160,1280]{1,0:T(8,128)(2,1)S(1)} %collective-permute-done.10.refs_6_.refs_8_), channel_id=1, source_target_pairs={{0,1},{1,0},{2,3},{3,2},{4,5},{5,4},{6,7},{7,6},{8,9},{9,8},{10,11... | collective-permute-start | bytes 1228808 | tf_op jit(solution)/shard_map/ppermute | solution.py:290
  64.1 1.7 %cross.6 = (f32[160,640]{1,0:T(8,128)S(1)}, bf16[160,640]{1,0:T(8,128)(2,1)S(1)}, bf16[160,1280]{1,0:T(8,128)(2,1)S(1)}) custom-call(bf16[640,1536]{1,0:T(8,128)(2,1)S(1)} %stack.5.rows, bf16[320,1536]{1,0:T(8,128)(2,1)S(1)} %collective-permute-done.8.first, bf16[320,1536]{1,0:T(8,128)(2,1)S(1)} %collective-permute-done.9.second), custom_call_target="tpu_custom_call" | custom-call | flops 1258291200 | bytes 12582912 | tf_op jit(solution)/shard_map/cross/pallas_call | solution.py:176
  65.8 0.7 collective-permute-done.14.refs_7_.refs_9_
  66.8 2.8 %collective-permute-start.19 = (bf16[160,1280]{1,0:T(8,128)(2,1)S(1)}, bf16[160,1280]{1,0:T(8,128)(2,1)S(1)}, u32[]{:S(2)}, u32[]{:S(2)}) collective-permute-start(bf16[160,1280]{1,0:T(8,128)(2,1)S(1)} %collective-permute-done.14.refs_7_.refs_9_), channel_id=1, source_target_pairs={{0,1},{1,0},{2,3},{3,2},{4,5},{5,4},{6,7},{7,6},{8,9},{9,8},{10,11... | collective-permute-start | bytes 1228808 | tf_op jit(solution)/shard_map/ppermute | solution.py:290
  69.6 3.3 %collective-permute-done.12.first = bf16[320,1536]{1,0:T(8,128)(2,1)S(1)} collective-permute-done((bf16[320,1536]{1,0:T(8,128)(2,1)S(1)}, bf16[320,1536]{1,0:T(8,128)(2,1)S(1)}, u32[]{:S(2)}, u32[]{:S(2)}) %collective-permute-start.12) | collective-permute-done | bytes 983072 | tf_op jit(solution)/shard_map/ppermute | solution.py:290
  73.2 1.7 %cross.7 = (f32[160,640]{1,0:T(8,128)S(1)}, bf16[160,640]{1,0:T(8,128)(2,1)S(1)}, bf16[160,640]{1,0:T(8,128)(2,1)S(1)}, bf16[160,640]{1,0:T(8,128)(2,1)S(1)}) custom-call(bf16[640,1536]{1,0:T(8,128)(2,1)S(1)} %stack.5.rows, bf16[320,1536]{1,0:T(8,128)(2,1)S(1)} %collective-permute-done.12.first, bf16[320,1536]{1,0:T(8,128)(2,1)S(1)} %collective-permute-done.13.second), custom_call_target="tpu_custom_call" | custom-call | flops 1258291200 | bytes 12582912 | tf_op jit(solution)/shard_map/cross/pallas_call | solution.py:176
  75.0 3.4 %collective-permute-start.22 = (bf16[160,1280]{1,0:T(8,128)(2,1)S(1)}, bf16[160,1280]{1,0:T(8,128)(2,1)S(1)}, u32[]{:S(2)}, u32[]{:S(2)}) collective-permute-start(bf16[160,1280]{1,0:T(8,128)(2,1)S(1)} %collective-permute-done.17.refs_8_.refs_10_), channel_id=1, source_target_pairs={{0,1},{1,0},{2,3},{3,2},{4,5},{5,4},{6,7},{7,6},{8,9},{9,8},{10,11... | collective-permute-start | bytes 1228808 | tf_op jit(solution)/shard_map/ppermute | solution.py:290
  78.7 1.3 %collective-permute-start.23 = (bf16[160,640]{1,0:T(8,128)(2,1)S(1)}, bf16[160,640]{1,0:T(8,128)(2,1)S(1)}, u32[]{:S(2)}, u32[]{:S(2)}) collective-permute-start(bf16[160,640]{1,0:T(8,128)(2,1)S(1)} %get-tuple-element.70), channel_id=1, source_target_pairs={{0,3},{1,2},{2,1},{3,0},{4,7},{5,6},{6,5},{7,4},{8,11},{9,10},{10,... | collective-permute-start | bytes 614408 | tf_op jit(solution)/shard_map/ppermute | solution.py:290
  80.3 2.1 %place.2.refs_16_ = f32[160,10240]{1,0:T(8,128)} custom-call(f32[160,640]{1,0:T(8,128)S(1)} %get-tuple-element.44.refs_0_, f32[160,640]{1,0:T(8,128)S(1)} %get-tuple-element.45.refs_1_, f32[160,640]{1,0:T(8,128)S(1)} %get-tuple-element.46.refs_2_, bf16[160,640]{1,0:T(8,128)(2,1)S(1)} %collective-permute-done.11.refs_3_.refs_4_, ...), custom_call_target="tpu_custom_call" | custom-call | tf_op jit(solution)/shard_map/place/pallas_call | solution.py:237
  82.4 2.8 %collective-permute-done.21.refs_11_ = bf16[160,640]{1,0:T(8,128)(2,1)S(1)} collective-permute-done((bf16[160,640]{1,0:T(8,128)(2,1)S(1)}, bf16[160,640]{1,0:T(8,128)(2,1)S(1)}, u32[]{:S(2)}, u32[]{:S(2)}) %collective-permute-start.21) | collective-permute-done | bytes 204832 | tf_op jit(solution)/shard_map/ppermute | solution.py:290
  85.1 4.5 %collective-permute-done.23.refs_15_ = bf16[160,640]{1,0:T(8,128)(2,1)S(1)} collective-permute-done((bf16[160,640]{1,0:T(8,128)(2,1)S(1)}, bf16[160,640]{1,0:T(8,128)(2,1)S(1)}, u32[]{:S(2)}, u32[]{:S(2)}) %collective-permute-start.23) | collective-permute-done | bytes 204832 | tf_op jit(solution)/shard_map/ppermute | solution.py:290
  89.6 1.8 %place.3 = f32[160,10240]{1,0:T(8,128)} custom-call(f32[160,640]{1,0:T(8,128)S(1)} %get-tuple-element.44.refs_0_, f32[160,640]{1,0:T(8,128)S(1)} %get-tuple-element.45.refs_1_, f32[160,640]{1,0:T(8,128)S(1)} %get-tuple-element.46.refs_2_, f32[160,640]{1,0:T(8,128)S(1)} %get-tuple-element.52.refs_3_, ...), custom_call_target="tpu_custom_call", output_to_operand_aliasing={{}: (16, {})} | custom-call | tf_op jit(solution)/shard_map/place/pallas_call | solution.py:237
  (32 shorter events, 3.4 us)
Async XLA Ops:
  0.0 0.7 copy-start
  0.7 0.7 copy-start.1
  7.8 8.9 %collective-permute-start = (bf16[960,128]{1,0:T(8,128)(2,1)S(1)}, bf16[960,128]{1,0:T(8,128)(2,1)S(1)}, u32[]{:S(2)}, u32[]{:S(2)}) collective-permute-start(bf16[960,128]{1,0:T(8,128)(2,1)S(1)} %get-tuple-element.39), channel_id=1, source_target_pairs={{0,64},{64,0},{1,65},{65,1},{2,66},{66,2},{3,67},{67,3},{4,68},{68... | collective-permute-start | bytes 737288 | tf_op jit(solution)/shard_map/ppermute | solution.py:285
  16.9 11.4 %collective-permute-start.4 = (bf16[160,1536]{1,0:T(8,128)(2,1)S(1)}, bf16[160,1536]{1,0:T(8,128)(2,1)S(1)}, u32[]{:S(2)}, u32[]{:S(2)}) collective-permute-start(bf16[160,1536]{1,0:T(8,128)(2,1)S(1)} %normalize.1.refs_0_), channel_id=1, source_target_pairs={{0,2},{1,3},{2,0},{3,1},{4,6},{5,7},{6,4},{7,5},{8,10},{9,11},{10,... | collective-permute-start | bytes 1474568 | tf_op jit(solution)/shard_map/ppermute | solution.py:290
  18.6 9.7 %collective-permute-start.3 = (bf16[160,1536]{1,0:T(8,128)(2,1)S(1)}, bf16[160,1536]{1,0:T(8,128)(2,1)S(1)}, u32[]{:S(2)}, u32[]{:S(2)}) collective-permute-start(bf16[160,1536]{1,0:T(8,128)(2,1)S(1)} %normalize.1.refs_0_), channel_id=1, source_target_pairs={{32,0},{9,1},{34,2},{11,3},{36,4},{13,5},{38,6},{15,7},{40,8},{1,9... | collective-permute-start | bytes 1474568 | tf_op jit(solution)/shard_map/ppermute | solution.py:290
  21.5 11.8 %collective-permute-start.2 = (bf16[160,1536]{1,0:T(8,128)(2,1)S(1)}, bf16[160,1536]{1,0:T(8,128)(2,1)S(1)}, u32[]{:S(2)}, u32[]{:S(2)}) collective-permute-start(bf16[160,1536]{1,0:T(8,128)(2,1)S(1)} %normalize.1.refs_0_), channel_id=1, source_target_pairs={{48,0},{13,1},{50,2},{15,3},{52,4},{1,5},{54,6},{3,7},{56,8},{5,9}... | collective-permute-start | bytes 1474568 | tf_op jit(solution)/shard_map/ppermute | solution.py:290
  21.9 11.8 %collective-permute-start.1 = (bf16[160,1536]{1,0:T(8,128)(2,1)S(1)}, bf16[160,1536]{1,0:T(8,128)(2,1)S(1)}, u32[]{:S(2)}, u32[]{:S(2)}) collective-permute-start(bf16[160,1536]{1,0:T(8,128)(2,1)S(1)} %normalize.1.refs_0_), channel_id=1, source_target_pairs={{16,0},{5,1},{18,2},{7,3},{20,4},{9,5},{22,6},{11,7},{24,8},{13,9}... | collective-permute-start | bytes 1474568 | tf_op jit(solution)/shard_map/ppermute | solution.py:290
  33.8 8.2 %collective-permute-start.5 = (bf16[320,1536]{1,0:T(8,128)(2,1)S(1)}, bf16[320,1536]{1,0:T(8,128)(2,1)S(1)}, u32[]{:S(2)}, u32[]{:S(2)}) collective-permute-start(bf16[320,1536]{1,0:T(8,128)(2,1)S(1)} %stack.4.refs_0_), channel_id=1, source_target_pairs={{0,1},{1,0},{2,3},{3,2},{4,5},{5,4},{6,7},{7,6},{8,9},{9,8},{10,11... | collective-permute-start | bytes 2949128 | tf_op jit(solution)/shard_map/ppermute | solution.py:290
  37.6 14.5 %collective-permute-start.7 = (bf16[320,1536]{1,0:T(8,128)(2,1)S(1)}, bf16[320,1536]{1,0:T(8,128)(2,1)S(1)}, u32[]{:S(2)}, u32[]{:S(2)}) collective-permute-start(bf16[320,1536]{1,0:T(8,128)(2,1)S(1)} %stack.7.second), channel_id=1, source_target_pairs={{12,0},{49,1},{14,2},{51,3},{0,4},{53,5},{2,6},{55,7},{4,8},{57,9}... | collective-permute-start | bytes 2949128 | tf_op jit(solution)/shard_map/ppermute | solution.py:290
  38.5 14.5 %collective-permute-start.6 = (bf16[320,1536]{1,0:T(8,128)(2,1)S(1)}, bf16[320,1536]{1,0:T(8,128)(2,1)S(1)}, u32[]{:S(2)}, u32[]{:S(2)}) collective-permute-start(bf16[320,1536]{1,0:T(8,128)(2,1)S(1)} %stack.6.first), channel_id=1, source_target_pairs={{4,0},{17,1},{6,2},{19,3},{8,4},{21,5},{10,6},{23,7},{12,8},{25,9}... | collective-permute-start | bytes 2949128 | tf_op jit(solution)/shard_map/ppermute | solution.py:290
  40.5 21.8 %collective-permute-start.8 = (bf16[320,1536]{1,0:T(8,128)(2,1)S(1)}, bf16[320,1536]{1,0:T(8,128)(2,1)S(1)}, u32[]{:S(2)}, u32[]{:S(2)}) collective-permute-start(bf16[320,1536]{1,0:T(8,128)(2,1)S(1)} %stack.7.second), channel_id=1, source_target_pairs={{4,0},{17,1},{6,2},{19,3},{8,4},{21,5},{10,6},{23,7},{12,8},{25,9}... | collective-permute-start | bytes 2949128 | tf_op jit(solution)/shard_map/ppermute | solution.py:290
  41.7 22.4 %collective-permute-start.9 = (bf16[320,1536]{1,0:T(8,128)(2,1)S(1)}, bf16[320,1536]{1,0:T(8,128)(2,1)S(1)}, u32[]{:S(2)}, u32[]{:S(2)}) collective-permute-start(bf16[320,1536]{1,0:T(8,128)(2,1)S(1)} %stack.6.first), channel_id=1, source_target_pairs={{12,0},{49,1},{14,2},{51,3},{0,4},{53,5},{2,6},{55,7},{4,8},{57,9}... | collective-permute-start | bytes 2949128 | tf_op jit(solution)/shard_map/ppermute | solution.py:290
  43.9 10.9 %collective-permute-start.10 = (bf16[160,1280]{1,0:T(8,128)(2,1)S(1)}, bf16[160,1280]{1,0:T(8,128)(2,1)S(1)}, u32[]{:S(2)}, u32[]{:S(2)}) collective-permute-start(bf16[160,1280]{1,0:T(8,128)(2,1)S(1)} %get-tuple-element.48), channel_id=1, source_target_pairs={{0,2},{1,3},{2,0},{3,1},{4,6},{5,7},{6,4},{7,5},{8,10},{9,11},{10,... | collective-permute-start | bytes 1228808 | tf_op jit(solution)/shard_map/ppermute | solution.py:290
  52.2 2.6 %collective-permute-start.11 = (bf16[160,640]{1,0:T(8,128)(2,1)S(1)}, bf16[160,640]{1,0:T(8,128)(2,1)S(1)}, u32[]{:S(2)}, u32[]{:S(2)}) collective-permute-start(bf16[160,640]{1,0:T(8,128)(2,1)S(1)} %get-tuple-element.49), channel_id=1, source_target_pairs={{0,1},{1,0},{2,3},{3,2},{4,5},{5,4},{6,7},{7,6},{8,9},{9,8},{10,11... | collective-permute-start | bytes 614408 | tf_op jit(solution)/shard_map/ppermute | solution.py:290
  54.8 18.1 %collective-permute-start.12 = (bf16[320,1536]{1,0:T(8,128)(2,1)S(1)}, bf16[320,1536]{1,0:T(8,128)(2,1)S(1)}, u32[]{:S(2)}, u32[]{:S(2)}) collective-permute-start(bf16[320,1536]{1,0:T(8,128)(2,1)S(1)} %collective-permute-done.6.first), channel_id=1, source_target_pairs={{4,0},{17,1},{6,2},{19,3},{8,4},{21,5},{10,6},{23,7},{12,8},{25,9}... | collective-permute-start | bytes 2949128 | tf_op jit(solution)/shard_map/ppermute | solution.py:290
  57.2 16.0 %collective-permute-start.13 = (bf16[320,1536]{1,0:T(8,128)(2,1)S(1)}, bf16[320,1536]{1,0:T(8,128)(2,1)S(1)}, u32[]{:S(2)}, u32[]{:S(2)}) collective-permute-start(bf16[320,1536]{1,0:T(8,128)(2,1)S(1)} %collective-permute-done.7.second), channel_id=1, source_target_pairs={{12,0},{49,1},{14,2},{51,3},{0,4},{53,5},{2,6},{55,7},{4,8},{57,9}... | collective-permute-start | bytes 2949128 | tf_op jit(solution)/shard_map/ppermute | solution.py:290
  57.2 9.3 %collective-permute-start.14 = (bf16[160,1280]{1,0:T(8,128)(2,1)S(1)}, bf16[160,1280]{1,0:T(8,128)(2,1)S(1)}, u32[]{:S(2)}, u32[]{:S(2)}) collective-permute-start(bf16[160,1280]{1,0:T(8,128)(2,1)S(1)} %get-tuple-element.55), channel_id=1, source_target_pairs={{0,2},{1,3},{2,0},{3,1},{4,6},{5,7},{6,4},{7,5},{8,10},{9,11},{10,... | collective-permute-start | bytes 1228808 | tf_op jit(solution)/shard_map/ppermute | solution.py:290
  62.4 4.2 %collective-permute-start.16 = (bf16[160,1280]{1,0:T(8,128)(2,1)S(1)}, bf16[160,1280]{1,0:T(8,128)(2,1)S(1)}, u32[]{:S(2)}, u32[]{:S(2)}) collective-permute-start(bf16[160,1280]{1,0:T(8,128)(2,1)S(1)} %collective-permute-done.10.refs_6_.refs_8_), channel_id=1, source_target_pairs={{0,1},{1,0},{2,3},{3,2},{4,5},{5,4},{6,7},{7,6},{8,9},{9,8},{10,11... | collective-permute-start | bytes 1228808 | tf_op jit(solution)/shard_map/ppermute | solution.py:290
  64.1 1.7 %collective-permute-start.15 = (bf16[160,640]{1,0:T(8,128)(2,1)S(1)}, bf16[160,640]{1,0:T(8,128)(2,1)S(1)}, u32[]{:S(2)}, u32[]{:S(2)}) collective-permute-start(bf16[160,640]{1,0:T(8,128)(2,1)S(1)} %get-tuple-element.56), channel_id=1, source_target_pairs={{0,1},{1,0},{2,3},{3,2},{4,5},{5,4},{6,7},{7,6},{8,9},{9,8},{10,11... | collective-permute-start | bytes 614408 | tf_op jit(solution)/shard_map/ppermute | solution.py:290
  66.5 8.4 %collective-permute-start.17 = (bf16[160,1280]{1,0:T(8,128)(2,1)S(1)}, bf16[160,1280]{1,0:T(8,128)(2,1)S(1)}, u32[]{:S(2)}, u32[]{:S(2)}) collective-permute-start(bf16[160,1280]{1,0:T(8,128)(2,1)S(1)} %get-tuple-element.61), channel_id=1, source_target_pairs={{0,2},{1,3},{2,0},{3,1},{4,6},{5,7},{6,4},{7,5},{8,10},{9,11},{10,... | collective-permute-start | bytes 1228808 | tf_op jit(solution)/shard_map/ppermute | solution.py:290
  66.8 8.2 %collective-permute-start.19 = (bf16[160,1280]{1,0:T(8,128)(2,1)S(1)}, bf16[160,1280]{1,0:T(8,128)(2,1)S(1)}, u32[]{:S(2)}, u32[]{:S(2)}) collective-permute-start(bf16[160,1280]{1,0:T(8,128)(2,1)S(1)} %collective-permute-done.14.refs_7_.refs_9_), channel_id=1, source_target_pairs={{0,1},{1,0},{2,3},{3,2},{4,5},{5,4},{6,7},{7,6},{8,9},{9,8},{10,11... | collective-permute-start | bytes 1228808 | tf_op jit(solution)/shard_map/ppermute | solution.py:290
  69.6 5.3 %collective-permute-start.18 = (bf16[160,640]{1,0:T(8,128)(2,1)S(1)}, bf16[160,640]{1,0:T(8,128)(2,1)S(1)}, u32[]{:S(2)}, u32[]{:S(2)}) collective-permute-start(bf16[160,640]{1,0:T(8,128)(2,1)S(1)} %get-tuple-element.62), channel_id=1, source_target_pairs={{0,1},{1,0},{2,3},{3,2},{4,5},{5,4},{6,7},{7,6},{8,9},{9,8},{10,11... | collective-permute-start | bytes 614408 | tf_op jit(solution)/shard_map/ppermute | solution.py:290
  75.0 5.3 %collective-permute-start.22 = (bf16[160,1280]{1,0:T(8,128)(2,1)S(1)}, bf16[160,1280]{1,0:T(8,128)(2,1)S(1)}, u32[]{:S(2)}, u32[]{:S(2)}) collective-permute-start(bf16[160,1280]{1,0:T(8,128)(2,1)S(1)} %collective-permute-done.17.refs_8_.refs_10_), channel_id=1, source_target_pairs={{0,1},{1,0},{2,3},{3,2},{4,5},{5,4},{6,7},{7,6},{8,9},{9,8},{10,11... | collective-permute-start | bytes 1228808 | tf_op jit(solution)/shard_map/ppermute | solution.py:290
  78.4 6.7 %collective-permute-start.21 = (bf16[160,640]{1,0:T(8,128)(2,1)S(1)}, bf16[160,640]{1,0:T(8,128)(2,1)S(1)}, u32[]{:S(2)}, u32[]{:S(2)}) collective-permute-start(bf16[160,640]{1,0:T(8,128)(2,1)S(1)} %get-tuple-element.67), channel_id=1, source_target_pairs={{0,2},{1,3},{2,0},{3,1},{4,6},{5,7},{6,4},{7,5},{8,10},{9,11},{10,... | collective-permute-start | bytes 614408 | tf_op jit(solution)/shard_map/ppermute | solution.py:290
  78.7 10.9 %collective-permute-start.23 = (bf16[160,640]{1,0:T(8,128)(2,1)S(1)}, bf16[160,640]{1,0:T(8,128)(2,1)S(1)}, u32[]{:S(2)}, u32[]{:S(2)}) collective-permute-start(bf16[160,640]{1,0:T(8,128)(2,1)S(1)} %get-tuple-element.70), channel_id=1, source_target_pairs={{0,3},{1,2},{2,1},{3,0},{4,7},{5,6},{6,5},{7,4},{8,11},{9,10},{10,... | collective-permute-start | bytes 614408 | tf_op jit(solution)/shard_map/ppermute | solution.py:290
  80.0 9.6 %collective-permute-start.20 = (bf16[160,640]{1,0:T(8,128)(2,1)S(1)}, bf16[160,640]{1,0:T(8,128)(2,1)S(1)}, u32[]{:S(2)}, u32[]{:S(2)}) collective-permute-start(bf16[160,640]{1,0:T(8,128)(2,1)S(1)} %get-tuple-element.65), channel_id=1, source_target_pairs={{0,1},{1,0},{2,3},{3,2},{4,5},{5,4},{6,7},{7,6},{8,9},{9,8},{10,11... | collective-permute-start | bytes 614408 | tf_op jit(solution)/shard_map/ppermute | solution.py:290

commit v4 on v3

--- a/solution.py
+++ b/solution.py
@@ -20,7 +20,7 @@
 TURN = 2.0 * math.pi / SAMPLES
 
 
-def whiten_kernel(start, width_ref, x_hbm, keep_ref, send_ref, held, table, total, sems):
+def whiten_kernel(bands, x_hbm, keep_ref, send_ref, held, table, total, sems):
     def fetch(piece):
         block = pl.ds(piece * ROWS, ROWS)
         return pltpu.make_async_copy(x_hbm.at[block], held.at[block], sems.at[piece])
@@ -28,7 +28,7 @@
     for piece in range(0, WINS):
         fetch(piece).start()
     lane = lax.broadcasted_iota(jnp.int32, (1, 128), 1)
-    freq = jnp.where(lane < BINS, start[0] + lane, start[1] + lane - BINS)
+    freq = jnp.where(lane < BINS, bands[0] + lane, bands[1] + lane - BINS)
     coarse = lax.broadcasted_iota(jnp.int32, (SAMPLES // PARTS, 128), 0) * PARTS
     fine = lax.broadcasted_iota(jnp.int32, (PARTS, 128), 0)
     angle_a = ((freq * coarse) & (SAMPLES - 1)).astype(jnp.float32) * TURN
@@ -38,11 +38,11 @@
     cos_b, sin_b = jnp.cos(angle_b), jnp.sin(angle_b)
     row = lax.broadcasted_iota(jnp.int32, (256, 128), 0) & 127
     col = lax.broadcasted_iota(jnp.int32, (256, 128), 1)
-    half = jnp.where(col < BINS, width_ref[0], width_ref[1])
+    half = jnp.where(col < BINS, bands[2], bands[3])
     inside = ((row < BINS) == (col < BINS)) & (jnp.abs(row - col) <= half)
     mask = inside.astype(jnp.float32).astype(jnp.bfloat16)
     bin_id = lane & (BINS - 1)
-    width = jnp.where(lane < BINS, width_ref[0], width_ref[1])
+    width = jnp.where(lane < BINS, bands[2], bands[3])
     count = jnp.minimum(bin_id + width, BINS - 1) - jnp.maximum(bin_id - width, 0) + 1
     share = 1.0 / count.astype(jnp.float32)
     first = lax.broadcasted_iota(jnp.int32, (STEP_ROWS, 128), 1) < BINS
@@ -87,13 +87,12 @@
         send_ref[block, :] = jnp.where(mine, band1, band0).astype(jnp.bfloat16)
 
 
-def whiten(flat, band_start, half_width):
+def whiten(flat, bands):
     total = flat.shape[0]
     out = jax.ShapeDtypeStruct((total, 128), jnp.bfloat16)
     return pl.pallas_call(
         whiten_kernel,
         in_specs=[
-            pl.BlockSpec(memory_space=pltpu.SMEM),
             pl.BlockSpec(memory_space=pltpu.SMEM),
             pl.BlockSpec(memory_space=pltpu.HBM),
         ],
@@ -106,7 +105,7 @@
         ],
         compiler_params=pltpu.CompilerParams(vmem_limit_bytes=53 << 20),
         name="whiten",
-    )(band_start, half_width, flat)
+    )(bands, flat)
 
 
 def normalize_kernel(keep_ref, got_ref, out_ref):
@@ -185,9 +184,47 @@
     )(rows, first, second)
 
 
+FIRST = 512
+
+
+def first_cross_kernel(rows, pair0, pair1, mine_ref, c_ref, x_ref, here_ref, cols):
+    cols[:ROWS, :] = pair0[ROWS:, :]
+    cols[ROWS : 3 * ROWS, :] = pair1[...]
+    cols[3 * ROWS :, :] = pair0[:ROWS, :]
+    product = lax.dot_general(
+        rows[...], cols[...], (((1,), (1,)), ((), ())), preferred_element_type=jnp.float32
+    )
+    mine_ref[...] = product[:ROWS]
+    x_ref[:, :FIRST] = product[ROWS : 2 * ROWS, :FIRST].astype(jnp.bfloat16)
+    c_ref[...] = product[2 * ROWS : 3 * ROWS].astype(jnp.bfloat16)
+    x_ref[:, FIRST:] = product[3 * ROWS :, :FIRST].astype(jnp.bfloat16)
+    here_ref[...] = lax.dot_general(
+        rows[:ROWS, :], rows[...], (((1,), (1,)), ((), ())), preferred_element_type=jnp.float32
+    )
+
+
+def first_cross(rows, pair0, pair1):
+    wide = jax.ShapeDtypeStruct((ROWS, GROUP), jnp.float32)
+    return pl.pallas_call(
+        first_cross_kernel,
+        out_shape=[
+            wide,
+            jax.ShapeDtypeStruct((ROWS, GROUP), jnp.bfloat16),
+            jax.ShapeDtypeStruct((ROWS, 2 * FIRST), jnp.bfloat16),
+            wide,
+        ],
+        scratch_shapes=[pltpu.VMEM((4 * ROWS, DEPTH), jnp.bfloat16)],
+        compiler_params=pltpu.CompilerParams(vmem_limit_bytes=12 << 20),
+        cost_estimate=pl.CostEstimate(
+            flops=2 * GROUP * GROUP * DEPTH, transcendentals=0, bytes_accessed=12 << 20
+        ),
+        name="cross",
+    )(rows, pair0, pair1)
+
+
 NEAR = (0, 1, -1, 2)
 GROUPS = (
-    ((0, 0), (1, 0), (-1, 0), (2, 0)),
+    ((1, 0), (-1, 0), (2, 0), (0, 0)),
     ((0, 1), (1, 1), (-1, -1), (2, -1)),
     ((-1, 1), (2, 1), (0, -1), (1, -1)),
     ((0, 2), (1, 2), (-1, 2), (2, 2)),
@@ -195,7 +232,7 @@
 SPOT = {offset: (g, i) for g, group in enumerate(GROUPS) for i, offset in enumerate(group)}
 
 
-def place_kernel(blocks, groups, kinds, *refs):
+def place_kernel(blocks, kinds, *refs):
     out, buf, sems = refs[-3:]
     pieces = {}
     for index, kind in enumerate(kinds):
@@ -217,9 +254,12 @@
             for n, (du, dv) in enumerate(blocks):
                 for turn in range(4):
                     g, i = SPOT[(dv, du) if turn % 2 else (du, dv)]
-                    ref, base = pieces[turn, g], 0
-                    if ref.shape[1] == 2 * GROUP and turn == 3:
-                        base = GROUP
+                    if (du, dv) == (0, 0):
+                        ref, base, i = pieces[4, 0], 0, (0, 2, 1, 3)[turn]
+                    else:
+                        ref = pieces[turn, g]
+                        split = turn == 3 and ref.shape[1] > GROUP
+                        base = ref.shape[1] // 2 if split else 0
                     value = ref[:, base + i * ROWS : base + (i + 1) * ROWS].astype(jnp.float32)
                     at = (slot ^ turn) * ROWS
                     buf[n, :, at : at + ROWS] = value
@@ -231,11 +271,15 @@
 
 def place(blocks, pieces, out):
     vmem = pl.BlockSpec(memory_space=pltpu.VMEM)
-    groups = sorted({g for _, g in pieces})
-    kinds = sorted(pieces)
+    used = {(4, 0)} if (0, 0) in blocks else set()
+    for du, dv in blocks:
+        if (du, dv) != (0, 0):
+            for turn in range(4):
+                used.add((turn, SPOT[(dv, du) if turn % 2 else (du, dv)][0]))
+    kinds = sorted(used, key=lambda kind: (kind[1], kind[0]))
     prior = () if out is None else (out,)
     return pl.pallas_call(
-        lambda *refs: place_kernel(blocks, groups, kinds, *refs),
+        lambda *refs: place_kernel(blocks, kinds, *refs),
         in_specs=[vmem] * len(kinds) + [pl.BlockSpec(memory_space=pl.ANY)] * len(prior),
         out_specs=pl.BlockSpec(memory_space=pl.ANY),
         out_shape=jax.ShapeDtypeStruct((ROWS, 16 * GROUP), jnp.float32),
@@ -281,7 +325,7 @@
 
 def local(traces, band_start, half_width):
     flat = jnp.transpose(traces, (1, 0, 2)).reshape(WINS * ROWS, SAMPLES)
-    keep, send = whiten(flat, band_start, half_width)
+    keep, send = whiten(flat, jnp.concatenate([band_start, half_width]))
     got = lax.ppermute(send, "band", [(0, 1), (1, 0)])
     own = normalize(keep, got)
     hold = lax.optimization_barrier
@@ -289,26 +333,26 @@
     def move(value, pairs):
         return lax.ppermute(value, "chan", pairs)
 
-    ahead, behind = move(own, from_first(1)), move(own, from_first(-1))
-    far, over = move(own, from_first(2)), move(own, flip(2))
-    ahead, behind, far, over = hold((ahead, behind, far, over))
+    over, far = move(own, flip(2)), move(own, from_first(2))
+    behind, ahead = move(own, from_first(-1)), move(own, from_first(1))
+    over, far, behind, ahead = hold((over, far, behind, ahead))
     mates = stack(own, over)
     across = move(mates, flip(1))
     pair0, pair1 = stack(own, ahead), stack(behind, far)
     up0, down1 = move(pair0, from_second(1)), move(pair1, from_second(-1))
     up1, down0 = move(pair1, from_second(1)), move(pair0, from_second(-1))
     rows = stack(mates, across)
-    mine0, c0, x0 = cross(rows, pair0, pair1, True)
+    mine0, c0, x0, here = first_cross(rows, pair0, pair1)
     x0 = move(x0, flip(2))
     c0 = move(c0, flip(1))
     mine1, c1, x1 = cross(rows, up0, down1, True)
     x1, x0, c0, up0, down1 = hold((x1, x0, c0, up0, down1))
+    up2, down2 = move(up0, from_second(1)), move(down1, from_second(-1))
     x1 = move(x1, flip(2))
-    up2, down2 = move(up0, from_second(1)), move(down1, from_second(-1))
     xc0 = move(x0, flip(1))
     c1 = move(c1, flip(1))
     mine2, c2, x2 = cross(rows, up1, down0, True)
-    x2, x1, c1, xc0 = hold((x2, x1, c1, xc0))
+    x2, c1, xc0 = hold((x2, c1, xc0))
     x2 = move(x2, flip(2))
     xc1 = move(x1, flip(1))
     c2 = move(c2, flip(1))
@@ -317,14 +361,16 @@
     x3, xc3, c3 = move(x3, flip(2)), move(xc3, flip(3)), move(c3, flip(1))
     xc2 = move(x2, flip(1))
     early = [(du, dv) for du in NEAR for dv in NEAR if du != 2 and dv != 2]
-    late = [(du, dv) for du in NEAR for dv in NEAR if du == 2 or dv == 2]
-    pieces = {}
+    middle = [(0, 2), (1, 2), (-1, 2)]
+    late = [(2, dv) for dv in NEAR]
+    pieces = {(4, 0): here}
     for g, parts in enumerate(((mine0, c0, x0, xc0), (mine1, c1, x1, xc1), (mine2, c2, x2, xc2))):
         for turn in range(4):
             pieces[turn, g] = parts[turn]
     out = place(early, pieces, None)
-    for turn, part in enumerate((mine3, c3, x3, xc3)):
-        pieces[turn, 3] = part
+    pieces[0, 3], pieces[2, 3] = mine3, x3
+    out = place(middle, pieces, out)
+    pieces[1, 3], pieces[3, 3] = c3, xc3
     return place(late, pieces, out)[None]
 
 

time: 92.5 us -> 90.9 us (0.983)
  starting transfers between devices: 33 us -> 31.2 us
  Pallas kernels: 17.8 us -> 19.2 us
  local copies, waits for them, and re-layouts: 1.31 us -> 0 us
    pallas_call x2 -> x4, Pallas kernels: 3.86 us -> 6.97 us  [the longest x3 4.69 us: place(): pl.pallas_call(lambda *refs: place_kernel(blocks, kinds, *refs), in_specs...]
    ppermute x23, starting transfers between devices: 29.3 us -> 27.5 us  [move(): return lax.ppermute(value, 'chan', pairs)]
    pallas_call x4 -> x3, Pallas kernels: 6.86 us -> 5.14 us  [cross(): pl.pallas_call(cross_kernel, out_shape=[mine, narrow, wide] if merged els...]
    unnamed x4 -> x0, local copies, waits for them, and re-layouts: 1.31 us -> none
  transfers between devices with their start and end apart: 24 -> 24, of which waited for: 11 -> 10; matrix products, arithmetic and copies ran while one was open for 0% -> 0% of each run, Pallas kernels for 10% -> 12%
where the time goes in v4:
time: 90.9 us; the launch traced here: 90.8 us
  waiting for transfers between devices  39.3 us (43%)
  starting transfers between devices  31.2 us (34%)
  Pallas kernels  19.2 us (21%)
    ppermute x23, waiting for transfers between devices, move(): return lax.ppermute(value, 'chan', pairs)  34.1 us
    ppermute x23, starting transfers between devices, move(): return lax.ppermute(value, 'chan', pairs)  27.5 us
    pallas_call x1, Pallas kernels, whiten(): pl.pallas_call(whiten_kernel, in_specs=[pl.BlockSpec(memory_space=pltpu.S...  6.49 us
    ppermute x1, waiting for transfers between devices, local(): got = lax.ppermute(send, 'band', [(0, 1), (1, 0)])  5.2 us
    pallas_call x3, Pallas kernels, cross(): pl.pallas_call(cross_kernel, out_shape=[mine, narrow, wide] if merged els...  5.14 us
    pallas_call x3, Pallas kernels, place(): pl.pallas_call(lambda *refs: place_kernel(blocks, kinds, *refs), in_specs...  4.69 us
    ppermute x1, starting transfers between devices, local(): got = lax.ppermute(send, 'band', [(0, 1), (1, 0)])  3.65 us
    pallas_call x1, Pallas kernels, first_cross(): pl.pallas_call(first_cross_kernel, out_shape=[wide, jax.ShapeDtypeStruct(...  2.28 us
  transfers between devices with their start and end apart: 24, of which 10 were waited for; matrix products, arithmetic and copies ran while one was open for 0% of the time, Pallas kernels for 12%

profile of v4, /device:TPU:1, one launch (start us, length us, event | category | flops | bytes accessed | tf_op | source)
XLA Modules:
  0.0 90.8 jit_solution(6775704269712304166)
XLA Ops:
  0.7 6.5 %whiten.1 = (bf16[960,128]{1,0:T(8,128)(2,1)S(1)}, bf16[960,128]{1,0:T(8,128)(2,1)S(1)}) custom-call(s32[4]{0:T(128)S(1)} %pad_add_fusion.bands, bf16[960,4096]{1,0:T(8,128)(2,1)} %bitcast.4), custom_call_target="tpu_custom_call" | custom-call | tf_op jit(solution)/shard_map/whiten/pallas_call | solution.py:93
  7.2 3.7 %collective-permute-start = (bf16[960,128]{1,0:T(8,128)(2,1)S(1)}, bf16[960,128]{1,0:T(8,128)(2,1)S(1)}, u32[]{:S(2)}, u32[]{:S(2)}) collective-permute-start(bf16[960,128]{1,0:T(8,128)(2,1)S(1)} %get-tuple-element.39), channel_id=1, source_target_pairs={{0,64},{64,0},{1,65},{65,1},{2,66},{66,2},{3,67},{67,3},{4,68},{68... | collective-permute-start | bytes 737288 | tf_op jit(solution)/shard_map/ppermute | solution.py:329
  10.9 5.2 %collective-permute-done.got_ref = bf16[960,128]{1,0:T(8,128)(2,1)S(1)} collective-permute-done((bf16[960,128]{1,0:T(8,128)(2,1)S(1)}, bf16[960,128]{1,0:T(8,128)(2,1)S(1)}, u32[]{:S(2)}, u32[]{:S(2)}) %collective-permute-start) | collective-permute-done | bytes 245792 | tf_op jit(solution)/shard_map/ppermute | solution.py:329
  16.3 3.2 %collective-permute-start.4 = (bf16[160,1536]{1,0:T(8,128)(2,1)S(1)}, bf16[160,1536]{1,0:T(8,128)(2,1)S(1)}, u32[]{:S(2)}, u32[]{:S(2)}) collective-permute-start(bf16[160,1536]{1,0:T(8,128)(2,1)S(1)} %normalize.1.refs_0_), channel_id=1, source_target_pairs={{16,0},{5,1},{18,2},{7,3},{20,4},{9,5},{22,6},{11,7},{24,8},{13,9}... | collective-permute-start | bytes 1474568 | tf_op jit(solution)/shard_map/ppermute | solution.py:334
  19.5 1.6 %collective-permute-start.2 = (bf16[160,1536]{1,0:T(8,128)(2,1)S(1)}, bf16[160,1536]{1,0:T(8,128)(2,1)S(1)}, u32[]{:S(2)}, u32[]{:S(2)}) collective-permute-start(bf16[160,1536]{1,0:T(8,128)(2,1)S(1)} %normalize.1.refs_0_), channel_id=1, source_target_pairs={{32,0},{9,1},{34,2},{11,3},{36,4},{13,5},{38,6},{15,7},{40,8},{1,9... | collective-permute-start | bytes 1474568 | tf_op jit(solution)/shard_map/ppermute | solution.py:334
  21.2 1.2 %collective-permute-start.1 = (bf16[160,1536]{1,0:T(8,128)(2,1)S(1)}, bf16[160,1536]{1,0:T(8,128)(2,1)S(1)}, u32[]{:S(2)}, u32[]{:S(2)}) collective-permute-start(bf16[160,1536]{1,0:T(8,128)(2,1)S(1)} %normalize.1.refs_0_), channel_id=1, source_target_pairs={{0,2},{1,3},{2,0},{3,1},{4,6},{5,7},{6,4},{7,5},{8,10},{9,11},{10,... | collective-permute-start | bytes 1474568 | tf_op jit(solution)/shard_map/ppermute | solution.py:334
  22.4 8.2 %collective-permute-done.4.refs_1_ = bf16[160,1536]{1,0:T(8,128)(2,1)S(1)} collective-permute-done((bf16[160,1536]{1,0:T(8,128)(2,1)S(1)}, bf16[160,1536]{1,0:T(8,128)(2,1)S(1)}, u32[]{:S(2)}, u32[]{:S(2)}) %collective-permute-start.4) | collective-permute-done | bytes 491552 | tf_op jit(solution)/shard_map/ppermute | solution.py:334
  30.6 3.4 %collective-permute-done.3.refs_0_ = bf16[160,1536]{1,0:T(8,128)(2,1)S(1)} collective-permute-done((bf16[160,1536]{1,0:T(8,128)(2,1)S(1)}, bf16[160,1536]{1,0:T(8,128)(2,1)S(1)}, u32[]{:S(2)}, u32[]{:S(2)}) %collective-permute-start.3) | collective-permute-done | bytes 491552 | tf_op jit(solution)/shard_map/ppermute | solution.py:334
  34.1 3.8 %collective-permute-start.5 = (bf16[320,1536]{1,0:T(8,128)(2,1)S(1)}, bf16[320,1536]{1,0:T(8,128)(2,1)S(1)}, u32[]{:S(2)}, u32[]{:S(2)}) collective-permute-start(bf16[320,1536]{1,0:T(8,128)(2,1)S(1)} %stack.4.refs_0_), channel_id=1, source_target_pairs={{0,1},{1,0},{2,3},{3,2},{4,5},{5,4},{6,7},{7,6},{8,9},{9,8},{10,11... | collective-permute-start | bytes 2949128 | tf_op jit(solution)/shard_map/ppermute | solution.py:334
  38.1 2.7 %collective-permute-start.6 = (bf16[320,1536]{1,0:T(8,128)(2,1)S(1)}, bf16[320,1536]{1,0:T(8,128)(2,1)S(1)}, u32[]{:S(2)}, u32[]{:S(2)}) collective-permute-start(bf16[320,1536]{1,0:T(8,128)(2,1)S(1)} %stack.6.pair0), channel_id=1, source_target_pairs={{4,0},{17,1},{6,2},{19,3},{8,4},{21,5},{10,6},{23,7},{12,8},{25,9}... | collective-permute-start | bytes 2949128 | tf_op jit(solution)/shard_map/ppermute | solution.py:334
  40.9 1.4 %collective-permute-start.12 = (bf16[320,1536]{1,0:T(8,128)(2,1)S(1)}, bf16[320,1536]{1,0:T(8,128)(2,1)S(1)}, u32[]{:S(2)}, u32[]{:S(2)}) collective-permute-start(bf16[320,1536]{1,0:T(8,128)(2,1)S(1)} %stack.6.pair0), channel_id=1, source_target_pairs={{12,0},{49,1},{14,2},{51,3},{0,4},{53,5},{2,6},{55,7},{4,8},{57,9}... | collective-permute-start | bytes 2949128 | tf_op jit(solution)/shard_map/ppermute | solution.py:334
  42.4 2.3 %cross.4 = (f32[160,640]{1,0:T(8,128)S(1)}, bf16[160,640]{1,0:T(8,128)(2,1)S(1)}, bf16[160,1024]{1,0:T(8,128)(2,1)S(1)}, f32[160,640]{1,0:T(8,128)S(1)}) custom-call(bf16[640,1536]{1,0:T(8,128)(2,1)S(1)} %stack.5.rows, bf16[320,1536]{1,0:T(8,128)(2,1)S(1)} %stack.6.pair0, bf16[320,1536]{1,0:T(8,128)(2,1)S(1)} %stack.7.pair1), custom_call_target="tpu_custom_call" | custom-call | flops 1258291200 | bytes 12582912 | tf_op jit(solution)/shard_map/cross/pallas_call | solution.py:208
  44.7 1.3 %collective-permute-start.8 = (bf16[160,1024]{1,0:T(8,128)(2,1)S(1)}, bf16[160,1024]{1,0:T(8,128)(2,1)S(1)}, u32[]{:S(2)}, u32[]{:S(2)}) collective-permute-start(bf16[160,1024]{1,0:T(8,128)(2,1)S(1)} %get-tuple-element.46), channel_id=1, source_target_pairs={{0,2},{1,3},{2,0},{3,1},{4,6},{5,7},{6,4},{7,5},{8,10},{9,11},{10,... | collective-permute-start | bytes 983048 | tf_op jit(solution)/shard_map/ppermute | solution.py:334
  46.0 6.5 %collective-permute-done.7.second = bf16[320,1536]{1,0:T(8,128)(2,1)S(1)} collective-permute-done((bf16[320,1536]{1,0:T(8,128)(2,1)S(1)}, bf16[320,1536]{1,0:T(8,128)(2,1)S(1)}, u32[]{:S(2)}, u32[]{:S(2)}) %collective-permute-start.7) | collective-permute-done | bytes 983072 | tf_op jit(solution)/shard_map/ppermute | solution.py:334
  53.3 1.7 %cross.5 = (f32[160,640]{1,0:T(8,128)S(1)}, bf16[160,640]{1,0:T(8,128)(2,1)S(1)}, bf16[160,1280]{1,0:T(8,128)(2,1)S(1)}) custom-call(bf16[640,1536]{1,0:T(8,128)(2,1)S(1)} %stack.5.rows, bf16[320,1536]{1,0:T(8,128)(2,1)S(1)} %collective-permute-done.6.first, bf16[320,1536]{1,0:T(8,128)(2,1)S(1)} %collective-permute-done.7.second), custom_call_target="tpu_custom_call" | custom-call | flops 1258291200 | bytes 12582912 | tf_op jit(solution)/shard_map/cross/pallas_call | solution.py:175
  55.0 2.0 %collective-permute-start.13 = (bf16[320,1536]{1,0:T(8,128)(2,1)S(1)}, bf16[320,1536]{1,0:T(8,128)(2,1)S(1)}, u32[]{:S(2)}, u32[]{:S(2)}) collective-permute-start(bf16[320,1536]{1,0:T(8,128)(2,1)S(1)} %collective-permute-done.6.first), channel_id=1, source_target_pairs={{4,0},{17,1},{6,2},{19,3},{8,4},{21,5},{10,6},{23,7},{12,8},{25,9}... | collective-permute-start | bytes 2949128 | tf_op jit(solution)/shard_map/ppermute | solution.py:334
  57.1 1.2 %collective-permute-start.10 = (bf16[160,1280]{1,0:T(8,128)(2,1)S(1)}, bf16[160,1280]{1,0:T(8,128)(2,1)S(1)}, u32[]{:S(2)}, u32[]{:S(2)}) collective-permute-start(bf16[160,1280]{1,0:T(8,128)(2,1)S(1)} %get-tuple-element.50), channel_id=1, source_target_pairs={{0,2},{1,3},{2,0},{3,1},{4,6},{5,7},{6,4},{7,5},{8,10},{9,11},{10,... | collective-permute-start | bytes 1228808 | tf_op jit(solution)/shard_map/ppermute | solution.py:334
  58.3 4.1 %collective-permute-done.11.first = bf16[320,1536]{1,0:T(8,128)(2,1)S(1)} collective-permute-done((bf16[320,1536]{1,0:T(8,128)(2,1)S(1)}, bf16[320,1536]{1,0:T(8,128)(2,1)S(1)}, u32[]{:S(2)}, u32[]{:S(2)}) %collective-permute-start.11) | collective-permute-done | bytes 983072 | tf_op jit(solution)/shard_map/ppermute | solution.py:334
  62.4 2.0 %collective-permute-start.16 = (bf16[160,1024]{1,0:T(8,128)(2,1)S(1)}, bf16[160,1024]{1,0:T(8,128)(2,1)S(1)}, u32[]{:S(2)}, u32[]{:S(2)}) collective-permute-start(bf16[160,1024]{1,0:T(8,128)(2,1)S(1)} %collective-permute-done.8.refs_2_.refs_1_), channel_id=1, source_target_pairs={{0,1},{1,0},{2,3},{3,2},{4,5},{5,4},{6,7},{7,6},{8,9},{9,8},{10,11... | collective-permute-start | bytes 983048 | tf_op jit(solution)/shard_map/ppermute | solution.py:334
  64.4 1.7 %cross.6 = (f32[160,640]{1,0:T(8,128)S(1)}, bf16[160,640]{1,0:T(8,128)(2,1)S(1)}, bf16[160,1280]{1,0:T(8,128)(2,1)S(1)}) custom-call(bf16[640,1536]{1,0:T(8,128)(2,1)S(1)} %stack.5.rows, bf16[320,1536]{1,0:T(8,128)(2,1)S(1)} %collective-permute-done.11.first, bf16[320,1536]{1,0:T(8,128)(2,1)S(1)} %collective-permute-done.12.second), custom_call_target="tpu_custom_call" | custom-call | flops 1258291200 | bytes 12582912 | tf_op jit(solution)/shard_map/cross/pallas_call | solution.py:175
  66.1 1.3 %collective-permute-start.17 = (bf16[160,1280]{1,0:T(8,128)(2,1)S(1)}, bf16[160,1280]{1,0:T(8,128)(2,1)S(1)}, u32[]{:S(2)}, u32[]{:S(2)}) collective-permute-start(bf16[160,1280]{1,0:T(8,128)(2,1)S(1)} %get-tuple-element.58), channel_id=1, source_target_pairs={{0,2},{1,3},{2,0},{3,1},{4,6},{5,7},{6,4},{7,5},{8,10},{9,11},{10,... | collective-permute-start | bytes 1228808 | tf_op jit(solution)/shard_map/ppermute | solution.py:334
  67.4 1.6 %collective-permute-start.19 = (bf16[160,1280]{1,0:T(8,128)(2,1)S(1)}, bf16[160,1280]{1,0:T(8,128)(2,1)S(1)}, u32[]{:S(2)}, u32[]{:S(2)}) collective-permute-start(bf16[160,1280]{1,0:T(8,128)(2,1)S(1)} %collective-permute-done.10.refs_7_.refs_3_), channel_id=1, source_target_pairs={{0,1},{1,0},{2,3},{3,2},{4,5},{5,4},{6,7},{7,6},{8,9},{9,8},{10,11... | collective-permute-start | bytes 1228808 | tf_op jit(solution)/shard_map/ppermute | solution.py:334
  69.0 4.0 %collective-permute-done.13.first = bf16[320,1536]{1,0:T(8,128)(2,1)S(1)} collective-permute-done((bf16[320,1536]{1,0:T(8,128)(2,1)S(1)}, bf16[320,1536]{1,0:T(8,128)(2,1)S(1)}, u32[]{:S(2)}, u32[]{:S(2)}) %collective-permute-start.13) | collective-permute-done | bytes 983072 | tf_op jit(solution)/shard_map/ppermute | solution.py:334
  73.5 1.7 %cross.7 = (f32[160,640]{1,0:T(8,128)S(1)}, bf16[160,640]{1,0:T(8,128)(2,1)S(1)}, bf16[160,640]{1,0:T(8,128)(2,1)S(1)}, bf16[160,640]{1,0:T(8,128)(2,1)S(1)}) custom-call(bf16[640,1536]{1,0:T(8,128)(2,1)S(1)} %stack.5.rows, bf16[320,1536]{1,0:T(8,128)(2,1)S(1)} %collective-permute-done.13.first, bf16[320,1536]{1,0:T(8,128)(2,1)S(1)} %collective-permute-done.14.second), custom_call_target="tpu_custom_call" | custom-call | flops 1258291200 | bytes 12582912 | tf_op jit(solution)/shard_map/cross/pallas_call | solution.py:175
  75.2 1.5 %collective-permute-done.17.refs_11_.refs_5_ = bf16[160,1280]{1,0:T(8,128)(2,1)S(1)} collective-permute-done((bf16[160,1280]{1,0:T(8,128)(2,1)S(1)}, bf16[160,1280]{1,0:T(8,128)(2,1)S(1)}, u32[]{:S(2)}, u32[]{:S(2)}) %collective-permute-start.17) | collective-permute-done | bytes 409632 | tf_op jit(solution)/shard_map/ppermute | solution.py:334
  76.7 1.4 %collective-permute-start.23 = (bf16[160,1280]{1,0:T(8,128)(2,1)S(1)}, bf16[160,1280]{1,0:T(8,128)(2,1)S(1)}, u32[]{:S(2)}, u32[]{:S(2)}) collective-permute-start(bf16[160,1280]{1,0:T(8,128)(2,1)S(1)} %collective-permute-done.17.refs_11_.refs_5_), channel_id=1, source_target_pairs={{0,1},{1,0},{2,3},{3,2},{4,5},{5,4},{6,7},{7,6},{8,9},{9,8},{10,11... | collective-permute-start | bytes 1228808 | tf_op jit(solution)/shard_map/ppermute | solution.py:334
  78.1 1.2 %collective-permute-start.21 = (bf16[160,640]{1,0:T(8,128)(2,1)S(1)}, bf16[160,640]{1,0:T(8,128)(2,1)S(1)}, u32[]{:S(2)}, u32[]{:S(2)}) collective-permute-start(bf16[160,640]{1,0:T(8,128)(2,1)S(1)} %get-tuple-element.63), channel_id=1, source_target_pairs={{0,2},{1,3},{2,0},{3,1},{4,6},{5,7},{6,4},{7,5},{8,10},{9,11},{10,... | collective-permute-start | bytes 614408 | tf_op jit(solution)/shard_map/ppermute | solution.py:334
  79.9 2.1 %place.3.refs_8_ = f32[160,10240]{1,0:T(8,128)} custom-call(f32[160,640]{1,0:T(8,128)S(1)} %get-tuple-element.44.refs_0_, bf16[160,640]{1,0:T(8,128)(2,1)S(1)} %collective-permute-done.9.refs_1_.refs_0_, bf16[160,1024]{1,0:T(8,128)(2,1)S(1)} %collective-permute-done.8.refs_2_.refs_1_, bf16[160,1024]{1,0:T(8,128)(2,1)S(1)} %collective-permute-done.16.refs_3_.refs_1_, ...), custom_call_target="tpu_custom_call" | custom-call | tf_op jit(solution)/shard_map/place/pallas_call | solution.py:281
  82.1 2.7 %collective-permute-done.21.refs_7_.refs_8_ = bf16[160,640]{1,0:T(8,128)(2,1)S(1)} collective-permute-done((bf16[160,640]{1,0:T(8,128)(2,1)S(1)}, bf16[160,640]{1,0:T(8,128)(2,1)S(1)}, u32[]{:S(2)}, u32[]{:S(2)}) %collective-permute-start.21) | collective-permute-done | bytes 204832 | tf_op jit(solution)/shard_map/ppermute | solution.py:334
  84.8 1.2 %place.4.refs_10_ = f32[160,10240]{1,0:T(8,128)} custom-call(bf16[160,640]{1,0:T(8,128)(2,1)S(1)} %collective-permute-done.9.refs_1_.refs_0_, bf16[160,1024]{1,0:T(8,128)(2,1)S(1)} %collective-permute-done.16.refs_3_.refs_1_, bf16[160,640]{1,0:T(8,128)(2,1)S(1)} %collective-permute-done.15.refs_6_.refs_2_, ...), custom_call_target="tpu_custom_call", output_to_operand_aliasing={{}: (8, {})} | custom-call | tf_op jit(solution)/shard_map/place/pallas_call | solution.py:281
  86.0 3.3 %collective-permute-done.22.refs_9_ = bf16[160,640]{1,0:T(8,128)(2,1)S(1)} collective-permute-done((bf16[160,640]{1,0:T(8,128)(2,1)S(1)}, bf16[160,640]{1,0:T(8,128)(2,1)S(1)}, u32[]{:S(2)}, u32[]{:S(2)}) %collective-permute-start.22) | collective-permute-done | bytes 204832 | tf_op jit(solution)/shard_map/ppermute | solution.py:334
  89.3 1.3 %place.5 = f32[160,10240]{1,0:T(8,128)} custom-call(f32[160,640]{1,0:T(8,128)S(1)} %get-tuple-element.44.refs_0_, bf16[160,1024]{1,0:T(8,128)(2,1)S(1)} %collective-permute-done.8.refs_2_.refs_1_, f32[160,640]{1,0:T(8,128)S(1)} %get-tuple-element.49.refs_5_.refs_2_, ...), custom_call_target="tpu_custom_call", output_to_operand_aliasing={{}: (10, {})} | custom-call | tf_op jit(solution)/shard_map/place/pallas_call | solution.py:281
  (30 shorter events, 3.6 us)
Async XLA Ops:
  7.2 8.9 %collective-permute-start = (bf16[960,128]{1,0:T(8,128)(2,1)S(1)}, bf16[960,128]{1,0:T(8,128)(2,1)S(1)}, u32[]{:S(2)}, u32[]{:S(2)}) collective-permute-start(bf16[960,128]{1,0:T(8,128)(2,1)S(1)} %get-tuple-element.39), channel_id=1, source_target_pairs={{0,64},{64,0},{1,65},{65,1},{2,66},{66,2},{3,67},{67,3},{4,68},{68... | collective-permute-start | bytes 737288 | tf_op jit(solution)/shard_map/ppermute | solution.py:329
  16.3 14.2 %collective-permute-start.4 = (bf16[160,1536]{1,0:T(8,128)(2,1)S(1)}, bf16[160,1536]{1,0:T(8,128)(2,1)S(1)}, u32[]{:S(2)}, u32[]{:S(2)}) collective-permute-start(bf16[160,1536]{1,0:T(8,128)(2,1)S(1)} %normalize.1.refs_0_), channel_id=1, source_target_pairs={{16,0},{5,1},{18,2},{7,3},{20,4},{9,5},{22,6},{11,7},{24,8},{13,9}... | collective-permute-start | bytes 1474568 | tf_op jit(solution)/shard_map/ppermute | solution.py:334
  19.5 14.5 %collective-permute-start.3 = (bf16[160,1536]{1,0:T(8,128)(2,1)S(1)}, bf16[160,1536]{1,0:T(8,128)(2,1)S(1)}, u32[]{:S(2)}, u32[]{:S(2)}) collective-permute-start(bf16[160,1536]{1,0:T(8,128)(2,1)S(1)} %normalize.1.refs_0_), channel_id=1, source_target_pairs={{48,0},{13,1},{50,2},{15,3},{52,4},{1,5},{54,6},{3,7},{56,8},{5,9}... | collective-permute-start | bytes 1474568 | tf_op jit(solution)/shard_map/ppermute | solution.py:334
  19.5 14.5 %collective-permute-start.2 = (bf16[160,1536]{1,0:T(8,128)(2,1)S(1)}, bf16[160,1536]{1,0:T(8,128)(2,1)S(1)}, u32[]{:S(2)}, u32[]{:S(2)}) collective-permute-start(bf16[160,1536]{1,0:T(8,128)(2,1)S(1)} %normalize.1.refs_0_), channel_id=1, source_target_pairs={{32,0},{9,1},{34,2},{11,3},{36,4},{13,5},{38,6},{15,7},{40,8},{1,9... | collective-permute-start | bytes 1474568 | tf_op jit(solution)/shard_map/ppermute | solution.py:334
  21.2 12.8 %collective-permute-start.1 = (bf16[160,1536]{1,0:T(8,128)(2,1)S(1)}, bf16[160,1536]{1,0:T(8,128)(2,1)S(1)}, u32[]{:S(2)}, u32[]{:S(2)}) collective-permute-start(bf16[160,1536]{1,0:T(8,128)(2,1)S(1)} %normalize.1.refs_0_), channel_id=1, source_target_pairs={{0,2},{1,3},{2,0},{3,1},{4,6},{5,7},{6,4},{7,5},{8,10},{9,11},{10,... | collective-permute-start | bytes 1474568 | tf_op jit(solution)/shard_map/ppermute | solution.py:334
  34.1 8.2 %collective-permute-start.5 = (bf16[320,1536]{1,0:T(8,128)(2,1)S(1)}, bf16[320,1536]{1,0:T(8,128)(2,1)S(1)}, u32[]{:S(2)}, u32[]{:S(2)}) collective-permute-start(bf16[320,1536]{1,0:T(8,128)(2,1)S(1)} %stack.4.refs_0_), channel_id=1, source_target_pairs={{0,1},{1,0},{2,3},{3,2},{4,5},{5,4},{6,7},{7,6},{8,9},{9,8},{10,11... | collective-permute-start | bytes 2949128 | tf_op jit(solution)/shard_map/ppermute | solution.py:334
  37.9 14.5 %collective-permute-start.7 = (bf16[320,1536]{1,0:T(8,128)(2,1)S(1)}, bf16[320,1536]{1,0:T(8,128)(2,1)S(1)}, u32[]{:S(2)}, u32[]{:S(2)}) collective-permute-start(bf16[320,1536]{1,0:T(8,128)(2,1)S(1)} %stack.7.pair1), channel_id=1, source_target_pairs={{12,0},{49,1},{14,2},{51,3},{0,4},{53,5},{2,6},{55,7},{4,8},{57,9}... | collective-permute-start | bytes 2949128 | tf_op jit(solution)/shard_map/ppermute | solution.py:334
  38.1 15.2 %collective-permute-start.6 = (bf16[320,1536]{1,0:T(8,128)(2,1)S(1)}, bf16[320,1536]{1,0:T(8,128)(2,1)S(1)}, u32[]{:S(2)}, u32[]{:S(2)}) collective-permute-start(bf16[320,1536]{1,0:T(8,128)(2,1)S(1)} %stack.6.pair0), channel_id=1, source_target_pairs={{4,0},{17,1},{6,2},{19,3},{8,4},{21,5},{10,6},{23,7},{12,8},{25,9}... | collective-permute-start | bytes 2949128 | tf_op jit(solution)/shard_map/ppermute | solution.py:334
  40.8 21.6 %collective-permute-start.11 = (bf16[320,1536]{1,0:T(8,128)(2,1)S(1)}, bf16[320,1536]{1,0:T(8,128)(2,1)S(1)}, u32[]{:S(2)}, u32[]{:S(2)}) collective-permute-start(bf16[320,1536]{1,0:T(8,128)(2,1)S(1)} %stack.7.pair1), channel_id=1, source_target_pairs={{4,0},{17,1},{6,2},{19,3},{8,4},{21,5},{10,6},{23,7},{12,8},{25,9}... | collective-permute-start | bytes 2949128 | tf_op jit(solution)/shard_map/ppermute | solution.py:334
  40.9 23.5 %collective-permute-start.12 = (bf16[320,1536]{1,0:T(8,128)(2,1)S(1)}, bf16[320,1536]{1,0:T(8,128)(2,1)S(1)}, u32[]{:S(2)}, u32[]{:S(2)}) collective-permute-start(bf16[320,1536]{1,0:T(8,128)(2,1)S(1)} %stack.6.pair0), channel_id=1, source_target_pairs={{12,0},{49,1},{14,2},{51,3},{0,4},{53,5},{2,6},{55,7},{4,8},{57,9}... | collective-permute-start | bytes 2949128 | tf_op jit(solution)/shard_map/ppermute | solution.py:334
  44.7 10.4 %collective-permute-start.8 = (bf16[160,1024]{1,0:T(8,128)(2,1)S(1)}, bf16[160,1024]{1,0:T(8,128)(2,1)S(1)}, u32[]{:S(2)}, u32[]{:S(2)}) collective-permute-start(bf16[160,1024]{1,0:T(8,128)(2,1)S(1)} %get-tuple-element.46), channel_id=1, source_target_pairs={{0,2},{1,3},{2,0},{3,1},{4,6},{5,7},{6,4},{7,5},{8,10},{9,11},{10,... | collective-permute-start | bytes 983048 | tf_op jit(solution)/shard_map/ppermute | solution.py:334
  52.4 2.6 %collective-permute-start.9 = (bf16[160,640]{1,0:T(8,128)(2,1)S(1)}, bf16[160,640]{1,0:T(8,128)(2,1)S(1)}, u32[]{:S(2)}, u32[]{:S(2)}) collective-permute-start(bf16[160,640]{1,0:T(8,128)(2,1)S(1)} %get-tuple-element.47), channel_id=1, source_target_pairs={{0,1},{1,0},{2,3},{3,2},{4,5},{5,4},{6,7},{7,6},{8,9},{9,8},{10,11... | collective-permute-start | bytes 614408 | tf_op jit(solution)/shard_map/ppermute | solution.py:334
  55.0 17.9 %collective-permute-start.13 = (bf16[320,1536]{1,0:T(8,128)(2,1)S(1)}, bf16[320,1536]{1,0:T(8,128)(2,1)S(1)}, u32[]{:S(2)}, u32[]{:S(2)}) collective-permute-start(bf16[320,1536]{1,0:T(8,128)(2,1)S(1)} %collective-permute-done.6.first), channel_id=1, source_target_pairs={{4,0},{17,1},{6,2},{19,3},{8,4},{21,5},{10,6},{23,7},{12,8},{25,9}... | collective-permute-start | bytes 2949128 | tf_op jit(solution)/shard_map/ppermute | solution.py:334
  57.1 16.4 %collective-permute-start.14 = (bf16[320,1536]{1,0:T(8,128)(2,1)S(1)}, bf16[320,1536]{1,0:T(8,128)(2,1)S(1)}, u32[]{:S(2)}, u32[]{:S(2)}) collective-permute-start(bf16[320,1536]{1,0:T(8,128)(2,1)S(1)} %collective-permute-done.7.second), channel_id=1, source_target_pairs={{12,0},{49,1},{14,2},{51,3},{0,4},{53,5},{2,6},{55,7},{4,8},{57,9}... | collective-permute-start | bytes 2949128 | tf_op jit(solution)/shard_map/ppermute | solution.py:334
  57.1 10.3 %collective-permute-start.10 = (bf16[160,1280]{1,0:T(8,128)(2,1)S(1)}, bf16[160,1280]{1,0:T(8,128)(2,1)S(1)}, u32[]{:S(2)}, u32[]{:S(2)}) collective-permute-start(bf16[160,1280]{1,0:T(8,128)(2,1)S(1)} %get-tuple-element.50), channel_id=1, source_target_pairs={{0,2},{1,3},{2,0},{3,1},{4,6},{5,7},{6,4},{7,5},{8,10},{9,11},{10,... | collective-permute-start | bytes 1228808 | tf_op jit(solution)/shard_map/ppermute | solution.py:334
  62.4 3.7 %collective-permute-start.16 = (bf16[160,1024]{1,0:T(8,128)(2,1)S(1)}, bf16[160,1024]{1,0:T(8,128)(2,1)S(1)}, u32[]{:S(2)}, u32[]{:S(2)}) collective-permute-start(bf16[160,1024]{1,0:T(8,128)(2,1)S(1)} %collective-permute-done.8.refs_2_.refs_1_), channel_id=1, source_target_pairs={{0,1},{1,0},{2,3},{3,2},{4,5},{5,4},{6,7},{7,6},{8,9},{9,8},{10,11... | collective-permute-start | bytes 983048 | tf_op jit(solution)/shard_map/ppermute | solution.py:334
  64.3 1.7 %collective-permute-start.15 = (bf16[160,640]{1,0:T(8,128)(2,1)S(1)}, bf16[160,640]{1,0:T(8,128)(2,1)S(1)}, u32[]{:S(2)}, u32[]{:S(2)}) collective-permute-start(bf16[160,640]{1,0:T(8,128)(2,1)S(1)} %get-tuple-element.57), channel_id=1, source_target_pairs={{0,1},{1,0},{2,3},{3,2},{4,5},{5,4},{6,7},{7,6},{8,9},{9,8},{10,11... | collective-permute-start | bytes 614408 | tf_op jit(solution)/shard_map/ppermute | solution.py:334
  66.1 10.6 %collective-permute-start.17 = (bf16[160,1280]{1,0:T(8,128)(2,1)S(1)}, bf16[160,1280]{1,0:T(8,128)(2,1)S(1)}, u32[]{:S(2)}, u32[]{:S(2)}) collective-permute-start(bf16[160,1280]{1,0:T(8,128)(2,1)S(1)} %get-tuple-element.58), channel_id=1, source_target_pairs={{0,2},{1,3},{2,0},{3,1},{4,6},{5,7},{6,4},{7,5},{8,10},{9,11},{10,... | collective-permute-start | bytes 1228808 | tf_op jit(solution)/shard_map/ppermute | solution.py:334
  67.4 9.3 %collective-permute-start.19 = (bf16[160,1280]{1,0:T(8,128)(2,1)S(1)}, bf16[160,1280]{1,0:T(8,128)(2,1)S(1)}, u32[]{:S(2)}, u32[]{:S(2)}) collective-permute-start(bf16[160,1280]{1,0:T(8,128)(2,1)S(1)} %collective-permute-done.10.refs_7_.refs_3_), channel_id=1, source_target_pairs={{0,1},{1,0},{2,3},{3,2},{4,5},{5,4},{6,7},{7,6},{8,9},{9,8},{10,11... | collective-permute-start | bytes 1228808 | tf_op jit(solution)/shard_map/ppermute | solution.py:334
  68.9 6.3 %collective-permute-start.18 = (bf16[160,640]{1,0:T(8,128)(2,1)S(1)}, bf16[160,640]{1,0:T(8,128)(2,1)S(1)}, u32[]{:S(2)}, u32[]{:S(2)}) collective-permute-start(bf16[160,640]{1,0:T(8,128)(2,1)S(1)} %get-tuple-element.59), channel_id=1, source_target_pairs={{0,1},{1,0},{2,3},{3,2},{4,5},{5,4},{6,7},{7,6},{8,9},{9,8},{10,11... | collective-permute-start | bytes 614408 | tf_op jit(solution)/shard_map/ppermute | solution.py:334
  76.7 3.2 %collective-permute-start.23 = (bf16[160,1280]{1,0:T(8,128)(2,1)S(1)}, bf16[160,1280]{1,0:T(8,128)(2,1)S(1)}, u32[]{:S(2)}, u32[]{:S(2)}) collective-permute-start(bf16[160,1280]{1,0:T(8,128)(2,1)S(1)} %collective-permute-done.17.refs_11_.refs_5_), channel_id=1, source_target_pairs={{0,1},{1,0},{2,3},{3,2},{4,5},{5,4},{6,7},{7,6},{8,9},{9,8},{10,11... | collective-permute-start | bytes 1228808 | tf_op jit(solution)/shard_map/ppermute | solution.py:334
  78.1 6.7 %collective-permute-start.21 = (bf16[160,640]{1,0:T(8,128)(2,1)S(1)}, bf16[160,640]{1,0:T(8,128)(2,1)S(1)}, u32[]{:S(2)}, u32[]{:S(2)}) collective-permute-start(bf16[160,640]{1,0:T(8,128)(2,1)S(1)} %get-tuple-element.63), channel_id=1, source_target_pairs={{0,2},{1,3},{2,0},{3,1},{4,6},{5,7},{6,4},{7,5},{8,10},{9,11},{10,... | collective-permute-start | bytes 614408 | tf_op jit(solution)/shard_map/ppermute | solution.py:334
  79.3 10.0 %collective-permute-start.22 = (bf16[160,640]{1,0:T(8,128)(2,1)S(1)}, bf16[160,640]{1,0:T(8,128)(2,1)S(1)}, u32[]{:S(2)}, u32[]{:S(2)}) collective-permute-start(bf16[160,640]{1,0:T(8,128)(2,1)S(1)} %get-tuple-element.64), channel_id=1, source_target_pairs={{0,3},{1,2},{2,1},{3,0},{4,7},{5,6},{6,5},{7,4},{8,11},{9,10},{10,... | collective-permute-start | bytes 614408 | tf_op jit(solution)/shard_map/ppermute | solution.py:334
  79.7 9.6 %collective-permute-start.20 = (bf16[160,640]{1,0:T(8,128)(2,1)S(1)}, bf16[160,640]{1,0:T(8,128)(2,1)S(1)}, u32[]{:S(2)}, u32[]{:S(2)}) collective-permute-start(bf16[160,640]{1,0:T(8,128)(2,1)S(1)} %get-tuple-element.62), channel_id=1, source_target_pairs={{0,1},{1,0},{2,3},{3,2},{4,5},{5,4},{6,7},{7,6},{8,9},{9,8},{10,11... | collective-permute-start | bytes 614408 | tf_op jit(solution)/shard_map/ppermute | solution.py:334

commit v5 on v4

--- a/solution.py
+++ b/solution.py
@@ -333,9 +333,9 @@
     def move(value, pairs):
         return lax.ppermute(value, "chan", pairs)
 
-    over, far = move(own, flip(2)), move(own, from_first(2))
-    behind, ahead = move(own, from_first(-1)), move(own, from_first(1))
-    over, far, behind, ahead = hold((over, far, behind, ahead))
+    over, ahead = move(own, flip(2)), move(own, from_first(1))
+    behind, far = move(own, from_first(-1)), move(own, from_first(2))
+    over, ahead, behind, far = hold((over, ahead, behind, far))
     mates = stack(own, over)
     across = move(mates, flip(1))
     pair0, pair1 = stack(own, ahead), stack(behind, far)

time: 90.9 us -> 90 us (0.990)
  waiting for transfers between devices: 39.3 us -> 37.3 us
  starting transfers between devices: 31.2 us -> 32.4 us
    ppermute x23, waiting for transfers between devices: 34.1 us -> 32 us  [move(): return lax.ppermute(value, 'chan', pairs)]
    ppermute x23, starting transfers between devices: 27.5 us -> 28.8 us  [move(): return lax.ppermute(value, 'chan', pairs)]
  transfers between devices with their start and end apart: 24 -> 24, of which waited for: 10 -> 12; matrix products, arithmetic and copies ran while one was open for 0% -> 0% of each run, Pallas kernels for 12% -> 12%
where the time goes in v5:
time: 90 us; the launch traced here: 89.9 us
  waiting for transfers between devices  37.3 us (41%)
  starting transfers between devices  32.4 us (36%)
  Pallas kernels  19.2 us (21%)
    ppermute x23, waiting for transfers between devices, move(): return lax.ppermute(value, 'chan', pairs)  32 us
    ppermute x23, starting transfers between devices, move(): return lax.ppermute(value, 'chan', pairs)  28.8 us
    pallas_call x1, Pallas kernels, whiten(): pl.pallas_call(whiten_kernel, in_specs=[pl.BlockSpec(memory_space=pltpu.S...  6.49 us
    ppermute x1, waiting for transfers between devices, local(): got = lax.ppermute(send, 'band', [(0, 1), (1, 0)])  5.2 us
    pallas_call x3, Pallas kernels, cross(): pl.pallas_call(cross_kernel, out_shape=[mine, narrow, wide] if merged els...  5.13 us
    pallas_call x3, Pallas kernels, place(): pl.pallas_call(lambda *refs: place_kernel(blocks, kinds, *refs), in_specs...  4.69 us
    ppermute x1, starting transfers between devices, local(): got = lax.ppermute(send, 'band', [(0, 1), (1, 0)])  3.65 us
    pallas_call x1, Pallas kernels, first_cross(): pl.pallas_call(first_cross_kernel, out_shape=[wide, jax.ShapeDtypeStruct(...  2.28 us
  transfers between devices with their start and end apart: 24, of which 12 were waited for; matrix products, arithmetic and copies ran while one was open for 0% of the time, Pallas kernels for 12%

profile of v5, /device:TPU:1, one launch (start us, length us, event | category | flops | bytes accessed | tf_op | source)
XLA Modules:
  0.0 89.9 jit_solution(3184745883830305597)
XLA Ops:
  0.7 6.5 %whiten.1 = (bf16[960,128]{1,0:T(8,128)(2,1)S(1)}, bf16[960,128]{1,0:T(8,128)(2,1)S(1)}) custom-call(s32[4]{0:T(128)S(1)} %pad_add_fusion.bands, bf16[960,4096]{1,0:T(8,128)(2,1)} %bitcast.4), custom_call_target="tpu_custom_call" | custom-call | tf_op jit(solution)/shard_map/whiten/pallas_call | solution.py:93
  7.2 3.7 %collective-permute-start = (bf16[960,128]{1,0:T(8,128)(2,1)S(1)}, bf16[960,128]{1,0:T(8,128)(2,1)S(1)}, u32[]{:S(2)}, u32[]{:S(2)}) collective-permute-start(bf16[960,128]{1,0:T(8,128)(2,1)S(1)} %get-tuple-element.39), channel_id=1, source_target_pairs={{0,64},{64,0},{1,65},{65,1},{2,66},{66,2},{3,67},{67,3},{4,68},{68... | collective-permute-start | bytes 737288 | tf_op jit(solution)/shard_map/ppermute | solution.py:329
  10.9 5.2 %collective-permute-done.got_ref = bf16[960,128]{1,0:T(8,128)(2,1)S(1)} collective-permute-done((bf16[960,128]{1,0:T(8,128)(2,1)S(1)}, bf16[960,128]{1,0:T(8,128)(2,1)S(1)}, u32[]{:S(2)}, u32[]{:S(2)}) %collective-permute-start) | collective-permute-done | bytes 245792 | tf_op jit(solution)/shard_map/ppermute | solution.py:329
  16.3 3.4 %collective-permute-start.4 = (bf16[160,1536]{1,0:T(8,128)(2,1)S(1)}, bf16[160,1536]{1,0:T(8,128)(2,1)S(1)}, u32[]{:S(2)}, u32[]{:S(2)}) collective-permute-start(bf16[160,1536]{1,0:T(8,128)(2,1)S(1)} %normalize.1.refs_0_), channel_id=1, source_target_pairs={{32,0},{9,1},{34,2},{11,3},{36,4},{13,5},{38,6},{15,7},{40,8},{1,9... | collective-permute-start | bytes 1474568 | tf_op jit(solution)/shard_map/ppermute | solution.py:334
  20.1 2.3 %collective-permute-start.2 = (bf16[160,1536]{1,0:T(8,128)(2,1)S(1)}, bf16[160,1536]{1,0:T(8,128)(2,1)S(1)}, u32[]{:S(2)}, u32[]{:S(2)}) collective-permute-start(bf16[160,1536]{1,0:T(8,128)(2,1)S(1)} %normalize.1.refs_0_), channel_id=1, source_target_pairs={{16,0},{5,1},{18,2},{7,3},{20,4},{9,5},{22,6},{11,7},{24,8},{13,9}... | collective-permute-start | bytes 1474568 | tf_op jit(solution)/shard_map/ppermute | solution.py:334
  22.4 1.2 %collective-permute-start.1 = (bf16[160,1536]{1,0:T(8,128)(2,1)S(1)}, bf16[160,1536]{1,0:T(8,128)(2,1)S(1)}, u32[]{:S(2)}, u32[]{:S(2)}) collective-permute-start(bf16[160,1536]{1,0:T(8,128)(2,1)S(1)} %normalize.1.refs_0_), channel_id=1, source_target_pairs={{0,2},{1,3},{2,0},{3,1},{4,6},{5,7},{6,4},{7,5},{8,10},{9,11},{10,... | collective-permute-start | bytes 1474568 | tf_op jit(solution)/shard_map/ppermute | solution.py:334
  23.6 2.7 %collective-permute-done.4.refs_1_ = bf16[160,1536]{1,0:T(8,128)(2,1)S(1)} collective-permute-done((bf16[160,1536]{1,0:T(8,128)(2,1)S(1)}, bf16[160,1536]{1,0:T(8,128)(2,1)S(1)}, u32[]{:S(2)}, u32[]{:S(2)}) %collective-permute-start.4) | collective-permute-done | bytes 491552 | tf_op jit(solution)/shard_map/ppermute | solution.py:334
  26.3 5.2 %collective-permute-done.3.refs_0_ = bf16[160,1536]{1,0:T(8,128)(2,1)S(1)} collective-permute-done((bf16[160,1536]{1,0:T(8,128)(2,1)S(1)}, bf16[160,1536]{1,0:T(8,128)(2,1)S(1)}, u32[]{:S(2)}, u32[]{:S(2)}) %collective-permute-start.3) | collective-permute-done | bytes 491552 | tf_op jit(solution)/shard_map/ppermute | solution.py:334
  32.1 4.1 %collective-permute-start.5 = (bf16[320,1536]{1,0:T(8,128)(2,1)S(1)}, bf16[320,1536]{1,0:T(8,128)(2,1)S(1)}, u32[]{:S(2)}, u32[]{:S(2)}) collective-permute-start(bf16[320,1536]{1,0:T(8,128)(2,1)S(1)} %stack.4.refs_0_), channel_id=1, source_target_pairs={{0,1},{1,0},{2,3},{3,2},{4,5},{5,4},{6,7},{7,6},{8,9},{9,8},{10,11... | collective-permute-start | bytes 2949128 | tf_op jit(solution)/shard_map/ppermute | solution.py:334
  36.3 1.7 %collective-permute-start.7 = (bf16[320,1536]{1,0:T(8,128)(2,1)S(1)}, bf16[320,1536]{1,0:T(8,128)(2,1)S(1)}, u32[]{:S(2)}, u32[]{:S(2)}) collective-permute-start(bf16[320,1536]{1,0:T(8,128)(2,1)S(1)} %stack.7.pair1), channel_id=1, source_target_pairs={{12,0},{49,1},{14,2},{51,3},{0,4},{53,5},{2,6},{55,7},{4,8},{57,9}... | collective-permute-start | bytes 2949128 | tf_op jit(solution)/shard_map/ppermute | solution.py:334
  38.0 1.3 %collective-permute-start.6 = (bf16[320,1536]{1,0:T(8,128)(2,1)S(1)}, bf16[320,1536]{1,0:T(8,128)(2,1)S(1)}, u32[]{:S(2)}, u32[]{:S(2)}) collective-permute-start(bf16[320,1536]{1,0:T(8,128)(2,1)S(1)} %stack.6.pair0), channel_id=1, source_target_pairs={{4,0},{17,1},{6,2},{19,3},{8,4},{21,5},{10,6},{23,7},{12,8},{25,9}... | collective-permute-start | bytes 2949128 | tf_op jit(solution)/shard_map/ppermute | solution.py:334
  39.3 1.4 %collective-permute-start.11 = (bf16[320,1536]{1,0:T(8,128)(2,1)S(1)}, bf16[320,1536]{1,0:T(8,128)(2,1)S(1)}, u32[]{:S(2)}, u32[]{:S(2)}) collective-permute-start(bf16[320,1536]{1,0:T(8,128)(2,1)S(1)} %stack.7.pair1), channel_id=1, source_target_pairs={{4,0},{17,1},{6,2},{19,3},{8,4},{21,5},{10,6},{23,7},{12,8},{25,9}... | collective-permute-start | bytes 2949128 | tf_op jit(solution)/shard_map/ppermute | solution.py:334
  40.9 2.3 %cross.4 = (f32[160,640]{1,0:T(8,128)S(1)}, bf16[160,640]{1,0:T(8,128)(2,1)S(1)}, bf16[160,1024]{1,0:T(8,128)(2,1)S(1)}, f32[160,640]{1,0:T(8,128)S(1)}) custom-call(bf16[640,1536]{1,0:T(8,128)(2,1)S(1)} %stack.5.rows, bf16[320,1536]{1,0:T(8,128)(2,1)S(1)} %stack.6.pair0, bf16[320,1536]{1,0:T(8,128)(2,1)S(1)} %stack.7.pair1), custom_call_target="tpu_custom_call" | custom-call | flops 1258291200 | bytes 12582912 | tf_op jit(solution)/shard_map/cross/pallas_call | solution.py:208
  43.2 1.3 %collective-permute-start.8 = (bf16[160,1024]{1,0:T(8,128)(2,1)S(1)}, bf16[160,1024]{1,0:T(8,128)(2,1)S(1)}, u32[]{:S(2)}, u32[]{:S(2)}) collective-permute-start(bf16[160,1024]{1,0:T(8,128)(2,1)S(1)} %get-tuple-element.46), channel_id=1, source_target_pairs={{0,2},{1,3},{2,0},{3,1},{4,6},{5,7},{6,4},{7,5},{8,10},{9,11},{10,... | collective-permute-start | bytes 983048 | tf_op jit(solution)/shard_map/ppermute | solution.py:334
  44.5 6.4 %collective-permute-done.7.second = bf16[320,1536]{1,0:T(8,128)(2,1)S(1)} collective-permute-done((bf16[320,1536]{1,0:T(8,128)(2,1)S(1)}, bf16[320,1536]{1,0:T(8,128)(2,1)S(1)}, u32[]{:S(2)}, u32[]{:S(2)}) %collective-permute-start.7) | collective-permute-done | bytes 983072 | tf_op jit(solution)/shard_map/ppermute | solution.py:334
  51.7 1.7 %cross.5 = (f32[160,640]{1,0:T(8,128)S(1)}, bf16[160,640]{1,0:T(8,128)(2,1)S(1)}, bf16[160,1280]{1,0:T(8,128)(2,1)S(1)}) custom-call(bf16[640,1536]{1,0:T(8,128)(2,1)S(1)} %stack.5.rows, bf16[320,1536]{1,0:T(8,128)(2,1)S(1)} %collective-permute-done.6.first, bf16[320,1536]{1,0:T(8,128)(2,1)S(1)} %collective-permute-done.7.second), custom_call_target="tpu_custom_call" | custom-call | flops 1258291200 | bytes 12582912 | tf_op jit(solution)/shard_map/cross/pallas_call | solution.py:175
  53.4 3.1 %collective-permute-start.13 = (bf16[320,1536]{1,0:T(8,128)(2,1)S(1)}, bf16[320,1536]{1,0:T(8,128)(2,1)S(1)}, u32[]{:S(2)}, u32[]{:S(2)}) collective-permute-start(bf16[320,1536]{1,0:T(8,128)(2,1)S(1)} %collective-permute-done.6.first), channel_id=1, source_target_pairs={{4,0},{17,1},{6,2},{19,3},{8,4},{21,5},{10,6},{23,7},{12,8},{25,9}... | collective-permute-start | bytes 2949128 | tf_op jit(solution)/shard_map/ppermute | solution.py:334
  56.5 1.2 %collective-permute-start.10 = (bf16[160,1280]{1,0:T(8,128)(2,1)S(1)}, bf16[160,1280]{1,0:T(8,128)(2,1)S(1)}, u32[]{:S(2)}, u32[]{:S(2)}) collective-permute-start(bf16[160,1280]{1,0:T(8,128)(2,1)S(1)} %get-tuple-element.50), channel_id=1, source_target_pairs={{0,2},{1,3},{2,0},{3,1},{4,6},{5,7},{6,4},{7,5},{8,10},{9,11},{10,... | collective-permute-start | bytes 1228808 | tf_op jit(solution)/shard_map/ppermute | solution.py:334
  57.7 4.1 %collective-permute-done.11.first = bf16[320,1536]{1,0:T(8,128)(2,1)S(1)} collective-permute-done((bf16[320,1536]{1,0:T(8,128)(2,1)S(1)}, bf16[320,1536]{1,0:T(8,128)(2,1)S(1)}, u32[]{:S(2)}, u32[]{:S(2)}) %collective-permute-start.11) | collective-permute-done | bytes 983072 | tf_op jit(solution)/shard_map/ppermute | solution.py:334
  62.4 1.7 %cross.6 = (f32[160,640]{1,0:T(8,128)S(1)}, bf16[160,640]{1,0:T(8,128)(2,1)S(1)}, bf16[160,1280]{1,0:T(8,128)(2,1)S(1)}) custom-call(bf16[640,1536]{1,0:T(8,128)(2,1)S(1)} %stack.5.rows, bf16[320,1536]{1,0:T(8,128)(2,1)S(1)} %collective-permute-done.11.first, bf16[320,1536]{1,0:T(8,128)(2,1)S(1)} %collective-permute-done.12.second), custom_call_target="tpu_custom_call" | custom-call | flops 1258291200 | bytes 12582912 | tf_op jit(solution)/shard_map/cross/pallas_call | solution.py:175
  64.1 1.3 %collective-permute-start.17 = (bf16[160,1280]{1,0:T(8,128)(2,1)S(1)}, bf16[160,1280]{1,0:T(8,128)(2,1)S(1)}, u32[]{:S(2)}, u32[]{:S(2)}) collective-permute-start(bf16[160,1280]{1,0:T(8,128)(2,1)S(1)} %get-tuple-element.58), channel_id=1, source_target_pairs={{0,2},{1,3},{2,0},{3,1},{4,6},{5,7},{6,4},{7,5},{8,10},{9,11},{10,... | collective-permute-start | bytes 1228808 | tf_op jit(solution)/shard_map/ppermute | solution.py:334
  65.4 1.9 %collective-permute-done.10.refs_7_.refs_3_ = bf16[160,1280]{1,0:T(8,128)(2,1)S(1)} collective-permute-done((bf16[160,1280]{1,0:T(8,128)(2,1)S(1)}, bf16[160,1280]{1,0:T(8,128)(2,1)S(1)}, u32[]{:S(2)}, u32[]{:S(2)}) %collective-permute-start.10) | collective-permute-done | bytes 409632 | tf_op jit(solution)/shard_map/ppermute | solution.py:334
  67.3 1.9 %collective-permute-start.19 = (bf16[160,1280]{1,0:T(8,128)(2,1)S(1)}, bf16[160,1280]{1,0:T(8,128)(2,1)S(1)}, u32[]{:S(2)}, u32[]{:S(2)}) collective-permute-start(bf16[160,1280]{1,0:T(8,128)(2,1)S(1)} %collective-permute-done.10.refs_7_.refs_3_), channel_id=1, source_target_pairs={{0,1},{1,0},{2,3},{3,2},{4,5},{5,4},{6,7},{7,6},{8,9},{9,8},{10,11... | collective-permute-start | bytes 1228808 | tf_op jit(solution)/shard_map/ppermute | solution.py:334
  69.1 3.3 %collective-permute-done.13.first = bf16[320,1536]{1,0:T(8,128)(2,1)S(1)} collective-permute-done((bf16[320,1536]{1,0:T(8,128)(2,1)S(1)}, bf16[320,1536]{1,0:T(8,128)(2,1)S(1)}, u32[]{:S(2)}, u32[]{:S(2)}) %collective-permute-start.13) | collective-permute-done | bytes 983072 | tf_op jit(solution)/shard_map/ppermute | solution.py:334
  72.4 1.7 %cross.7 = (f32[160,640]{1,0:T(8,128)S(1)}, bf16[160,640]{1,0:T(8,128)(2,1)S(1)}, bf16[160,640]{1,0:T(8,128)(2,1)S(1)}, bf16[160,640]{1,0:T(8,128)(2,1)S(1)}) custom-call(bf16[640,1536]{1,0:T(8,128)(2,1)S(1)} %stack.5.rows, bf16[320,1536]{1,0:T(8,128)(2,1)S(1)} %collective-permute-done.13.first, bf16[320,1536]{1,0:T(8,128)(2,1)S(1)} %collective-permute-done.14.second), custom_call_target="tpu_custom_call" | custom-call | flops 1258291200 | bytes 12582912 | tf_op jit(solution)/shard_map/cross/pallas_call | solution.py:175
  74.1 1.9 %collective-permute-done.17.refs_11_.refs_5_ = bf16[160,1280]{1,0:T(8,128)(2,1)S(1)} collective-permute-done((bf16[160,1280]{1,0:T(8,128)(2,1)S(1)}, bf16[160,1280]{1,0:T(8,128)(2,1)S(1)}, u32[]{:S(2)}, u32[]{:S(2)}) %collective-permute-start.17) | collective-permute-done | bytes 409632 | tf_op jit(solution)/shard_map/ppermute | solution.py:334
  77.2 1.2 %collective-permute-start.21 = (bf16[160,640]{1,0:T(8,128)(2,1)S(1)}, bf16[160,640]{1,0:T(8,128)(2,1)S(1)}, u32[]{:S(2)}, u32[]{:S(2)}) collective-permute-start(bf16[160,640]{1,0:T(8,128)(2,1)S(1)} %get-tuple-element.63), channel_id=1, source_target_pairs={{0,2},{1,3},{2,0},{3,1},{4,6},{5,7},{6,4},{7,5},{8,10},{9,11},{10,... | collective-permute-start | bytes 614408 | tf_op jit(solution)/shard_map/ppermute | solution.py:334
  79.1 2.1 %place.3.refs_8_ = f32[160,10240]{1,0:T(8,128)} custom-call(f32[160,640]{1,0:T(8,128)S(1)} %get-tuple-element.44.refs_0_, bf16[160,640]{1,0:T(8,128)(2,1)S(1)} %collective-permute-done.9.refs_1_.refs_0_, bf16[160,1024]{1,0:T(8,128)(2,1)S(1)} %collective-permute-done.8.refs_2_.refs_1_, bf16[160,1024]{1,0:T(8,128)(2,1)S(1)} %collective-permute-done.16.refs_3_.refs_1_, ...), custom_call_target="tpu_custom_call" | custom-call | tf_op jit(solution)/shard_map/place/pallas_call | solution.py:281
  81.2 2.7 %collective-permute-done.21.refs_7_.refs_8_ = bf16[160,640]{1,0:T(8,128)(2,1)S(1)} collective-permute-done((bf16[160,640]{1,0:T(8,128)(2,1)S(1)}, bf16[160,640]{1,0:T(8,128)(2,1)S(1)}, u32[]{:S(2)}, u32[]{:S(2)}) %collective-permute-start.21) | collective-permute-done | bytes 204832 | tf_op jit(solution)/shard_map/ppermute | solution.py:334
  83.9 1.2 %place.4.refs_10_ = f32[160,10240]{1,0:T(8,128)} custom-call(bf16[160,640]{1,0:T(8,128)(2,1)S(1)} %collective-permute-done.9.refs_1_.refs_0_, bf16[160,1024]{1,0:T(8,128)(2,1)S(1)} %collective-permute-done.16.refs_3_.refs_1_, bf16[160,640]{1,0:T(8,128)(2,1)S(1)} %collective-permute-done.15.refs_6_.refs_2_, ...), custom_call_target="tpu_custom_call", output_to_operand_aliasing={{}: (8, {})} | custom-call | tf_op jit(solution)/shard_map/place/pallas_call | solution.py:281
  85.1 3.3 %collective-permute-done.22.refs_9_ = bf16[160,640]{1,0:T(8,128)(2,1)S(1)} collective-permute-done((bf16[160,640]{1,0:T(8,128)(2,1)S(1)}, bf16[160,640]{1,0:T(8,128)(2,1)S(1)}, u32[]{:S(2)}, u32[]{:S(2)}) %collective-permute-start.22) | collective-permute-done | bytes 204832 | tf_op jit(solution)/shard_map/ppermute | solution.py:334
  88.4 1.3 %place.5 = f32[160,10240]{1,0:T(8,128)} custom-call(f32[160,640]{1,0:T(8,128)S(1)} %get-tuple-element.44.refs_0_, bf16[160,1024]{1,0:T(8,128)(2,1)S(1)} %collective-permute-done.8.refs_2_.refs_1_, f32[160,640]{1,0:T(8,128)S(1)} %get-tuple-element.49.refs_5_.refs_2_, ...), custom_call_target="tpu_custom_call", output_to_operand_aliasing={{}: (10, {})} | custom-call | tf_op jit(solution)/shard_map/place/pallas_call | solution.py:281
  (30 shorter events, 5.3 us)
Async XLA Ops:
  7.2 8.9 %collective-permute-start = (bf16[960,128]{1,0:T(8,128)(2,1)S(1)}, bf16[960,128]{1,0:T(8,128)(2,1)S(1)}, u32[]{:S(2)}, u32[]{:S(2)}) collective-permute-start(bf16[960,128]{1,0:T(8,128)(2,1)S(1)} %get-tuple-element.39), channel_id=1, source_target_pairs={{0,64},{64,0},{1,65},{65,1},{2,66},{66,2},{3,67},{67,3},{4,68},{68... | collective-permute-start | bytes 737288 | tf_op jit(solution)/shard_map/ppermute | solution.py:329
  16.3 9.9 %collective-permute-start.4 = (bf16[160,1536]{1,0:T(8,128)(2,1)S(1)}, bf16[160,1536]{1,0:T(8,128)(2,1)S(1)}, u32[]{:S(2)}, u32[]{:S(2)}) collective-permute-start(bf16[160,1536]{1,0:T(8,128)(2,1)S(1)} %normalize.1.refs_0_), channel_id=1, source_target_pairs={{32,0},{9,1},{34,2},{11,3},{36,4},{13,5},{38,6},{15,7},{40,8},{1,9... | collective-permute-start | bytes 1474568 | tf_op jit(solution)/shard_map/ppermute | solution.py:334
  19.7 11.8 %collective-permute-start.3 = (bf16[160,1536]{1,0:T(8,128)(2,1)S(1)}, bf16[160,1536]{1,0:T(8,128)(2,1)S(1)}, u32[]{:S(2)}, u32[]{:S(2)}) collective-permute-start(bf16[160,1536]{1,0:T(8,128)(2,1)S(1)} %normalize.1.refs_0_), channel_id=1, source_target_pairs={{48,0},{13,1},{50,2},{15,3},{52,4},{1,5},{54,6},{3,7},{56,8},{5,9}... | collective-permute-start | bytes 1474568 | tf_op jit(solution)/shard_map/ppermute | solution.py:334
  20.1 11.8 %collective-permute-start.2 = (bf16[160,1536]{1,0:T(8,128)(2,1)S(1)}, bf16[160,1536]{1,0:T(8,128)(2,1)S(1)}, u32[]{:S(2)}, u32[]{:S(2)}) collective-permute-start(bf16[160,1536]{1,0:T(8,128)(2,1)S(1)} %normalize.1.refs_0_), channel_id=1, source_target_pairs={{16,0},{5,1},{18,2},{7,3},{20,4},{9,5},{22,6},{11,7},{24,8},{13,9}... | collective-permute-start | bytes 1474568 | tf_op jit(solution)/shard_map/ppermute | solution.py:334
  22.4 9.6 %collective-permute-start.1 = (bf16[160,1536]{1,0:T(8,128)(2,1)S(1)}, bf16[160,1536]{1,0:T(8,128)(2,1)S(1)}, u32[]{:S(2)}, u32[]{:S(2)}) collective-permute-start(bf16[160,1536]{1,0:T(8,128)(2,1)S(1)} %normalize.1.refs_0_), channel_id=1, source_target_pairs={{0,2},{1,3},{2,0},{3,1},{4,6},{5,7},{6,4},{7,5},{8,10},{9,11},{10,... | collective-permute-start | bytes 1474568 | tf_op jit(solution)/shard_map/ppermute | solution.py:334
  32.1 8.6 %collective-permute-start.5 = (bf16[320,1536]{1,0:T(8,128)(2,1)S(1)}, bf16[320,1536]{1,0:T(8,128)(2,1)S(1)}, u32[]{:S(2)}, u32[]{:S(2)}) collective-permute-start(bf16[320,1536]{1,0:T(8,128)(2,1)S(1)} %stack.4.refs_0_), channel_id=1, source_target_pairs={{0,1},{1,0},{2,3},{3,2},{4,5},{5,4},{6,7},{7,6},{8,9},{9,8},{10,11... | collective-permute-start | bytes 2949128 | tf_op jit(solution)/shard_map/ppermute | solution.py:334
  36.3 14.7 %collective-permute-start.7 = (bf16[320,1536]{1,0:T(8,128)(2,1)S(1)}, bf16[320,1536]{1,0:T(8,128)(2,1)S(1)}, u32[]{:S(2)}, u32[]{:S(2)}) collective-permute-start(bf16[320,1536]{1,0:T(8,128)(2,1)S(1)} %stack.7.pair1), channel_id=1, source_target_pairs={{12,0},{49,1},{14,2},{51,3},{0,4},{53,5},{2,6},{55,7},{4,8},{57,9}... | collective-permute-start | bytes 2949128 | tf_op jit(solution)/shard_map/ppermute | solution.py:334
  38.0 13.6 %collective-permute-start.6 = (bf16[320,1536]{1,0:T(8,128)(2,1)S(1)}, bf16[320,1536]{1,0:T(8,128)(2,1)S(1)}, u32[]{:S(2)}, u32[]{:S(2)}) collective-permute-start(bf16[320,1536]{1,0:T(8,128)(2,1)S(1)} %stack.6.pair0), channel_id=1, source_target_pairs={{4,0},{17,1},{6,2},{19,3},{8,4},{21,5},{10,6},{23,7},{12,8},{25,9}... | collective-permute-start | bytes 2949128 | tf_op jit(solution)/shard_map/ppermute | solution.py:334
  39.3 22.6 %collective-permute-start.11 = (bf16[320,1536]{1,0:T(8,128)(2,1)S(1)}, bf16[320,1536]{1,0:T(8,128)(2,1)S(1)}, u32[]{:S(2)}, u32[]{:S(2)}) collective-permute-start(bf16[320,1536]{1,0:T(8,128)(2,1)S(1)} %stack.7.pair1), channel_id=1, source_target_pairs={{4,0},{17,1},{6,2},{19,3},{8,4},{21,5},{10,6},{23,7},{12,8},{25,9}... | collective-permute-start | bytes 2949128 | tf_op jit(solution)/shard_map/ppermute | solution.py:334
  40.7 21.3 %collective-permute-start.12 = (bf16[320,1536]{1,0:T(8,128)(2,1)S(1)}, bf16[320,1536]{1,0:T(8,128)(2,1)S(1)}, u32[]{:S(2)}, u32[]{:S(2)}) collective-permute-start(bf16[320,1536]{1,0:T(8,128)(2,1)S(1)} %stack.6.pair0), channel_id=1, source_target_pairs={{12,0},{49,1},{14,2},{51,3},{0,4},{53,5},{2,6},{55,7},{4,8},{57,9}... | collective-permute-start | bytes 2949128 | tf_op jit(solution)/shard_map/ppermute | solution.py:334
  43.2 10.2 %collective-permute-start.8 = (bf16[160,1024]{1,0:T(8,128)(2,1)S(1)}, bf16[160,1024]{1,0:T(8,128)(2,1)S(1)}, u32[]{:S(2)}, u32[]{:S(2)}) collective-permute-start(bf16[160,1024]{1,0:T(8,128)(2,1)S(1)} %get-tuple-element.46), channel_id=1, source_target_pairs={{0,2},{1,3},{2,0},{3,1},{4,6},{5,7},{6,4},{7,5},{8,10},{9,11},{10,... | collective-permute-start | bytes 983048 | tf_op jit(solution)/shard_map/ppermute | solution.py:334
  50.9 2.5 %collective-permute-start.9 = (bf16[160,640]{1,0:T(8,128)(2,1)S(1)}, bf16[160,640]{1,0:T(8,128)(2,1)S(1)}, u32[]{:S(2)}, u32[]{:S(2)}) collective-permute-start(bf16[160,640]{1,0:T(8,128)(2,1)S(1)} %get-tuple-element.47), channel_id=1, source_target_pairs={{0,1},{1,0},{2,3},{3,2},{4,5},{5,4},{6,7},{7,6},{8,9},{9,8},{10,11... | collective-permute-start | bytes 614408 | tf_op jit(solution)/shard_map/ppermute | solution.py:334
  53.4 19.0 %collective-permute-start.13 = (bf16[320,1536]{1,0:T(8,128)(2,1)S(1)}, bf16[320,1536]{1,0:T(8,128)(2,1)S(1)}, u32[]{:S(2)}, u32[]{:S(2)}) collective-permute-start(bf16[320,1536]{1,0:T(8,128)(2,1)S(1)} %collective-permute-done.6.first), channel_id=1, source_target_pairs={{4,0},{17,1},{6,2},{19,3},{8,4},{21,5},{10,6},{23,7},{12,8},{25,9}... | collective-permute-start | bytes 2949128 | tf_op jit(solution)/shard_map/ppermute | solution.py:334
  56.5 15.9 %collective-permute-start.14 = (bf16[320,1536]{1,0:T(8,128)(2,1)S(1)}, bf16[320,1536]{1,0:T(8,128)(2,1)S(1)}, u32[]{:S(2)}, u32[]{:S(2)}) collective-permute-start(bf16[320,1536]{1,0:T(8,128)(2,1)S(1)} %collective-permute-done.7.second), channel_id=1, source_target_pairs={{12,0},{49,1},{14,2},{51,3},{0,4},{53,5},{2,6},{55,7},{4,8},{57,9}... | collective-permute-start | bytes 2949128 | tf_op jit(solution)/shard_map/ppermute | solution.py:334
  56.5 10.8 %collective-permute-start.10 = (bf16[160,1280]{1,0:T(8,128)(2,1)S(1)}, bf16[160,1280]{1,0:T(8,128)(2,1)S(1)}, u32[]{:S(2)}, u32[]{:S(2)}) collective-permute-start(bf16[160,1280]{1,0:T(8,128)(2,1)S(1)} %get-tuple-element.50), channel_id=1, source_target_pairs={{0,2},{1,3},{2,0},{3,1},{4,6},{5,7},{6,4},{7,5},{8,10},{9,11},{10,... | collective-permute-start | bytes 1228808 | tf_op jit(solution)/shard_map/ppermute | solution.py:334
  61.9 2.2 %collective-permute-start.16 = (bf16[160,1024]{1,0:T(8,128)(2,1)S(1)}, bf16[160,1024]{1,0:T(8,128)(2,1)S(1)}, u32[]{:S(2)}, u32[]{:S(2)}) collective-permute-start(bf16[160,1024]{1,0:T(8,128)(2,1)S(1)} %collective-permute-done.8.refs_2_.refs_1_), channel_id=1, source_target_pairs={{0,1},{1,0},{2,3},{3,2},{4,5},{5,4},{6,7},{7,6},{8,9},{9,8},{10,11... | collective-permute-start | bytes 983048 | tf_op jit(solution)/shard_map/ppermute | solution.py:334
  62.0 2.1 %collective-permute-start.15 = (bf16[160,640]{1,0:T(8,128)(2,1)S(1)}, bf16[160,640]{1,0:T(8,128)(2,1)S(1)}, u32[]{:S(2)}, u32[]{:S(2)}) collective-permute-start(bf16[160,640]{1,0:T(8,128)(2,1)S(1)} %get-tuple-element.57), channel_id=1, source_target_pairs={{0,1},{1,0},{2,3},{3,2},{4,5},{5,4},{6,7},{7,6},{8,9},{9,8},{10,11... | collective-permute-start | bytes 614408 | tf_op jit(solution)/shard_map/ppermute | solution.py:334
  64.1 11.9 %collective-permute-start.17 = (bf16[160,1280]{1,0:T(8,128)(2,1)S(1)}, bf16[160,1280]{1,0:T(8,128)(2,1)S(1)}, u32[]{:S(2)}, u32[]{:S(2)}) collective-permute-start(bf16[160,1280]{1,0:T(8,128)(2,1)S(1)} %get-tuple-element.58), channel_id=1, source_target_pairs={{0,2},{1,3},{2,0},{3,1},{4,6},{5,7},{6,4},{7,5},{8,10},{9,11},{10,... | collective-permute-start | bytes 1228808 | tf_op jit(solution)/shard_map/ppermute | solution.py:334
  67.3 8.8 %collective-permute-start.19 = (bf16[160,1280]{1,0:T(8,128)(2,1)S(1)}, bf16[160,1280]{1,0:T(8,128)(2,1)S(1)}, u32[]{:S(2)}, u32[]{:S(2)}) collective-permute-start(bf16[160,1280]{1,0:T(8,128)(2,1)S(1)} %collective-permute-done.10.refs_7_.refs_3_), channel_id=1, source_target_pairs={{0,1},{1,0},{2,3},{3,2},{4,5},{5,4},{6,7},{7,6},{8,9},{9,8},{10,11... | collective-permute-start | bytes 1228808 | tf_op jit(solution)/shard_map/ppermute | solution.py:334
  69.1 5.0 %collective-permute-start.18 = (bf16[160,640]{1,0:T(8,128)(2,1)S(1)}, bf16[160,640]{1,0:T(8,128)(2,1)S(1)}, u32[]{:S(2)}, u32[]{:S(2)}) collective-permute-start(bf16[160,640]{1,0:T(8,128)(2,1)S(1)} %get-tuple-element.59), channel_id=1, source_target_pairs={{0,1},{1,0},{2,3},{3,2},{4,5},{5,4},{6,7},{7,6},{8,9},{9,8},{10,11... | collective-permute-start | bytes 614408 | tf_op jit(solution)/shard_map/ppermute | solution.py:334
  76.1 3.0 %collective-permute-start.23 = (bf16[160,1280]{1,0:T(8,128)(2,1)S(1)}, bf16[160,1280]{1,0:T(8,128)(2,1)S(1)}, u32[]{:S(2)}, u32[]{:S(2)}) collective-permute-start(bf16[160,1280]{1,0:T(8,128)(2,1)S(1)} %collective-permute-done.17.refs_11_.refs_5_), channel_id=1, source_target_pairs={{0,1},{1,0},{2,3},{3,2},{4,5},{5,4},{6,7},{7,6},{8,9},{9,8},{10,11... | collective-permute-start | bytes 1228808 | tf_op jit(solution)/shard_map/ppermute | solution.py:334
  77.2 6.7 %collective-permute-start.21 = (bf16[160,640]{1,0:T(8,128)(2,1)S(1)}, bf16[160,640]{1,0:T(8,128)(2,1)S(1)}, u32[]{:S(2)}, u32[]{:S(2)}) collective-permute-start(bf16[160,640]{1,0:T(8,128)(2,1)S(1)} %get-tuple-element.63), channel_id=1, source_target_pairs={{0,2},{1,3},{2,0},{3,1},{4,6},{5,7},{6,4},{7,5},{8,10},{9,11},{10,... | collective-permute-start | bytes 614408 | tf_op jit(solution)/shard_map/ppermute | solution.py:334
  78.4 10.0 %collective-permute-start.22 = (bf16[160,640]{1,0:T(8,128)(2,1)S(1)}, bf16[160,640]{1,0:T(8,128)(2,1)S(1)}, u32[]{:S(2)}, u32[]{:S(2)}) collective-permute-start(bf16[160,640]{1,0:T(8,128)(2,1)S(1)} %get-tuple-element.64), channel_id=1, source_target_pairs={{0,3},{1,2},{2,1},{3,0},{4,7},{5,6},{6,5},{7,4},{8,11},{9,10},{10,... | collective-permute-start | bytes 614408 | tf_op jit(solution)/shard_map/ppermute | solution.py:334
  78.8 9.6 %collective-permute-start.20 = (bf16[160,640]{1,0:T(8,128)(2,1)S(1)}, bf16[160,640]{1,0:T(8,128)(2,1)S(1)}, u32[]{:S(2)}, u32[]{:S(2)}) collective-permute-start(bf16[160,640]{1,0:T(8,128)(2,1)S(1)} %get-tuple-element.62), channel_id=1, source_target_pairs={{0,1},{1,0},{2,3},{3,2},{4,5},{5,4},{6,7},{7,6},{8,9},{9,8},{10,11... | collective-permute-start | bytes 614408 | tf_op jit(solution)/shard_map/ppermute | solution.py:334

commit v6 on v5

--- a/solution.py
+++ b/solution.py
@@ -333,9 +333,9 @@
     def move(value, pairs):
         return lax.ppermute(value, "chan", pairs)
 
-    over, ahead = move(own, flip(2)), move(own, from_first(1))
+    ahead, over = move(own, from_first(1)), move(own, flip(2))
     behind, far = move(own, from_first(-1)), move(own, from_first(2))
-    over, ahead, behind, far = hold((over, ahead, behind, far))
+    ahead, over, behind, far = hold((ahead, over, behind, far))
     mates = stack(own, over)
     across = move(mates, flip(1))
     pair0, pair1 = stack(own, ahead), stack(behind, far)

time: 90 us -> 88.6 us (0.984)
  waiting for transfers between devices: 37.3 us -> 35.7 us
    ppermute x23, waiting for transfers between devices: 32 us -> 30.5 us  [move(): return lax.ppermute(value, 'chan', pairs)]
where the time goes in v6:
time: 88.6 us; the launch traced here: 88.5 us
  waiting for transfers between devices  35.7 us (40%)
  starting transfers between devices  32.6 us (37%)
  Pallas kernels  19.2 us (22%)
    ppermute x23, waiting for transfers between devices, move(): return lax.ppermute(value, 'chan', pairs)  30.5 us
    ppermute x23, starting transfers between devices, move(): return lax.ppermute(value, 'chan', pairs)  29 us
    pallas_call x1, Pallas kernels, whiten(): pl.pallas_call(whiten_kernel, in_specs=[pl.BlockSpec(memory_space=pltpu.S...  6.49 us
    ppermute x1, waiting for transfers between devices, local(): got = lax.ppermute(send, 'band', [(0, 1), (1, 0)])  5.2 us
    pallas_call x3, Pallas kernels, cross(): pl.pallas_call(cross_kernel, out_shape=[mine, narrow, wide] if merged els...  5.14 us
    pallas_call x3, Pallas kernels, place(): pl.pallas_call(lambda *refs: place_kernel(blocks, kinds, *refs), in_specs...  4.69 us
    ppermute x1, starting transfers between devices, local(): got = lax.ppermute(send, 'band', [(0, 1), (1, 0)])  3.65 us
    pallas_call x1, Pallas kernels, first_cross(): pl.pallas_call(first_cross_kernel, out_shape=[wide, jax.ShapeDtypeStruct(...  2.28 us
  transfers between devices with their start and end apart: 24, of which 12 were waited for; matrix products, arithmetic and copies ran while one was open for 0% of the time, Pallas kernels for 12%

profile of v6, /device:TPU:1, one launch (start us, length us, event | category | flops | bytes accessed | tf_op | source)
XLA Modules:
  0.0 88.5 jit_solution(8783385290741423016)
XLA Ops:
  0.7 6.5 %whiten.1 = (bf16[960,128]{1,0:T(8,128)(2,1)S(1)}, bf16[960,128]{1,0:T(8,128)(2,1)S(1)}) custom-call(s32[4]{0:T(128)S(1)} %pad_add_fusion.bands, bf16[960,4096]{1,0:T(8,128)(2,1)} %bitcast.4), custom_call_target="tpu_custom_call" | custom-call | tf_op jit(solution)/shard_map/whiten/pallas_call | solution.py:93
  7.2 3.7 %collective-permute-start = (bf16[960,128]{1,0:T(8,128)(2,1)S(1)}, bf16[960,128]{1,0:T(8,128)(2,1)S(1)}, u32[]{:S(2)}, u32[]{:S(2)}) collective-permute-start(bf16[960,128]{1,0:T(8,128)(2,1)S(1)} %get-tuple-element.39), channel_id=1, source_target_pairs={{0,64},{64,0},{1,65},{65,1},{2,66},{66,2},{3,67},{67,3},{4,68},{68... | collective-permute-start | bytes 737288 | tf_op jit(solution)/shard_map/ppermute | solution.py:329
  10.9 5.2 %collective-permute-done.got_ref = bf16[960,128]{1,0:T(8,128)(2,1)S(1)} collective-permute-done((bf16[960,128]{1,0:T(8,128)(2,1)S(1)}, bf16[960,128]{1,0:T(8,128)(2,1)S(1)}, u32[]{:S(2)}, u32[]{:S(2)}) %collective-permute-start) | collective-permute-done | bytes 245792 | tf_op jit(solution)/shard_map/ppermute | solution.py:329
  16.3 3.4 %collective-permute-start.4 = (bf16[160,1536]{1,0:T(8,128)(2,1)S(1)}, bf16[160,1536]{1,0:T(8,128)(2,1)S(1)}, u32[]{:S(2)}, u32[]{:S(2)}) collective-permute-start(bf16[160,1536]{1,0:T(8,128)(2,1)S(1)} %normalize.1.refs_0_), channel_id=1, source_target_pairs={{32,0},{9,1},{34,2},{11,3},{36,4},{13,5},{38,6},{15,7},{40,8},{1,9... | collective-permute-start | bytes 1474568 | tf_op jit(solution)/shard_map/ppermute | solution.py:334
  20.1 1.2 %collective-permute-start.2 = (bf16[160,1536]{1,0:T(8,128)(2,1)S(1)}, bf16[160,1536]{1,0:T(8,128)(2,1)S(1)}, u32[]{:S(2)}, u32[]{:S(2)}) collective-permute-start(bf16[160,1536]{1,0:T(8,128)(2,1)S(1)} %normalize.1.refs_0_), channel_id=1, source_target_pairs={{0,2},{1,3},{2,0},{3,1},{4,6},{5,7},{6,4},{7,5},{8,10},{9,11},{10,... | collective-permute-start | bytes 1474568 | tf_op jit(solution)/shard_map/ppermute | solution.py:334
  21.3 2.3 %collective-permute-start.1 = (bf16[160,1536]{1,0:T(8,128)(2,1)S(1)}, bf16[160,1536]{1,0:T(8,128)(2,1)S(1)}, u32[]{:S(2)}, u32[]{:S(2)}) collective-permute-start(bf16[160,1536]{1,0:T(8,128)(2,1)S(1)} %normalize.1.refs_0_), channel_id=1, source_target_pairs={{16,0},{5,1},{18,2},{7,3},{20,4},{9,5},{22,6},{11,7},{24,8},{13,9}... | collective-permute-start | bytes 1474568 | tf_op jit(solution)/shard_map/ppermute | solution.py:334
  23.6 2.7 %collective-permute-done.4.refs_1_ = bf16[160,1536]{1,0:T(8,128)(2,1)S(1)} collective-permute-done((bf16[160,1536]{1,0:T(8,128)(2,1)S(1)}, bf16[160,1536]{1,0:T(8,128)(2,1)S(1)}, u32[]{:S(2)}, u32[]{:S(2)}) %collective-permute-start.4) | collective-permute-done | bytes 491552 | tf_op jit(solution)/shard_map/ppermute | solution.py:334
  26.3 5.2 %collective-permute-done.3.refs_0_ = bf16[160,1536]{1,0:T(8,128)(2,1)S(1)} collective-permute-done((bf16[160,1536]{1,0:T(8,128)(2,1)S(1)}, bf16[160,1536]{1,0:T(8,128)(2,1)S(1)}, u32[]{:S(2)}, u32[]{:S(2)}) %collective-permute-start.3) | collective-permute-done | bytes 491552 | tf_op jit(solution)/shard_map/ppermute | solution.py:334
  32.0 3.5 %collective-permute-start.5 = (bf16[320,1536]{1,0:T(8,128)(2,1)S(1)}, bf16[320,1536]{1,0:T(8,128)(2,1)S(1)}, u32[]{:S(2)}, u32[]{:S(2)}) collective-permute-start(bf16[320,1536]{1,0:T(8,128)(2,1)S(1)} %stack.4.refs_0_), channel_id=1, source_target_pairs={{0,1},{1,0},{2,3},{3,2},{4,5},{5,4},{6,7},{7,6},{8,9},{9,8},{10,11... | collective-permute-start | bytes 2949128 | tf_op jit(solution)/shard_map/ppermute | solution.py:334
  36.5 2.0 %collective-permute-start.6 = (bf16[320,1536]{1,0:T(8,128)(2,1)S(1)}, bf16[320,1536]{1,0:T(8,128)(2,1)S(1)}, u32[]{:S(2)}, u32[]{:S(2)}) collective-permute-start(bf16[320,1536]{1,0:T(8,128)(2,1)S(1)} %stack.6.pair0), channel_id=1, source_target_pairs={{4,0},{17,1},{6,2},{19,3},{8,4},{21,5},{10,6},{23,7},{12,8},{25,9}... | collective-permute-start | bytes 2949128 | tf_op jit(solution)/shard_map/ppermute | solution.py:334
  38.4 1.2 %collective-permute-start.11 = (bf16[320,1536]{1,0:T(8,128)(2,1)S(1)}, bf16[320,1536]{1,0:T(8,128)(2,1)S(1)}, u32[]{:S(2)}, u32[]{:S(2)}) collective-permute-start(bf16[320,1536]{1,0:T(8,128)(2,1)S(1)} %stack.7.pair1), channel_id=1, source_target_pairs={{4,0},{17,1},{6,2},{19,3},{8,4},{21,5},{10,6},{23,7},{12,8},{25,9}... | collective-permute-start | bytes 2949128 | tf_op jit(solution)/shard_map/ppermute | solution.py:334
  40.0 2.3 %cross.4 = (f32[160,640]{1,0:T(8,128)S(1)}, bf16[160,640]{1,0:T(8,128)(2,1)S(1)}, bf16[160,1024]{1,0:T(8,128)(2,1)S(1)}, f32[160,640]{1,0:T(8,128)S(1)}) custom-call(bf16[640,1536]{1,0:T(8,128)(2,1)S(1)} %stack.5.rows, bf16[320,1536]{1,0:T(8,128)(2,1)S(1)} %stack.6.pair0, bf16[320,1536]{1,0:T(8,128)(2,1)S(1)} %stack.7.pair1), custom_call_target="tpu_custom_call" | custom-call | flops 1258291200 | bytes 12582912 | tf_op jit(solution)/shard_map/cross/pallas_call | solution.py:208
  42.3 1.3 %collective-permute-start.8 = (bf16[160,1024]{1,0:T(8,128)(2,1)S(1)}, bf16[160,1024]{1,0:T(8,128)(2,1)S(1)}, u32[]{:S(2)}, u32[]{:S(2)}) collective-permute-start(bf16[160,1024]{1,0:T(8,128)(2,1)S(1)} %get-tuple-element.46), channel_id=1, source_target_pairs={{0,2},{1,3},{2,0},{3,1},{4,6},{5,7},{6,4},{7,5},{8,10},{9,11},{10,... | collective-permute-start | bytes 983048 | tf_op jit(solution)/shard_map/ppermute | solution.py:334
  43.6 6.4 %collective-permute-done.7.second = bf16[320,1536]{1,0:T(8,128)(2,1)S(1)} collective-permute-done((bf16[320,1536]{1,0:T(8,128)(2,1)S(1)}, bf16[320,1536]{1,0:T(8,128)(2,1)S(1)}, u32[]{:S(2)}, u32[]{:S(2)}) %collective-permute-start.7) | collective-permute-done | bytes 983072 | tf_op jit(solution)/shard_map/ppermute | solution.py:334
  50.9 1.7 %cross.5 = (f32[160,640]{1,0:T(8,128)S(1)}, bf16[160,640]{1,0:T(8,128)(2,1)S(1)}, bf16[160,1280]{1,0:T(8,128)(2,1)S(1)}) custom-call(bf16[640,1536]{1,0:T(8,128)(2,1)S(1)} %stack.5.rows, bf16[320,1536]{1,0:T(8,128)(2,1)S(1)} %collective-permute-done.6.first, bf16[320,1536]{1,0:T(8,128)(2,1)S(1)} %collective-permute-done.7.second), custom_call_target="tpu_custom_call" | custom-call | flops 1258291200 | bytes 12582912 | tf_op jit(solution)/shard_map/cross/pallas_call | solution.py:175
  52.7 2.5 %collective-permute-start.13 = (bf16[320,1536]{1,0:T(8,128)(2,1)S(1)}, bf16[320,1536]{1,0:T(8,128)(2,1)S(1)}, u32[]{:S(2)}, u32[]{:S(2)}) collective-permute-start(bf16[320,1536]{1,0:T(8,128)(2,1)S(1)} %collective-permute-done.6.first), channel_id=1, source_target_pairs={{4,0},{17,1},{6,2},{19,3},{8,4},{21,5},{10,6},{23,7},{12,8},{25,9}... | collective-permute-start | bytes 2949128 | tf_op jit(solution)/shard_map/ppermute | solution.py:334
  55.1 1.2 %collective-permute-start.10 = (bf16[160,1280]{1,0:T(8,128)(2,1)S(1)}, bf16[160,1280]{1,0:T(8,128)(2,1)S(1)}, u32[]{:S(2)}, u32[]{:S(2)}) collective-permute-start(bf16[160,1280]{1,0:T(8,128)(2,1)S(1)} %get-tuple-element.50), channel_id=1, source_target_pairs={{0,2},{1,3},{2,0},{3,1},{4,6},{5,7},{6,4},{7,5},{8,10},{9,11},{10,... | collective-permute-start | bytes 1228808 | tf_op jit(solution)/shard_map/ppermute | solution.py:334
  56.4 3.9 %collective-permute-done.11.first = bf16[320,1536]{1,0:T(8,128)(2,1)S(1)} collective-permute-done((bf16[320,1536]{1,0:T(8,128)(2,1)S(1)}, bf16[320,1536]{1,0:T(8,128)(2,1)S(1)}, u32[]{:S(2)}, u32[]{:S(2)}) %collective-permute-start.11) | collective-permute-done | bytes 983072 | tf_op jit(solution)/shard_map/ppermute | solution.py:334
  60.3 1.7 %collective-permute-start.16 = (bf16[160,1024]{1,0:T(8,128)(2,1)S(1)}, bf16[160,1024]{1,0:T(8,128)(2,1)S(1)}, u32[]{:S(2)}, u32[]{:S(2)}) collective-permute-start(bf16[160,1024]{1,0:T(8,128)(2,1)S(1)} %collective-permute-done.8.refs_2_.refs_1_), channel_id=1, source_target_pairs={{0,1},{1,0},{2,3},{3,2},{4,5},{5,4},{6,7},{7,6},{8,9},{9,8},{10,11... | collective-permute-start | bytes 983048 | tf_op jit(solution)/shard_map/ppermute | solution.py:334
  62.0 1.7 %cross.6 = (f32[160,640]{1,0:T(8,128)S(1)}, bf16[160,640]{1,0:T(8,128)(2,1)S(1)}, bf16[160,1280]{1,0:T(8,128)(2,1)S(1)}) custom-call(bf16[640,1536]{1,0:T(8,128)(2,1)S(1)} %stack.5.rows, bf16[320,1536]{1,0:T(8,128)(2,1)S(1)} %collective-permute-done.11.first, bf16[320,1536]{1,0:T(8,128)(2,1)S(1)} %collective-permute-done.12.second), custom_call_target="tpu_custom_call" | custom-call | flops 1258291200 | bytes 12582912 | tf_op jit(solution)/shard_map/cross/pallas_call | solution.py:175
  63.7 1.3 %collective-permute-start.17 = (bf16[160,1280]{1,0:T(8,128)(2,1)S(1)}, bf16[160,1280]{1,0:T(8,128)(2,1)S(1)}, u32[]{:S(2)}, u32[]{:S(2)}) collective-permute-start(bf16[160,1280]{1,0:T(8,128)(2,1)S(1)} %get-tuple-element.58), channel_id=1, source_target_pairs={{0,2},{1,3},{2,0},{3,1},{4,6},{5,7},{6,4},{7,5},{8,10},{9,11},{10,... | collective-permute-start | bytes 1228808 | tf_op jit(solution)/shard_map/ppermute | solution.py:334
  65.1 2.0 %collective-permute-start.19 = (bf16[160,1280]{1,0:T(8,128)(2,1)S(1)}, bf16[160,1280]{1,0:T(8,128)(2,1)S(1)}, u32[]{:S(2)}, u32[]{:S(2)}) collective-permute-start(bf16[160,1280]{1,0:T(8,128)(2,1)S(1)} %collective-permute-done.10.refs_7_.refs_3_), channel_id=1, source_target_pairs={{0,1},{1,0},{2,3},{3,2},{4,5},{5,4},{6,7},{7,6},{8,9},{9,8},{10,11... | collective-permute-start | bytes 1228808 | tf_op jit(solution)/shard_map/ppermute | solution.py:334
  67.1 3.8 %collective-permute-done.13.first = bf16[320,1536]{1,0:T(8,128)(2,1)S(1)} collective-permute-done((bf16[320,1536]{1,0:T(8,128)(2,1)S(1)}, bf16[320,1536]{1,0:T(8,128)(2,1)S(1)}, u32[]{:S(2)}, u32[]{:S(2)}) %collective-permute-start.13) | collective-permute-done | bytes 983072 | tf_op jit(solution)/shard_map/ppermute | solution.py:334
  71.1 1.7 %cross.7 = (f32[160,640]{1,0:T(8,128)S(1)}, bf16[160,640]{1,0:T(8,128)(2,1)S(1)}, bf16[160,640]{1,0:T(8,128)(2,1)S(1)}, bf16[160,640]{1,0:T(8,128)(2,1)S(1)}) custom-call(bf16[640,1536]{1,0:T(8,128)(2,1)S(1)} %stack.5.rows, bf16[320,1536]{1,0:T(8,128)(2,1)S(1)} %collective-permute-done.13.first, bf16[320,1536]{1,0:T(8,128)(2,1)S(1)} %collective-permute-done.14.second), custom_call_target="tpu_custom_call" | custom-call | flops 1258291200 | bytes 12582912 | tf_op jit(solution)/shard_map/cross/pallas_call | solution.py:175
  72.8 1.7 %collective-permute-done.17.refs_11_.refs_5_ = bf16[160,1280]{1,0:T(8,128)(2,1)S(1)} collective-permute-done((bf16[160,1280]{1,0:T(8,128)(2,1)S(1)}, bf16[160,1280]{1,0:T(8,128)(2,1)S(1)}, u32[]{:S(2)}, u32[]{:S(2)}) %collective-permute-start.17) | collective-permute-done | bytes 409632 | tf_op jit(solution)/shard_map/ppermute | solution.py:334
  74.6 1.2 %collective-permute-start.23 = (bf16[160,1280]{1,0:T(8,128)(2,1)S(1)}, bf16[160,1280]{1,0:T(8,128)(2,1)S(1)}, u32[]{:S(2)}, u32[]{:S(2)}) collective-permute-start(bf16[160,1280]{1,0:T(8,128)(2,1)S(1)} %collective-permute-done.17.refs_11_.refs_5_), channel_id=1, source_target_pairs={{0,1},{1,0},{2,3},{3,2},{4,5},{5,4},{6,7},{7,6},{8,9},{9,8},{10,11... | collective-permute-start | bytes 1228808 | tf_op jit(solution)/shard_map/ppermute | solution.py:334
  75.8 1.2 %collective-permute-start.21 = (bf16[160,640]{1,0:T(8,128)(2,1)S(1)}, bf16[160,640]{1,0:T(8,128)(2,1)S(1)}, u32[]{:S(2)}, u32[]{:S(2)}) collective-permute-start(bf16[160,640]{1,0:T(8,128)(2,1)S(1)} %get-tuple-element.63), channel_id=1, source_target_pairs={{0,2},{1,3},{2,0},{3,1},{4,6},{5,7},{6,4},{7,5},{8,10},{9,11},{10,... | collective-permute-start | bytes 614408 | tf_op jit(solution)/shard_map/ppermute | solution.py:334
  77.7 2.1 %place.3.refs_8_ = f32[160,10240]{1,0:T(8,128)} custom-call(f32[160,640]{1,0:T(8,128)S(1)} %get-tuple-element.44.refs_0_, bf16[160,640]{1,0:T(8,128)(2,1)S(1)} %collective-permute-done.9.refs_1_.refs_0_, bf16[160,1024]{1,0:T(8,128)(2,1)S(1)} %collective-permute-done.8.refs_2_.refs_1_, bf16[160,1024]{1,0:T(8,128)(2,1)S(1)} %collective-permute-done.16.refs_3_.refs_1_, ...), custom_call_target="tpu_custom_call" | custom-call | tf_op jit(solution)/shard_map/place/pallas_call | solution.py:281
  79.8 2.7 %collective-permute-done.21.refs_7_.refs_8_ = bf16[160,640]{1,0:T(8,128)(2,1)S(1)} collective-permute-done((bf16[160,640]{1,0:T(8,128)(2,1)S(1)}, bf16[160,640]{1,0:T(8,128)(2,1)S(1)}, u32[]{:S(2)}, u32[]{:S(2)}) %collective-permute-start.21) | collective-permute-done | bytes 204832 | tf_op jit(solution)/shard_map/ppermute | solution.py:334
  82.5 1.2 %place.4.refs_10_ = f32[160,10240]{1,0:T(8,128)} custom-call(bf16[160,640]{1,0:T(8,128)(2,1)S(1)} %collective-permute-done.9.refs_1_.refs_0_, bf16[160,1024]{1,0:T(8,128)(2,1)S(1)} %collective-permute-done.16.refs_3_.refs_1_, bf16[160,640]{1,0:T(8,128)(2,1)S(1)} %collective-permute-done.15.refs_6_.refs_2_, ...), custom_call_target="tpu_custom_call", output_to_operand_aliasing={{}: (8, {})} | custom-call | tf_op jit(solution)/shard_map/place/pallas_call | solution.py:281
  83.7 3.3 %collective-permute-done.22.refs_9_ = bf16[160,640]{1,0:T(8,128)(2,1)S(1)} collective-permute-done((bf16[160,640]{1,0:T(8,128)(2,1)S(1)}, bf16[160,640]{1,0:T(8,128)(2,1)S(1)}, u32[]{:S(2)}, u32[]{:S(2)}) %collective-permute-start.22) | collective-permute-done | bytes 204832 | tf_op jit(solution)/shard_map/ppermute | solution.py:334
  87.0 1.3 %place.5 = f32[160,10240]{1,0:T(8,128)} custom-call(f32[160,640]{1,0:T(8,128)S(1)} %get-tuple-element.44.refs_0_, bf16[160,1024]{1,0:T(8,128)(2,1)S(1)} %collective-permute-done.8.refs_2_.refs_1_, f32[160,640]{1,0:T(8,128)S(1)} %get-tuple-element.49.refs_5_.refs_2_, ...), custom_call_target="tpu_custom_call", output_to_operand_aliasing={{}: (10, {})} | custom-call | tf_op jit(solution)/shard_map/place/pallas_call | solution.py:281
  (30 shorter events, 5.1 us)
Async XLA Ops:
  7.2 8.9 %collective-permute-start = (bf16[960,128]{1,0:T(8,128)(2,1)S(1)}, bf16[960,128]{1,0:T(8,128)(2,1)S(1)}, u32[]{:S(2)}, u32[]{:S(2)}) collective-permute-start(bf16[960,128]{1,0:T(8,128)(2,1)S(1)} %get-tuple-element.39), channel_id=1, source_target_pairs={{0,64},{64,0},{1,65},{65,1},{2,66},{66,2},{3,67},{67,3},{4,68},{68... | collective-permute-start | bytes 737288 | tf_op jit(solution)/shard_map/ppermute | solution.py:329
  16.3 9.9 %collective-permute-start.4 = (bf16[160,1536]{1,0:T(8,128)(2,1)S(1)}, bf16[160,1536]{1,0:T(8,128)(2,1)S(1)}, u32[]{:S(2)}, u32[]{:S(2)}) collective-permute-start(bf16[160,1536]{1,0:T(8,128)(2,1)S(1)} %normalize.1.refs_0_), channel_id=1, source_target_pairs={{32,0},{9,1},{34,2},{11,3},{36,4},{13,5},{38,6},{15,7},{40,8},{1,9... | collective-permute-start | bytes 1474568 | tf_op jit(solution)/shard_map/ppermute | solution.py:334
  19.7 11.8 %collective-permute-start.3 = (bf16[160,1536]{1,0:T(8,128)(2,1)S(1)}, bf16[160,1536]{1,0:T(8,128)(2,1)S(1)}, u32[]{:S(2)}, u32[]{:S(2)}) collective-permute-start(bf16[160,1536]{1,0:T(8,128)(2,1)S(1)} %normalize.1.refs_0_), channel_id=1, source_target_pairs={{48,0},{13,1},{50,2},{15,3},{52,4},{1,5},{54,6},{3,7},{56,8},{5,9}... | collective-permute-start | bytes 1474568 | tf_op jit(solution)/shard_map/ppermute | solution.py:334
  20.1 11.4 %collective-permute-start.2 = (bf16[160,1536]{1,0:T(8,128)(2,1)S(1)}, bf16[160,1536]{1,0:T(8,128)(2,1)S(1)}, u32[]{:S(2)}, u32[]{:S(2)}) collective-permute-start(bf16[160,1536]{1,0:T(8,128)(2,1)S(1)} %normalize.1.refs_0_), channel_id=1, source_target_pairs={{0,2},{1,3},{2,0},{3,1},{4,6},{5,7},{6,4},{7,5},{8,10},{9,11},{10,... | collective-permute-start | bytes 1474568 | tf_op jit(solution)/shard_map/ppermute | solution.py:334
  21.3 10.6 %collective-permute-start.1 = (bf16[160,1536]{1,0:T(8,128)(2,1)S(1)}, bf16[160,1536]{1,0:T(8,128)(2,1)S(1)}, u32[]{:S(2)}, u32[]{:S(2)}) collective-permute-start(bf16[160,1536]{1,0:T(8,128)(2,1)S(1)} %normalize.1.refs_0_), channel_id=1, source_target_pairs={{16,0},{5,1},{18,2},{7,3},{20,4},{9,5},{22,6},{11,7},{24,8},{13,9}... | collective-permute-start | bytes 1474568 | tf_op jit(solution)/shard_map/ppermute | solution.py:334
  32.0 7.9 %collective-permute-start.5 = (bf16[320,1536]{1,0:T(8,128)(2,1)S(1)}, bf16[320,1536]{1,0:T(8,128)(2,1)S(1)}, u32[]{:S(2)}, u32[]{:S(2)}) collective-permute-start(bf16[320,1536]{1,0:T(8,128)(2,1)S(1)} %stack.4.refs_0_), channel_id=1, source_target_pairs={{0,1},{1,0},{2,3},{3,2},{4,5},{5,4},{6,7},{7,6},{8,9},{9,8},{10,11... | collective-permute-start | bytes 2949128 | tf_op jit(solution)/shard_map/ppermute | solution.py:334
  35.5 14.5 %collective-permute-start.7 = (bf16[320,1536]{1,0:T(8,128)(2,1)S(1)}, bf16[320,1536]{1,0:T(8,128)(2,1)S(1)}, u32[]{:S(2)}, u32[]{:S(2)}) collective-permute-start(bf16[320,1536]{1,0:T(8,128)(2,1)S(1)} %stack.7.pair1), channel_id=1, source_target_pairs={{12,0},{49,1},{14,2},{51,3},{0,4},{53,5},{2,6},{55,7},{4,8},{57,9}... | collective-permute-start | bytes 2949128 | tf_op jit(solution)/shard_map/ppermute | solution.py:334
  36.5 14.5 %collective-permute-start.6 = (bf16[320,1536]{1,0:T(8,128)(2,1)S(1)}, bf16[320,1536]{1,0:T(8,128)(2,1)S(1)}, u32[]{:S(2)}, u32[]{:S(2)}) collective-permute-start(bf16[320,1536]{1,0:T(8,128)(2,1)S(1)} %stack.6.pair0), channel_id=1, source_target_pairs={{4,0},{17,1},{6,2},{19,3},{8,4},{21,5},{10,6},{23,7},{12,8},{25,9}... | collective-permute-start | bytes 2949128 | tf_op jit(solution)/shard_map/ppermute | solution.py:334
  38.4 21.9 %collective-permute-start.11 = (bf16[320,1536]{1,0:T(8,128)(2,1)S(1)}, bf16[320,1536]{1,0:T(8,128)(2,1)S(1)}, u32[]{:S(2)}, u32[]{:S(2)}) collective-permute-start(bf16[320,1536]{1,0:T(8,128)(2,1)S(1)} %stack.7.pair1), channel_id=1, source_target_pairs={{4,0},{17,1},{6,2},{19,3},{8,4},{21,5},{10,6},{23,7},{12,8},{25,9}... | collective-permute-start | bytes 2949128 | tf_op jit(solution)/shard_map/ppermute | solution.py:334
  39.6 22.4 %collective-permute-start.12 = (bf16[320,1536]{1,0:T(8,128)(2,1)S(1)}, bf16[320,1536]{1,0:T(8,128)(2,1)S(1)}, u32[]{:S(2)}, u32[]{:S(2)}) collective-permute-start(bf16[320,1536]{1,0:T(8,128)(2,1)S(1)} %stack.6.pair0), channel_id=1, source_target_pairs={{12,0},{49,1},{14,2},{51,3},{0,4},{53,5},{2,6},{55,7},{4,8},{57,9}... | collective-permute-start | bytes 2949128 | tf_op jit(solution)/shard_map/ppermute | solution.py:334
  42.3 10.4 %collective-permute-start.8 = (bf16[160,1024]{1,0:T(8,128)(2,1)S(1)}, bf16[160,1024]{1,0:T(8,128)(2,1)S(1)}, u32[]{:S(2)}, u32[]{:S(2)}) collective-permute-start(bf16[160,1024]{1,0:T(8,128)(2,1)S(1)} %get-tuple-element.46), channel_id=1, source_target_pairs={{0,2},{1,3},{2,0},{3,1},{4,6},{5,7},{6,4},{7,5},{8,10},{9,11},{10,... | collective-permute-start | bytes 983048 | tf_op jit(solution)/shard_map/ppermute | solution.py:334
  50.1 2.6 %collective-permute-start.9 = (bf16[160,640]{1,0:T(8,128)(2,1)S(1)}, bf16[160,640]{1,0:T(8,128)(2,1)S(1)}, u32[]{:S(2)}, u32[]{:S(2)}) collective-permute-start(bf16[160,640]{1,0:T(8,128)(2,1)S(1)} %get-tuple-element.47), channel_id=1, source_target_pairs={{0,1},{1,0},{2,3},{3,2},{4,5},{5,4},{6,7},{7,6},{8,9},{9,8},{10,11... | collective-permute-start | bytes 614408 | tf_op jit(solution)/shard_map/ppermute | solution.py:334
  52.7 18.1 %collective-permute-start.13 = (bf16[320,1536]{1,0:T(8,128)(2,1)S(1)}, bf16[320,1536]{1,0:T(8,128)(2,1)S(1)}, u32[]{:S(2)}, u32[]{:S(2)}) collective-permute-start(bf16[320,1536]{1,0:T(8,128)(2,1)S(1)} %collective-permute-done.6.first), channel_id=1, source_target_pairs={{4,0},{17,1},{6,2},{19,3},{8,4},{21,5},{10,6},{23,7},{12,8},{25,9}... | collective-permute-start | bytes 2949128 | tf_op jit(solution)/shard_map/ppermute | solution.py:334
  55.1 16.0 %collective-permute-start.14 = (bf16[320,1536]{1,0:T(8,128)(2,1)S(1)}, bf16[320,1536]{1,0:T(8,128)(2,1)S(1)}, u32[]{:S(2)}, u32[]{:S(2)}) collective-permute-start(bf16[320,1536]{1,0:T(8,128)(2,1)S(1)} %collective-permute-done.7.second), channel_id=1, source_target_pairs={{12,0},{49,1},{14,2},{51,3},{0,4},{53,5},{2,6},{55,7},{4,8},{57,9}... | collective-permute-start | bytes 2949128 | tf_op jit(solution)/shard_map/ppermute | solution.py:334
  55.1 10.0 %collective-permute-start.10 = (bf16[160,1280]{1,0:T(8,128)(2,1)S(1)}, bf16[160,1280]{1,0:T(8,128)(2,1)S(1)}, u32[]{:S(2)}, u32[]{:S(2)}) collective-permute-start(bf16[160,1280]{1,0:T(8,128)(2,1)S(1)} %get-tuple-element.50), channel_id=1, source_target_pairs={{0,2},{1,3},{2,0},{3,1},{4,6},{5,7},{6,4},{7,5},{8,10},{9,11},{10,... | collective-permute-start | bytes 1228808 | tf_op jit(solution)/shard_map/ppermute | solution.py:334
  60.3 3.4 %collective-permute-start.16 = (bf16[160,1024]{1,0:T(8,128)(2,1)S(1)}, bf16[160,1024]{1,0:T(8,128)(2,1)S(1)}, u32[]{:S(2)}, u32[]{:S(2)}) collective-permute-start(bf16[160,1024]{1,0:T(8,128)(2,1)S(1)} %collective-permute-done.8.refs_2_.refs_1_), channel_id=1, source_target_pairs={{0,1},{1,0},{2,3},{3,2},{4,5},{5,4},{6,7},{7,6},{8,9},{9,8},{10,11... | collective-permute-start | bytes 983048 | tf_op jit(solution)/shard_map/ppermute | solution.py:334
  62.0 1.7 %collective-permute-start.15 = (bf16[160,640]{1,0:T(8,128)(2,1)S(1)}, bf16[160,640]{1,0:T(8,128)(2,1)S(1)}, u32[]{:S(2)}, u32[]{:S(2)}) collective-permute-start(bf16[160,640]{1,0:T(8,128)(2,1)S(1)} %get-tuple-element.57), channel_id=1, source_target_pairs={{0,1},{1,0},{2,3},{3,2},{4,5},{5,4},{6,7},{7,6},{8,9},{9,8},{10,11... | collective-permute-start | bytes 614408 | tf_op jit(solution)/shard_map/ppermute | solution.py:334
  63.7 10.8 %collective-permute-start.17 = (bf16[160,1280]{1,0:T(8,128)(2,1)S(1)}, bf16[160,1280]{1,0:T(8,128)(2,1)S(1)}, u32[]{:S(2)}, u32[]{:S(2)}) collective-permute-start(bf16[160,1280]{1,0:T(8,128)(2,1)S(1)} %get-tuple-element.58), channel_id=1, source_target_pairs={{0,2},{1,3},{2,0},{3,1},{4,6},{5,7},{6,4},{7,5},{8,10},{9,11},{10,... | collective-permute-start | bytes 1228808 | tf_op jit(solution)/shard_map/ppermute | solution.py:334
  65.1 9.4 %collective-permute-start.19 = (bf16[160,1280]{1,0:T(8,128)(2,1)S(1)}, bf16[160,1280]{1,0:T(8,128)(2,1)S(1)}, u32[]{:S(2)}, u32[]{:S(2)}) collective-permute-start(bf16[160,1280]{1,0:T(8,128)(2,1)S(1)} %collective-permute-done.10.refs_7_.refs_3_), channel_id=1, source_target_pairs={{0,1},{1,0},{2,3},{3,2},{4,5},{5,4},{6,7},{7,6},{8,9},{9,8},{10,11... | collective-permute-start | bytes 1228808 | tf_op jit(solution)/shard_map/ppermute | solution.py:334
  67.1 5.8 %collective-permute-start.18 = (bf16[160,640]{1,0:T(8,128)(2,1)S(1)}, bf16[160,640]{1,0:T(8,128)(2,1)S(1)}, u32[]{:S(2)}, u32[]{:S(2)}) collective-permute-start(bf16[160,640]{1,0:T(8,128)(2,1)S(1)} %get-tuple-element.59), channel_id=1, source_target_pairs={{0,1},{1,0},{2,3},{3,2},{4,5},{5,4},{6,7},{7,6},{8,9},{9,8},{10,11... | collective-permute-start | bytes 614408 | tf_op jit(solution)/shard_map/ppermute | solution.py:334
  74.6 3.1 %collective-permute-start.23 = (bf16[160,1280]{1,0:T(8,128)(2,1)S(1)}, bf16[160,1280]{1,0:T(8,128)(2,1)S(1)}, u32[]{:S(2)}, u32[]{:S(2)}) collective-permute-start(bf16[160,1280]{1,0:T(8,128)(2,1)S(1)} %collective-permute-done.17.refs_11_.refs_5_), channel_id=1, source_target_pairs={{0,1},{1,0},{2,3},{3,2},{4,5},{5,4},{6,7},{7,6},{8,9},{9,8},{10,11... | collective-permute-start | bytes 1228808 | tf_op jit(solution)/shard_map/ppermute | solution.py:334
  75.8 6.7 %collective-permute-start.21 = (bf16[160,640]{1,0:T(8,128)(2,1)S(1)}, bf16[160,640]{1,0:T(8,128)(2,1)S(1)}, u32[]{:S(2)}, u32[]{:S(2)}) collective-permute-start(bf16[160,640]{1,0:T(8,128)(2,1)S(1)} %get-tuple-element.63), channel_id=1, source_target_pairs={{0,2},{1,3},{2,0},{3,1},{4,6},{5,7},{6,4},{7,5},{8,10},{9,11},{10,... | collective-permute-start | bytes 614408 | tf_op jit(solution)/shard_map/ppermute | solution.py:334
  77.0 10.0 %collective-permute-start.22 = (bf16[160,640]{1,0:T(8,128)(2,1)S(1)}, bf16[160,640]{1,0:T(8,128)(2,1)S(1)}, u32[]{:S(2)}, u32[]{:S(2)}) collective-permute-start(bf16[160,640]{1,0:T(8,128)(2,1)S(1)} %get-tuple-element.64), channel_id=1, source_target_pairs={{0,3},{1,2},{2,1},{3,0},{4,7},{5,6},{6,5},{7,4},{8,11},{9,10},{10,... | collective-permute-start | bytes 614408 | tf_op jit(solution)/shard_map/ppermute | solution.py:334
  77.4 9.6 %collective-permute-start.20 = (bf16[160,640]{1,0:T(8,128)(2,1)S(1)}, bf16[160,640]{1,0:T(8,128)(2,1)S(1)}, u32[]{:S(2)}, u32[]{:S(2)}) collective-permute-start(bf16[160,640]{1,0:T(8,128)(2,1)S(1)} %get-tuple-element.62), channel_id=1, source_target_pairs={{0,1},{1,0},{2,3},{3,2},{4,5},{5,4},{6,7},{7,6},{8,9},{9,8},{10,11... | collective-permute-start | bytes 614408 | tf_op jit(solution)/shard_map/ppermute | solution.py:334
